TPU v7x, 32 devices: a whole 2x2x4 slice. The times are simulated.
32 devices in a mesh: row: 4 (over y, x), col: 4 (over z), cond: 2 (over core).
Axes of the slice: x: 2, y: 2, z: 4, core: 2. Of those that a mesh axis runs over, the one named last changes fastest.
Arguments:
- mask: float32 [512, 512], P('row', 'col'), may hold values from -1 to 1
- target: int32 [512, 512], P('row', 'col'), may hold values 0 or 1
- cond_index: int32 [4], P('cond'), may hold values from 0 to 7
- kernels: float32 [8, 2, 12, 576], replicated, may hold values from -6 to 6
- dose: float32 [8], replicated, may hold values from 0.7 to 1.4
Outputs:
- mask_grad: float32 [512, 512], P('row', 'col')
All inputs are finite; a program needn't handle non-finite values. No bound on the sum of `target` on one device may be relied on, other than what follows from the above.
Results may differ from a plain program's by a relative error of at most 0.0003.
Values sent between devices are 32-bit elements; how exact they have to be, the bound alone decides.
No kernel may reach another device: no remote copies, remote signals or barrier semaphores. Data moves between devices by JAX's collectives and lax.ppermute only.
A program may use at most 64 MiB of HBM per device.

v0:
```python
import math

import jax
import jax.numpy as jnp
from jax import lax
from jax.sharding import PartitionSpec as P

MARGIN = 128
BAND = 24


STEEP = 4.0
THRESH = 0.6


def extended(block, sides, width):
    for axis, dim in sides:
        count = lax.axis_size(axis)
        forward = [(i, i + 1) for i in range(count - 1)]
        backward = [(target, source) for source, target in forward]
        low = lax.ppermute(
            lax.slice_in_dim(block, block.shape[dim] - width, None, axis=dim), axis, forward
        )
        high = lax.ppermute(lax.slice_in_dim(block, 0, width, axis=dim), axis, backward)
        block = jnp.concatenate([low, block, high], axis=dim)
    return block


def highest(left_side, right_side):
    return jnp.dot(
        left_side, right_side, precision=lax.Precision.HIGHEST, preferred_element_type=jnp.float32
    )


def tables(length, start, window_size, band_size):
    frequency = jnp.arange(band_size, dtype=jnp.int32) - band_size // 2
    positions = jnp.arange(length, dtype=jnp.int32) + start
    phases = frequency[:, None] * positions[None, :] % window_size
    angles = phases.astype(jnp.float32) * (2.0 * math.pi / window_size)
    return (jnp.cos(angles), jnp.sin(angles))


def row_product(segment, row_start, window_size, band_size):
    cosine_table, sine_table = tables(segment.shape[0], row_start, window_size, band_size)
    return highest(jnp.concatenate([cosine_table, sine_table], axis=0), segment)


def col_product(partial_rows, col_start, window_size, band_size):
    cosine_table, sine_table = tables(partial_rows.shape[1], col_start, window_size, band_size)
    products = highest(partial_rows, jnp.concatenate([cosine_table, sine_table], axis=0).T)
    upper_cos = products[:band_size, :band_size]
    upper_sin = products[:band_size, band_size:]
    lower_cos = products[band_size:, :band_size]
    lower_sin = products[band_size:, band_size:]
    return jnp.stack([upper_cos - lower_sin, -lower_cos - upper_sin]) / window_size


def tile_loss(spectrum, kernel, dose_value, goal_map):
    tile_size = goal_map.shape[0]
    band_size = spectrum.shape[1]
    window_size = tile_size + 2 * MARGIN
    kernel_real = kernel[0].reshape(-1, band_size, band_size)
    kernel_imag = kernel[1].reshape(-1, band_size, band_size)
    kernel_count = kernel_real.shape[0]
    product_real = kernel_real * spectrum[0] - kernel_imag * spectrum[1]
    product_imag = kernel_real * spectrum[1] + kernel_imag * spectrum[0]
    stacked = jnp.concatenate([product_real, product_imag], axis=1)
    stacked = jnp.transpose(stacked, (1, 0, 2)).reshape(2 * band_size, kernel_count * band_size)
    cosine_table, sine_table = tables(tile_size, MARGIN, window_size, band_size)
    cosine_cols = cosine_table.T
    sine_cols = sine_table.T
    inverse_left = jnp.concatenate(
        [
            jnp.concatenate([cosine_cols, -sine_cols], 1),
            jnp.concatenate([sine_cols, cosine_cols], 1),
        ],
        0,
    )
    partial_rows = highest(inverse_left, stacked)
    rows_real = partial_rows[:tile_size].reshape(tile_size, kernel_count, band_size)
    rows_imag = partial_rows[tile_size:].reshape(tile_size, kernel_count, band_size)
    rows_both = jnp.concatenate([rows_real, rows_imag], axis=2)
    rows_both = jnp.transpose(rows_both, (1, 0, 2)).reshape(kernel_count * tile_size, 2 * band_size)
    inverse_right = jnp.concatenate(
        [
            jnp.concatenate([cosine_table, sine_table], 1),
            jnp.concatenate([-sine_table, cosine_table], 1),
        ],
        0,
    )
    fields = highest(rows_both, inverse_right)
    squared = (fields * fields).reshape(kernel_count, tile_size, 2, tile_size)
    intensity = jnp.sum(squared, axis=(0, 2)) / (kernel_count * band_size * band_size)
    resist = jax.nn.sigmoid(STEEP * (dose_value * intensity - THRESH))
    return jnp.sum(jnp.square(resist - goal_map))


def interior_adjoint(cotangent, tile_size, window_size):
    band_size = cotangent.shape[1]
    cosine_table, sine_table = tables(tile_size, MARGIN, window_size, band_size)
    joined = jnp.concatenate([cotangent[0], cotangent[1]], axis=1)
    right_side = jnp.concatenate(
        [
            jnp.concatenate([cosine_table, -sine_table], 1),
            jnp.concatenate([-sine_table, -cosine_table], 1),
        ],
        0,
    )
    halves = highest(joined, right_side)
    stacked = jnp.concatenate([halves[:, :tile_size], halves[:, tile_size:]], axis=0)
    left_side = jnp.concatenate([cosine_table, sine_table], axis=0).T
    return highest(left_side, stacked) / window_size


def shards(mask, target, cond_index, kernels, dose):
    tile_size = mask.shape[0]
    window_size = tile_size + 2 * MARGIN
    window = extended(mask, (("row", 0), ("col", 1)), MARGIN)
    spectrum = col_product(row_product(window, 0, window_size, BAND), 0, window_size, BAND)
    goal_map = target.astype(jnp.float32)
    summed = jnp.zeros((2, BAND, BAND), jnp.float32)
    for ordinal in range(cond_index.shape[0]):
        setting = cond_index[ordinal]
        kernel = lax.dynamic_index_in_dim(kernels, setting, 0, keepdims=False)
        dose_value = lax.dynamic_index_in_dim(dose, setting, 0, keepdims=False)
        summed = summed + jax.grad(tile_loss)(spectrum, kernel, dose_value, goal_map)
    combined = lax.psum(summed, "cond")
    return interior_adjoint(combined, tile_size, window_size)


def solution(mesh):
    in_specs = (P("row", "col"), P("row", "col"), P("cond"), P(), P())
    out_specs = P("row", "col")
    return jax.shard_map(shards, mesh=mesh, in_specs=in_specs, out_specs=out_specs, check_vma=False)
```

profile of v0, /device:TPU:5, one launch (start us, length us, event | category | flops | bytes accessed | tf_op | source)
XLA Modules:
  0.0 65.2 jit_solution(14127414394871676349)
XLA Ops:
  0.0 3.1 %collective-permute-start = (f32[128,128]{1,0:T(8,128)}, f32[128,128]{1,0:T(8,128)S(1)}, u32[]{:S(2)}, u32[]{:S(2)}) collective-permute-start(f32[128,128]{1,0:T(8,128)} %param.5), channel_id=1, source_target_pairs={{0,8},{8,16},{16,24},{1,9},{9,17},{17,25},{2,10},{10,18},{18,26},{... | collective-permute-start | bytes 196616 | tf_op jit(solution)/shard_map/ppermute | solution.py:21
  3.1 3.1 %collective-permute-start.1 = (f32[128,128]{1,0:T(8,128)}, f32[128,128]{1,0:T(8,128)S(1)}, u32[]{:S(2)}, u32[]{:S(2)}) collective-permute-start(f32[128,128]{1,0:T(8,128)} %param.5), channel_id=1, source_target_pairs={{8,0},{16,8},{24,16},{9,1},{17,9},{25,17},{10,2},{18,10},{26,18},{... | collective-permute-start | bytes 196616 | tf_op jit(solution)/shard_map/ppermute | solution.py:24
  6.2 0.2 fusion.44
  6.4 0.1 fusion.77
  6.6 1.3 %fusion.100 = (s32[1]{0:T(128)}, s32[1]{0:T(128)}) fusion(s32[2]{0:T(128)} %param.7), kind=kLoop, calls=%fused_computation.146 | loop fusion | bytes 16 | tf_op jit(solution)/shard_map/slice | solution.py:123
  11.9 1.4 %fusion.99 = (f32[1]{0:T(128)}, f32[1]{0:T(128)}) fusion(f32[8]{0:T(128)} %param.9, s32[]{:T(128)S(6)} %select_n.60, s32[]{:T(128)S(6)} %select_n.63), kind=kLoop, calls=%fused_computation.145 | loop fusion | bytes 24 | tf_op jit(solution)/shard_map/jit(dynamic_index_in_dim)/dynamic_slice | solution.py:125
  16.0 1.3 %dynamic-slice_reduce_fusion.3 = (f32[12,576]{1,0:T(8,128)S(1)}, f32[12,576]{1,0:T(8,128)S(1)}, f32[12,576]{1,0:T(8,128)S(1)}, f32[12,576]{1,0:T(8,128)S(1)}) fusion(f32[8,2,12,576]{3,1,2,0:T(2,128)} %param.8, s32[]{:T(128)S(6)} %select_n.60, s32[]{:T(128)S(6)} %add.158, s32[]{:T(128)S(6)} %select_n.63), kind=kLoop, calls=%fused_computation.77 | loop fusion | bytes 221196 | tf_op jit(solution)/shard_map/jvp()/slice | solution.py:63
  17.3 0.1 squeeze.31
  17.4 0.0 copy-start.1
  17.4 0.1 squeeze.32
  17.5 0.0 copy-start.3
  17.5 0.1 squeeze.34
  17.6 0.1 squeeze.35
  17.7 0.0 collective-permute-done
  17.8 0.8 %constant_dynamic-update-slice_fusion.1 = f32[384,128]{1,0:T(8,128)S(1)} fusion(f32[384,128]{1,0:T(8,128)S(1)} %constant_dynamic-update-slice_fusion.2, f32[128,128]{1,0:T(8,128)} %param.5), kind=kLoop, calls=%fused_computation.117 | loop fusion | bytes 131072
  18.6 0.0 collective-permute-done.1
  18.6 3.2 %collective-permute-start.2 = (f32[384,128]{1,0:T(8,128)S(1)}, f32[384,128]{1,0:T(8,128)S(1)}, u32[]{:S(2)}, u32[]{:S(2)}) collective-permute-start(f32[384,128]{1,0:T(8,128)S(1)} %constant_dynamic-update-slice_fusion), channel_id=1, source_target_pairs={{0,2},{2,4},{4,6},{1,3},{3,5},{5,7},{8,10},{10,12},{12,14},{9,11},... | collective-permute-start | bytes 589832 | tf_op jit(solution)/shard_map/ppermute | solution.py:21
  21.8 1.3 %collective-permute-start.3 = (f32[384,128]{1,0:T(8,128)S(1)}, f32[384,128]{1,0:T(8,128)S(1)}, u32[]{:S(2)}, u32[]{:S(2)}) collective-permute-start(f32[384,128]{1,0:T(8,128)S(1)} %constant_dynamic-update-slice_fusion), channel_id=1, source_target_pairs={{2,0},{4,2},{6,4},{3,1},{5,3},{7,5},{10,8},{12,10},{14,12},{11,9},... | collective-permute-start | bytes 589832 | tf_op jit(solution)/shard_map/ppermute | solution.py:24
  23.1 0.1 fusion.79
  23.3 1.6 %collective-permute-done.2 = f32[384,128]{1,0:T(8,128)S(1)} collective-permute-done((f32[384,128]{1,0:T(8,128)S(1)}, f32[384,128]{1,0:T(8,128)S(1)}, u32[]{:S(2)}, u32[]{:S(2)}) %collective-permute-start.2) | collective-permute-done | bytes 196640 | tf_op jit(solution)/shard_map/ppermute | solution.py:21
  24.8 3.8 %collective-permute-done.3 = f32[384,128]{1,0:T(8,128)S(1)} collective-permute-done((f32[384,128]{1,0:T(8,128)S(1)}, f32[384,128]{1,0:T(8,128)S(1)}, u32[]{:S(2)}, u32[]{:S(2)}) %collective-permute-start.3) | collective-permute-done | bytes 196640 | tf_op jit(solution)/shard_map/ppermute | solution.py:24
  28.7 0.4 fusion.6
  29.1 0.2 fusion.32
  29.3 0.1 fusion.57
  29.5 0.1 multiply_subtract_fusion.1
  29.5 0.0 copy-done.1
  29.5 0.0 copy-done.3
  29.5 0.8 %maximum_bitcast_fusion = (f32[48,12,24]{2,0,1:T(8,128)}, f32[48,12,24]{2,0,1:T(8,128)S(1)}) fusion(f32[12,24,24]{2,1,0:T(8,128)S(1)} %get-tuple-element.26, f32[12,24,24]{2,1,0:T(8,128)S(1)} %get-tuple-element.25, f32[12,24,24]{2,1,0:T(8,128)S(1)} %get-tuple-element.39, f32[12,24,24]{2,1,0:T(8,128)S(1)} %get-tuple-element.40), kind=kLoop, calls=%fused_computation.23 | loop fusion | flops 27648 | bytes 221184 | tf_op jit(solution)/shard_map/jvp()/transpose | solution.py:68
  30.3 0.1 copy.35
  30.4 0.4 fusion.71
  31.0 2.6 %fusion.102 = (f32[1536,256]{1,0:T(8,128)}, f32[1536,256]{1,0:T(8,128)S(1)}) fusion(f32[24,128]{1,0:T(8,128)S(1)} %get-tuple-element.51, f32[24,128]{1,0:T(8,128)S(1)} %get-tuple-element.49, f32[24,128]{1,0:T(8,128)S(1)} %get-tuple-element.50, f32[6,8,12,128]{3,2,1,0:T(8,128)S(1)} %bitcast.85), kind=kOutput, calls=%fused_computation.148 | convolution fusion | flops 226922496 | bytes 3477504 | tf_op jit(solution)/shard_map/jvp()/dot_general | solution.py:30
  33.6 2.1 %reshape.142 = f32[12,128,2,128]{3,2,1,0:T(2,128)S(1)} reshape(f32[1536,256]{1,0:T(8,128)} %get-tuple-element.60) | data formatting | bytes 3145728 | tf_op jit(solution)/shard_map/jvp()/reshape | solution.py:92
  35.6 1.7 %copy.28 = f32[48,12,24]{0,2,1:T(8,128)} copy(f32[48,12,24]{2,0,1:T(8,128)} %get-tuple-element.62) | data formatting | bytes 110592 | tf_op jit(solution)/shard_map/jvp()/transpose | solution.py:68
  37.4 1.3 %fusion.72 = f32[256,288]{0,1:T(8,128)S(1)} fusion(f32[48,288]{0,1:T(8,128)} %bitcast.92, f32[128,24]{0,1:T(8,128)S(1)} %get-tuple-element.47, f32[128,24]{0,1:T(8,128)S(1)} %get-tuple-element.46, f32[128,24]{0,1:T(8,128)S(1)} %get-tuple-element.45), kind=kOutput, calls=%fused_computation.120 | convolution fusion | flops 42504192 | bytes 387072 | tf_op jit(solution)/shard_map/jvp()/dot_general | solution.py:30
  38.8 3.1 %fusion.101 = (f32[1536,256]{1,0:T(8,128)}, f32[1536,256]{1,0:T(8,128)}) fusion(f32[24,128]{1,0:T(8,128)S(1)} %get-tuple-element.51, f32[24,128]{1,0:T(8,128)S(1)} %get-tuple-element.49, f32[24,128]{1,0:T(8,128)S(1)} %get-tuple-element.50, f32[6,8,12,128]{3,2,1,0:T(8,128)S(1)} %bitcast.86), kind=kOutput, calls=%fused_computation.147 | convolution fusion | flops 226922496 | bytes 3477504 | tf_op jit(solution)/shard_map/jvp()/dot_general | solution.py:30
  41.9 2.9 %reshape.128 = f32[12,128,2,128]{3,2,1,0:T(2,128)} reshape(f32[1536,256]{1,0:T(8,128)} %get-tuple-element.58) | data formatting | bytes 3145728 | tf_op jit(solution)/shard_map/jvp()/reshape | solution.py:92
  44.8 1.3 %reduce_sum.97 = f32[128,128]{1,0:T(8,128)} reduce(f32[12,128,2,128]{3,2,1,0:T(2,128)S(1)} %reshape.142, f32[]{:T(128)} %constant.70.clone.1), dimensions={0,2}, to_apply=%region_5.6 | reduce | flops 376832 | bytes 1638404 | tf_op jit(solution)/shard_map/jvp()/reduce_sum | solution.py:93
  46.1 2.7 %reduce_sum.86 = f32[128,128]{1,0:T(8,128)} reduce(f32[12,128,2,128]{3,2,1,0:T(2,128)} %reshape.128, f32[]{:T(128)} %constant.70.clone.1), dimensions={0,2}, to_apply=%region_0.1 | reduce | flops 376832 | bytes 1638404 | tf_op jit(solution)/shard_map/jvp()/reduce_sum | solution.py:93
  48.8 1.6 %fusion.28 = (f32[128,128]{1,0:T(8,128)S(1)}, f32[128,128]{1,0:T(8,128)}) fusion(s32[128,128]{1,0:T(8,128)} %param.6, f32[128,128]{1,0:T(8,128)} %reduce_sum.86, f32[]{:T(128)} %bitcast.11, f32[]{:T(128)} %bitcast.10, f32[]{:T(128)} %bitcast.28, f32[128,128]{1,0:T(8,128)} %reduce_sum.97, f32[]{:T(128)} %bitcast.27), kind=kLoop, calls=%fused_computation.50 | loop fusion | flops 442368 | bytes 327696 | tf_op jit(solution)/shard_map/transpose(jvp())/div | solution.py:93
  50.4 0.5 broadcast_in_dim.4
  50.9 0.0 copy-done
  50.9 2.4 %fusion.2 = f32[1536,48]{0,1:T(8,128)} fusion(f32[192,8,2,128]{3,2,1,0:T(2,128)S(1)} %bitcast.81, f32[1536,256]{1,0:T(8,128)S(1)} %copy-done, f32[24,128]{1,0:T(8,128)S(1)} %get-tuple-element.51, f32[24,128]{1,0:T(8,128)S(1)} %get-tuple-element.49, f32[24,128]{1,0:T(8,128)S(1)} %get-tuple-element.50), kind=kOutput, calls=%fused_computation.4 | convolution fusion | flops 227315712 | bytes 3477504 | tf_op jit(solution)/shard_map/transpose(jvp())/dot_general | solution.py:30
  53.4 0.0 copy-start.2
  53.4 1.1 %reshape.130 = f32[12,128,48]{1,0,2:T(8,128)S(1)} reshape(f32[1536,48]{0,1:T(8,128)} %fusion.2) | data formatting | bytes 589824 | tf_op jit(solution)/shard_map/transpose(jvp())/reshape | solution.py:83
  54.4 0.0 copy-start.5
  54.5 0.1 copy.31
  54.5 0.1 copy.32
  54.6 0.4 fusion.22
  55.0 0.1 copy.34
  55.1 0.0 copy-done.2
  55.1 0.0 copy-done.4
  55.1 0.1 multiply_reduce_fusion.7
  55.2 0.1 copy-done.5
  55.3 0.5 broadcast_in_dim.5
  55.8 1.7 %fusion = f32[1536,48]{0,1:T(8,128)S(1)} fusion(f32[192,8,2,128]{3,2,1,0:T(2,128)S(1)} %bitcast.82, f32[1536,256]{1,0:T(8,128)S(1)} %get-tuple-element.61, f32[24,128]{1,0:T(8,128)S(1)} %get-tuple-element.51, f32[24,128]{1,0:T(8,128)S(1)} %get-tuple-element.49, f32[24,128]{1,0:T(8,128)S(1)} %get-tuple-element.50), kind=kOutput, calls=%fused_computation.1 | convolution fusion | flops 227315712 | bytes 3477504 | tf_op jit(solution)/shard_map/transpose(jvp())/dot_general | solution.py:30
  57.6 0.1 reshape.144
  57.7 0.1 copy.38
  57.7 0.1 copy.39
  57.8 0.4 fusion.18
  58.2 0.1 copy.41
  58.3 0.1 multiply_reduce_fusion.3
  58.4 5.6 %psum.7 = f32[2,24,24]{2,1,0:T(8,128)S(1)} all-reduce(f32[2,24,24]{2,1,0:T(8,128)S(1)} %add_add_fusion), channel_id=1, replica_groups=mesh['row'=4,'col'=4,'cond'=2] {'cond'}, use_global_device_ids=true, to_apply=%region_10.11 | all-reduce | flops 1152 | bytes 9216 | tf_op jit(solution)/shard_map/psum | solution.py:127
  64.0 0.2 fusion.35
  64.3 0.9 %convolution_multiply_fusion = f32[128,128]{1,0:T(8,128)} fusion(f32[24,128]{1,0:T(8,128)S(1)} %get-tuple-element.50, f32[24,128]{1,0:T(8,128)S(1)} %get-tuple-element.51, f32[24,128]{1,0:T(8,128)S(1)} %get-tuple-element.36, f32[24,128]{1,0:T(8,128)S(1)} %get-tuple-element.35), kind=kOutput, calls=%fused_computation.8 | convolution fusion | flops 9465856 | bytes 114688 | tf_op jit(solution)/shard_map/dot_general | solution.py:30
  (21 shorter events, 0.3 us)
Async XLA Ops:
  0.0 17.7 %collective-permute-start = (f32[128,128]{1,0:T(8,128)}, f32[128,128]{1,0:T(8,128)S(1)}, u32[]{:S(2)}, u32[]{:S(2)}) collective-permute-start(f32[128,128]{1,0:T(8,128)} %param.5), channel_id=1, source_target_pairs={{0,8},{8,16},{16,24},{1,9},{9,17},{17,25},{2,10},{10,18},{18,26},{... | collective-permute-start | bytes 196616 | tf_op jit(solution)/shard_map/ppermute | solution.py:21
  3.1 15.5 %collective-permute-start.1 = (f32[128,128]{1,0:T(8,128)}, f32[128,128]{1,0:T(8,128)S(1)}, u32[]{:S(2)}, u32[]{:S(2)}) collective-permute-start(f32[128,128]{1,0:T(8,128)} %param.5), channel_id=1, source_target_pairs={{8,0},{16,8},{24,16},{9,1},{17,9},{25,17},{10,2},{18,10},{26,18},{... | collective-permute-start | bytes 196616 | tf_op jit(solution)/shard_map/ppermute | solution.py:24
  17.4 12.1 %copy-start.1 = (f32[12,24,24]{2,1,0:T(8,128)}, f32[12,24,24]{2,1,0:T(8,128)S(1)}, u32[]{:S(2)}) copy-start(f32[12,24,24]{2,1,0:T(8,128)S(1)} %squeeze.31) | copy-start | bytes 82948
  17.5 12.0 %copy-start.3 = (f32[12,24,24]{2,1,0:T(8,128)}, f32[12,24,24]{2,1,0:T(8,128)S(1)}, u32[]{:S(2)}) copy-start(f32[12,24,24]{2,1,0:T(8,128)S(1)} %squeeze.32) | copy-start | bytes 82948
  18.6 6.2 %collective-permute-start.2 = (f32[384,128]{1,0:T(8,128)S(1)}, f32[384,128]{1,0:T(8,128)S(1)}, u32[]{:S(2)}, u32[]{:S(2)}) collective-permute-start(f32[384,128]{1,0:T(8,128)S(1)} %constant_dynamic-update-slice_fusion), channel_id=1, source_target_pairs={{0,2},{2,4},{4,6},{1,3},{3,5},{5,7},{8,10},{10,12},{12,14},{9,11},... | collective-permute-start | bytes 589832 | tf_op jit(solution)/shard_map/ppermute | solution.py:21
  21.8 6.8 %collective-permute-start.3 = (f32[384,128]{1,0:T(8,128)S(1)}, f32[384,128]{1,0:T(8,128)S(1)}, u32[]{:S(2)}, u32[]{:S(2)}) collective-permute-start(f32[384,128]{1,0:T(8,128)S(1)} %constant_dynamic-update-slice_fusion), channel_id=1, source_target_pairs={{2,0},{4,2},{6,4},{3,1},{5,3},{7,5},{10,8},{12,10},{14,12},{11,9},... | collective-permute-start | bytes 589832 | tf_op jit(solution)/shard_map/ppermute | solution.py:24
  46.1 4.8 %copy-start = (f32[1536,256]{1,0:T(8,128)S(1)}, f32[1536,256]{1,0:T(8,128)}, u32[]{:S(2)}) copy-start(f32[1536,256]{1,0:T(8,128)} %get-tuple-element.59) | copy-start | bytes 4718596
  53.4 1.8 %copy-start.2 = (f32[12,24,24]{2,1,0:T(8,128)S(1)}, f32[12,24,24]{2,1,0:T(8,128)}, u32[]{:S(2)}) copy-start(f32[12,24,24]{2,1,0:T(8,128)} %copy-done.1) | copy-start | bytes 82948
  53.4 1.8 %copy-start.4 = (f32[12,24,24]{2,1,0:T(8,128)S(1)}, f32[12,24,24]{2,1,0:T(8,128)}, u32[]{:S(2)}) copy-start(f32[12,24,24]{2,1,0:T(8,128)} %copy-done.3) | copy-start | bytes 82948
  54.4 0.8 %copy-start.5 = (f32[128,128]{1,0:T(8,128)S(1)}, f32[128,128]{1,0:T(8,128)}, u32[]{:S(2)}) copy-start(f32[128,128]{1,0:T(8,128)} %get-tuple-element.34) | copy-start | bytes 196612
where the time goes:
time: 65.8 us; the launch traced here: 65.2 us
  local copies, waits for them, and re-layouts  15 us (23%)
  matrix products  14.1 us (21%)
  starting transfers between devices  10.7 us (16%)
  other arithmetic  7.17 us (11%)
  between operations  7.16 us (11%)
  blocking collectives  5.63 us (9%)
  waiting for transfers between devices  5.4 us (8%)
    dot_general x12, matrix products, highest(): jnp.dot(left_side, right_side, precision=lax.Precision.HIGHEST, preferred...  14.1 us
    ppermute x2, starting transfers between devices, extended(): lax.ppermute(lax.slice_in_dim(block, block.shape[dim] - width, None, axis...  6.32 us
    psum x1, blocking collectives, shards(): combined = lax.psum(summed, 'cond')  5.63 us
    reshape x2, local copies, waits for them, and re-layouts, tile_loss(): squared = (fields * fields).reshape(kernel_count, tile_size, 2, tile_size)  4.94 us
    ppermute x2, starting transfers between devices, extended(): lax.ppermute(lax.slice_in_dim(block, 0, width, axis=dim), axis, backward)  4.36 us
    reduce_sum x2, other arithmetic, tile_loss(): jnp.sum(squared, axis=(0, 2)) / (kernel_count * band_size * band_size)  3.94 us
    ppermute x2, waiting for transfers between devices, extended(): lax.ppermute(lax.slice_in_dim(block, 0, width, axis=dim), axis, backward)  3.85 us
    transpose x2, local copies, waits for them, and re-layouts, tile_loss(): jnp.transpose(stacked, (1, 0, 2))  1.86 us
  transfers between devices with their start and end apart: 4, of which 2 were waited for; matrix products, arithmetic and copies ran while one was open for 9% of the time, Pallas kernels for 0%

commit v1 on v0

v1 whole, which is shorter than its diff:
```python
import functools
import math

import jax
import jax.numpy as jnp
import numpy as np
from jax import lax
from jax.experimental import pallas as pl
from jax.experimental.pallas import tpu as pltpu
from jax.sharding import PartitionSpec as P

MARGIN = 128
BAND = 24
STEEP = 4.0
THRESH = 0.6

HALF = 64
AXES = ("row", "col", "cond")
BF = jnp.bfloat16
F32 = jnp.float32


def pieces(table, count):
    out, rest = [], np.asarray(table, np.float32)
    for _ in range(count):
        part = rest.astype(BF)
        out.append(part)
        rest = rest - part.astype(np.float32)
    return out


def angles(left, right, period):
    left, right = np.asarray(left, np.int64), np.asarray(right, np.int64)
    return (left[:, None] * right[None, :] % period) * (2.0 * math.pi / period)


def frequencies():
    return np.arange(BAND) - BAND // 2


def lanes(*blocks):
    rows = blocks[0][1].shape[0]
    width = -(-max(at + block.shape[1] for at, block in blocks) // 128) * 128
    out = np.zeros((rows, width))
    for at, block in blocks:
        out[:, at : at + block.shape[1]] = block
    return out


def rows_at(height, *blocks):
    out = np.zeros((height, blocks[0][1].shape[1]))
    for at, block in blocks:
        out[at : at + block.shape[0]] = block
    return out


def six(table):
    high, mid, low = pieces(table, 3)
    return np.concatenate([high, high, high, mid, mid, low], 1)


def three(table):
    high, low = pieces(table, 2)
    return np.concatenate([high, high, low], 1)


def stacked(table, count):
    return np.concatenate(pieces(table, count), 0)


def local_tables(tile, window):
    places = np.arange(tile)
    cols = []
    for at, shift in ((0, 0), (HALF, 2 * MARGIN), (2 * HALF, MARGIN), (3 * HALF, MARGIN)):
        phase = angles(places + shift, frequencies(), window)
        cols += [(at, np.cos(phase)), (at + BAND, -np.sin(phase))]
    col_table = lanes(*cols) / window
    real, imag = [], []
    for shift in (MARGIN, 0, 2 * MARGIN):
        phase = angles(frequencies(), places + shift, window)
        real.append(np.cos(phase))
        imag.append(-np.sin(phase))
    row_table = np.concatenate(real + imag, 0)
    return stacked(col_table, 3), six(row_table)


def field_tables(tile, window):
    count = 2 * BAND
    points = np.arange(count)
    phase = angles(frequencies(), points, count)
    cos, sin = np.cos(phase), np.sin(phase)
    real_rows = lanes((0, cos), (HALF, sin), (2 * HALF, -sin), (3 * HALF, cos))
    imag_rows = lanes((0, -sin), (HALF, cos), (2 * HALF, -cos), (3 * HALF, -sin))
    to_cols = rows_at(HALF, (0, real_rows), (BAND, imag_rows))
    to_rows = np.concatenate([cos.T, sin.T], 1)
    where = (np.arange(tile)[:, None] + MARGIN) / window - points[None, :] / count
    spread = np.ones((tile, count))
    for order in range(1, BAND):
        spread += 2.0 * np.cos(2.0 * math.pi * order * where)
    spread /= count
    spread_cols = rows_at(HALF, (0, spread.T))
    gather_cols = lanes((0, spread), (HALF, spread))
    from_rows = np.concatenate([cos, sin], 0)
    pad = np.zeros((HALF - count, BAND))
    c, s = cos.T, sin.T

    def both(real_part, imag_part):
        block = np.concatenate([real_part, imag_part], 1)
        return lanes((0, block), (HALF, block))

    blocks = [both(c, -s), both(s, c), both(-s, -c), both(c, -s)]
    empty = np.zeros((HALF - count, 2 * HALF))
    from_cols = np.concatenate([part for block in blocks for part in (block, empty)], 0)
    return (
        stacked(to_cols, 3),
        six(to_rows),
        stacked(spread_cols, 3),
        six(spread),
        three(spread.T),
        stacked(gather_cols, 2),
        three(from_rows),
        np.concatenate(pieces(from_cols, 2), 1),
    )


def adjoint_tables(tile, window):
    places = np.arange(tile) + MARGIN
    phase = angles(frequencies(), places, window)
    cos, sin = np.cos(phase), np.sin(phase)
    first = np.concatenate([cos, -sin], 1)
    second = np.concatenate([-sin, -cos], 1)
    cols = rows_at(
        2 * HALF, (0, first), (BAND, first), (HALF, second), (HALF + BAND, second)
    )
    rows = np.concatenate([cos.T, sin.T], 1) / window
    return stacked(cols, 2), three(rows)


def dot(left, right):
    return jnp.dot(left, right, preferred_element_type=F32)


def split(value, count):
    out, rest = [], value
    for step in range(count):
        part = rest.astype(BF)
        out.append(part)
        if step + 1 < count:
            rest = rest - part.astype(F32)
    return out


def lane_ids(shape):
    return lax.broadcasted_iota(jnp.int32, shape, len(shape) - 1)


def doubled(value):
    low_half = lane_ids(value.shape) < HALF
    high = value.astype(BF).astype(F32)
    rest = value - high
    mid = rest.astype(BF).astype(F32)
    first = jnp.where(low_half, high, rest).astype(BF)
    second = jnp.where(low_half, rest - mid, high).astype(BF)
    return jnp.concatenate([first, first, second], 1)


def doubled_weights(ref):
    size = ref.shape[0] // 3
    high, mid, low = ref[:size], ref[size : 2 * size], ref[2 * size :]
    return jnp.concatenate([high, high, mid, mid, high, low], 0)


def six_right(value):
    high, mid, low = split(value, 3)
    return jnp.concatenate([high, mid, low, high, mid, high], 0)


def three_right(value):
    high, low = split(value, 2)
    return jnp.concatenate([high, low, high], 0)


def local_kernel(where_ref, mask_ref, col_ref, row_ref, own_ref, send_ref):
    tile = mask_ref.shape[0]
    high, mid, low = split(mask_ref[...], 3)
    left = jnp.concatenate([high, mid, low, high, mid, high], 1)
    ch, cm, cl = col_ref[:tile], col_ref[tile : 2 * tile], col_ref[2 * tile :]
    right = jnp.concatenate([ch, ch, ch, cm, cm, cl], 0)
    partial = dot(left, right)
    both = dot(row_ref[...], six_right(partial))
    top, bottom = both[: 3 * BAND], both[3 * BAND :]
    lane = lane_ids(top.shape) % HALF
    width = top.shape[1]
    turned = jnp.where(
        lane < BAND,
        -pltpu.roll(bottom, width - BAND, 1),
        jnp.where(lane < 2 * BAND, pltpu.roll(bottom, BAND, 1), 0.0),
    )
    result = top + turned
    own = result[:BAND]
    below = result[BAND : 2 * BAND]
    above = result[2 * BAND :]
    down, valid = where_ref[0], where_ref[1]
    chosen = jnp.where(down == 1, below, above)
    chosen = jnp.where(valid == 1, chosen, 0.0)
    own_ref[:BAND] = own[:, : 2 * HALF]
    own_ref[BAND:] = own[:, 2 * HALF :]
    send_ref[:BAND] = chosen[:, : 2 * HALF]
    send_ref[BAND:] = chosen[:, 2 * HALF :]


def field_kernel(
    where_ref, cond_ref, dose_ref, own_ref, near_ref, far_ref, side_ref, other_ref, ker_a_ref,
    ker_b_ref, target_ref, to_cols_ref, to_rows_ref, spread_cols_ref, spread_ref,
    gather_rows_ref, gather_cols_ref, from_rows_ref, from_cols_ref, out_ref, cols_ref, field_ref,
):
    conds = cond_ref.shape[0]
    count = 2 * BAND
    total = ker_a_ref.shape[0] // BAND
    per = total // conds
    tile = target_ref.shape[0]

    def half(value, first, valid):
        keep = (lane_ids(value.shape) < HALF) == (first == 1)
        kept = jnp.where(keep & (valid == 1), value, 0.0)
        return kept + pltpu.roll(kept, HALF, 1)

    spectrum = own_ref[BAND:] + near_ref[BAND:] + far_ref[BAND:]
    spectrum += half(side_ref[...], where_ref[2], where_ref[3])
    spectrum += half(other_ref[...], where_ref[4], where_ref[5])
    lane = lane_ids(spectrum.shape) % HALF
    real = jnp.where(lane < BAND, spectrum, 0.0)
    imag = jnp.where(lane >= BAND, spectrum, 0.0)
    real = real + pltpu.roll(real, BAND, 1)
    imag = imag + pltpu.roll(imag, 2 * HALF - BAND, 1)

    ker_a = ker_a_ref[...].reshape(total, BAND, 2 * HALF)
    ker_b = ker_b_ref[...].reshape(total, BAND, 2 * HALF)
    product = (ker_a * real[None] + ker_b * imag[None]).reshape(total * BAND, 2 * HALF)
    cols_ref[...] = dot(doubled(product), doubled_weights(to_cols_ref))

    sums = [jnp.zeros((count, 2 * HALF), F32) for _ in range(conds)]
    to_rows = to_rows_ref[...]
    for pair in range(total // 2):
        rights = []
        for k in (2 * pair, 2 * pair + 1):
            block = cols_ref[k * BAND : (k + 1) * BAND, :]
            block = jnp.concatenate([block[:, : 2 * HALF], block[:, 2 * HALF :]], 0)
            rights.append(six_right(block))
        both = dot(to_rows, jnp.concatenate(rights, 1))
        field_ref[pair] = both
        squares = both * both
        for part in range(2):
            c = (2 * pair + part) // per
            sums[c] = sums[c] + squares[:, part * 2 * HALF : (part + 1) * 2 * HALF]

    coarse = jnp.concatenate([value + pltpu.roll(value, HALF, 1) for value in sums], 0)
    wide = dot(doubled(coarse), doubled_weights(spread_cols_ref))
    right = jnp.concatenate(
        [six_right(wide[c * count : (c + 1) * count]) for c in range(conds)], 1
    )
    image = dot(spread_ref[...], right)

    goal = target_ref[...].astype(F32)
    norm = 1.0 / (per * BAND * BAND)
    slopes = []
    for c in range(conds):
        strength = dose_ref[cond_ref[c]]
        intensity = image[:, c * tile : (c + 1) * tile] * norm
        resist = jax.nn.sigmoid(STEEP * (strength * intensity - THRESH))
        slope = (resist - goal) * resist * (1.0 - resist)
        slopes.append(slope * (4.0 * STEEP * norm * strength))
    back = dot(gather_rows_ref[...], three_right(jnp.concatenate(slopes, 1)))
    high, low = split(
        jnp.concatenate([back[:, c * tile : (c + 1) * tile] for c in range(conds)], 0), 2
    )
    gh, gl = gather_cols_ref[:tile], gather_cols_ref[tile:]
    slope = dot(
        jnp.concatenate([high, low, high], 1), jnp.concatenate([gh, gh, gl], 0)
    )

    from_rows = from_rows_ref[...]
    for pair in range(total // 2):
        weight = [
            slope[((2 * pair + part) // per) * count : ((2 * pair + part) // per + 1) * count]
            for part in range(2)
        ]
        scaled = field_ref[pair] * jnp.concatenate(weight, 1)
        back = dot(from_rows, three_right(scaled))
        for part in range(2):
            block = back[:, part * 2 * HALF : (part + 1) * 2 * HALF]
            k = 2 * pair + part
            cols_ref[k * BAND : (k + 1) * BAND, :] = jnp.concatenate(
                [block[:BAND], block[BAND:]], 1
            )
    high, low = split(cols_ref[...], 2)
    weights = from_cols_ref[...]
    first = dot(high, weights)
    back = first[:, : 2 * HALF] + first[:, 2 * HALF :] + dot(low, weights[:, : 2 * HALF])
    back = back.reshape(total, BAND, 2 * HALF)
    sum_a = jnp.sum(ker_a_ref[...].reshape(total, BAND, 2 * HALF) * back, axis=0)
    sum_b = jnp.sum(ker_b_ref[...].reshape(total, BAND, 2 * HALF) * back, axis=0)
    out_ref[...] = jnp.where(lane_ids(sum_a.shape) < HALF, sum_a, sum_b)


def adjoint_kernel(mine_ref, theirs_ref, cols_ref, rows_ref, out_ref):
    tile = out_ref.shape[1]
    high, low = split(mine_ref[...] + theirs_ref[...], 2)
    size = cols_ref.shape[0] // 2
    ch, cl = cols_ref[:size], cols_ref[size:]
    halves = dot(jnp.concatenate([high, low, high], 1), jnp.concatenate([ch, ch, cl], 0))
    joined = jnp.concatenate([halves[:, :tile], halves[:, tile:]], 0)
    out_ref[...] = dot(rows_ref[...], three_right(joined))


VMEM = pl.BlockSpec(memory_space=pltpu.VMEM)
SMEM = pl.BlockSpec(memory_space=pltpu.SMEM)


def call(body, outs, specs, args, scratch=(), flops=1000000):
    shapes = [jax.ShapeDtypeStruct(shape, F32) for shape in outs]
    one = len(outs) == 1
    return pl.pallas_call(
        body,
        out_shape=shapes[0] if one else shapes,
        in_specs=specs,
        out_specs=VMEM if one else [VMEM] * len(outs),
        scratch_shapes=list(scratch),
        cost_estimate=pl.CostEstimate(flops=flops, bytes_accessed=1000000, transcendentals=0),
    )(*args)


def partner(at, core, size):
    other = at ^ 1 if core == 0 else ((at + 1) ^ 1) - 1
    return other if 0 <= other < size else None


def swaps(mesh_shape, along):
    rows, cols, cores = mesh_shape
    out = []
    for r in range(rows):
        for c in range(cols):
            for k in range(cores):
                at, size = (r, rows) if along == 0 else (c, cols)
                other = partner(at, k, size)
                if other is not None:
                    to = (other, c, k) if along == 0 else (r, other, k)
                elif along == 0:
                    to = (r, c ^ 1, k)
                else:
                    to = (r ^ 1, c, k)
                if to[0] < rows and to[1] < cols:
                    out.append((((r * cols) + c) * cores + k, ((to[0] * cols) + to[1]) * cores + to[2]))
    return out


def toward(at, core, size):
    onward = (at + core) % 2 == 0
    other = jnp.where(onward, at + 1, at - 1)
    valid = (other >= 0) & (other < size)
    return onward.astype(jnp.int32), valid.astype(jnp.int32)


def shards(mesh_shape, mask, target, cond_index, kernels, dose):
    tile = mask.shape[0]
    window = tile + 2 * MARGIN
    rows, cols, cores = mesh_shape
    row, col, core = (lax.axis_index(name) for name in AXES)
    down, valid = toward(row, core, rows)
    right, side_valid = toward(col, core, cols)
    other_right, other_valid = toward(col, 1 - core, cols)
    where = jnp.stack([down, valid, 1 - right, side_valid, 1 - other_right, other_valid])

    col_table, row_table = local_tables(tile, window)
    block = (2 * BAND, 2 * HALF)
    own, send = call(
        local_kernel, [block, block], [SMEM, VMEM, VMEM, VMEM], (where, mask, col_table, row_table)
    )
    swap = [(0, 1), (1, 0)]
    near = lax.ppermute(send, AXES, swaps(mesh_shape, 0))
    far = lax.ppermute(near, "cond", swap)
    message = own[:BAND] + near[:BAND] + far[:BAND]
    side = lax.ppermute(message, AXES, swaps(mesh_shape, 1))
    other = lax.ppermute(side, "cond", swap)

    conds = cond_index.shape[0]
    count = kernels.shape[2]
    chosen = [
        lax.dynamic_index_in_dim(kernels, cond_index[c], 0, keepdims=False).reshape(
            2, count * BAND, BAND
        )
        for c in range(conds)
    ]
    real = jnp.concatenate([value[0] for value in chosen], 0)
    imag = jnp.concatenate([value[1] for value in chosen], 0)
    gap = jnp.zeros((real.shape[0], HALF - 2 * BAND), F32)
    ker_a = jnp.concatenate([real, imag, gap] * 2, 1)
    ker_b = jnp.concatenate([-imag, real, gap] * 2, 1)

    total = conds * count
    cotangent = call(
        field_kernel,
        [(BAND, 2 * HALF)],
        [SMEM] * 3 + [VMEM] * 16,
        (where, cond_index, dose, own, near, far, side, other, ker_a, ker_b, target)
        + field_tables(tile, window),
        scratch=[
            pltpu.VMEM((total * BAND, 4 * HALF), F32),
            pltpu.VMEM((total // 2, 2 * BAND, 4 * HALF), F32),
        ],
    )
    theirs = lax.ppermute(cotangent, "cond", swap)
    return call(
        adjoint_kernel, [(tile, tile)], [VMEM] * 4, (cotangent, theirs) + adjoint_tables(tile, window)
    )


def solution(mesh):
    in_specs = (P("row", "col"), P("row", "col"), P("cond"), P(), P())
    out_specs = P("row", "col")
    shape = tuple(mesh.shape[name] for name in AXES)
    body = functools.partial(shards, shape)
    return jax.shard_map(body, mesh=mesh, in_specs=in_specs, out_specs=out_specs, check_vma=False)
```

time: 65.8 us -> 29.2 us (0.44)
  the two profiles are of different devices: /device:TPU:5 before, /device:TPU:0 now
where the time goes in v1:
time: 29.2 us; the launch traced here: 28.8 us
  Pallas kernels  8.34 us (29%)
  local copies, waits for them, and re-layouts  7.69 us (26%)
  starting transfers between devices  4.62 us (16%)
  waiting for transfers between devices  4.3 us (15%)
  between operations  3.87 us (13%)
    pallas_call x3, Pallas kernels, call(): pl.pallas_call(body, out_shape=shapes[0] if one else shapes, in_specs=spe...  8.34 us
    ppermute x1, starting transfers between devices, shards(): near = lax.ppermute(send, AXES, swaps(mesh_shape, 0))  2.97 us
    unnamed x16, local copies, waits for them, and re-layouts  2.39 us
    ppermute x1, waiting for transfers between devices, shards(): side = lax.ppermute(message, AXES, swaps(mesh_shape, 1))  1.88 us
    ppermute x1, starting transfers between devices, shards(): side = lax.ppermute(message, AXES, swaps(mesh_shape, 1))  1.58 us
    ppermute x1, waiting for transfers between devices, shards(): theirs = lax.ppermute(cotangent, 'cond', swap)  1.38 us
    slice x1, local copies, waits for them, and re-layouts, shards(): imag = jnp.concatenate([value[1] for value in chosen], 0)  1.26 us
    concatenate x1, local copies, waits for them, and re-layouts, shards(): ker_b = jnp.concatenate([-imag, real, gap] * 2, 1)  1.17 us
  transfers between devices with their start and end apart: 5, of which 3 were waited for; matrix products, arithmetic and copies ran while one was open for 16% of the time, Pallas kernels for 0%

profile of v1, /device:TPU:0, one launch (start us, length us, event | category | flops | bytes accessed | tf_op | source)
XLA Modules:
  0.0 28.8 jit_solution(496037935879534663)
XLA Ops:
  0.0 0.7 %stack.43.where_ref = s32[6]{0:T(128)} concatenate(s32[1]{0:T(128)} %bitcast, s32[1]{0:T(128)} %bitcast.1, s32[1]{0:T(128)} %bitcast.2, s32[1]{0:T(128)} %bitcast.3, s32[1]{0:T(128)} %bitcast.4, s32[1]{0:T(128)} %bitcast.5), dimensions={0} | concatenate | bytes 48 | tf_op jit(solution)/shard_map/stack | solution.py:372
  0.7 2.3 %shard_map.163 = (f32[48,128]{1,0:T(8,128)}, f32[48,128]{1,0:T(8,128)}) custom-call(s32[6]{0:T(128)} %stack.43.where_ref, f32[128,128]{1,0:T(8,128)} %mask_ref.1, bf16[384,256]{1,0:T(8,128)(2,1)} %constant.72.clone.col_ref, bf16[144,768]{1,0:T(8,128)(2,1)} %constant.73.clone.row_ref), custom_call_target="tpu_custom_call" | custom-call | flops 1000000 | bytes 1000000 | tf_op jit(solution)/shard_map/pallas_call | solution.py:323
  2.9 0.0 copy-start.6
  2.9 3.0 %collective-permute-start = (f32[48,128]{1,0:T(8,128)}, f32[48,128]{1,0:T(8,128)S(1)}, u32[]{:S(2)}, u32[]{:S(2)}) collective-permute-start(f32[48,128]{1,0:T(8,128)} %get-tuple-element.8), channel_id=1, source_target_pairs={{0,8},{1,3},{2,10},{3,1},{4,12},{5,7},{6,14},{7,5},{8,0},{9,17},{1... | collective-permute-start | bytes 73736 | tf_op jit(solution)/shard_map/ppermute | solution.py:380
  5.9 0.0 copy-done.6
  5.9 0.6 %fusion = (s32[1]{0:T(128)}, s32[1]{0:T(128)}) fusion(s32[2]{0:T(128)S(1)} %copy-done.6), kind=kLoop, calls=%fused_computation.10 | loop fusion | bytes 16 | tf_op jit(solution)/shard_map/slice | solution.py:389
  10.3 1.3 %dynamic-slice_reduce_fusion = (f32[12,576]{1,0:T(8,128)S(1)}, f32[12,576]{1,0:T(8,128)S(1)}, f32[12,576]{1,0:T(8,128)S(1)}, f32[12,576]{1,0:T(8,128)S(1)}) fusion(f32[8,2,12,576]{3,1,2,0:T(2,128)} %param.20, s32[]{:T(128)S(6)} %select_n.38, s32[]{:T(128)S(6)} %add.57, s32[]{:T(128)S(6)} %select_n.37), kind=kLoop, calls=%fused_computation | loop fusion | bytes 221196 | tf_op jit(solution)/shard_map/slice | solution.py:395
  11.5 0.1 squeeze.22
  11.6 0.0 collective-permute-done.near_ref
  11.6 0.0 copy-start.1
  11.6 0.1 collective-permute-start.1
  11.7 0.0 copy-start
  11.8 0.1 squeeze.25
  11.9 1.0 %collective-permute-done.1.far_ref = f32[48,128]{1,0:T(8,128)S(1)} collective-permute-done((f32[48,128]{1,0:T(8,128)S(1)}, f32[48,128]{1,0:T(8,128)S(1)}, u32[]{:S(2)}, u32[]{:S(2)}) %collective-permute-start.1) | collective-permute-done | bytes 24608 | tf_op jit(solution)/shard_map/ppermute | solution.py:381
  12.9 0.0 copy-start.2
  12.9 0.0 copy-done.1
  12.9 0.0 copy-done
  12.9 0.6 %copy-done.2 = f32[48,128]{1,0:T(8,128)} copy-done((f32[48,128]{1,0:T(8,128)}, f32[48,128]{1,0:T(8,128)S(1)}, u32[]{:S(2)}) %copy-start.2) | copy-done | bytes 24600
  13.5 1.6 %collective-permute-start.2 = (f32[24,128]{1,0:T(8,128)S(1)}, f32[24,128]{1,0:T(8,128)S(1)}, u32[]{:S(2)}, u32[]{:S(2)}) collective-permute-start(f32[24,128]{1,0:T(8,128)S(1)} %slice_add_fusion), channel_id=1, source_target_pairs={{0,2},{1,9},{2,0},{3,5},{4,6},{5,3},{6,4},{7,15},{8,10},{9,1},{10,... | collective-permute-start | bytes 36872 | tf_op jit(solution)/shard_map/ppermute | solution.py:383
  15.1 0.1 squeeze.24
  15.2 0.1 squeeze.26
  15.3 1.9 %collective-permute-done.2.side_ref = f32[24,128]{1,0:T(8,128)S(1)} collective-permute-done((f32[24,128]{1,0:T(8,128)S(1)}, f32[24,128]{1,0:T(8,128)S(1)}, u32[]{:S(2)}, u32[]{:S(2)}) %collective-permute-start.2) | collective-permute-done | bytes 12320 | tf_op jit(solution)/shard_map/ppermute | solution.py:383
  17.2 0.0 copy-start.3
  17.2 0.0 collective-permute-start.3
  17.2 0.6 %copy-done.3 = f32[24,128]{1,0:T(8,128)} copy-done((f32[24,128]{1,0:T(8,128)}, f32[24,128]{1,0:T(8,128)S(1)}, u32[]{:S(2)}) %copy-start.3) | copy-done | bytes 12312
  17.9 1.2 %concatenate.14.ker_a_ref = f32[576,128]{1,0:T(8,128)} concatenate(f32[576,24]{1,0:T(8,128)S(1)} %get-tuple-element.15, f32[576,24]{1,0:T(8,128)S(1)} %get-tuple-element.16, f32[576,16]{1,0:T(8,128)S(1)} %broadcast_in_dim.3, f32[576,24]{1,0:T(8,128)S(1)} %get-tuple-element.15, f32[576,24]{1,0:T(8,128)S(1)} %get-tuple-element.16, f32[576,16]{1,0:T(8,128)S(1)} %broadcast_in_dim.3), dimensions={1} | concatenate | bytes 589824 | tf_op jit(solution)/shard_map/concatenate | solution.py:397
  19.0 1.2 %concatenate.15.ker_b_ref = f32[576,128]{1,0:T(8,128)} concatenate(f32[576,24]{1,0:T(8,128)S(1)} %neg.3, f32[576,24]{1,0:T(8,128)S(1)} %get-tuple-element.15, f32[576,16]{1,0:T(8,128)S(1)} %broadcast_in_dim.3, f32[576,24]{1,0:T(8,128)S(1)} %neg.3, f32[576,24]{1,0:T(8,128)S(1)} %get-tuple-element.15, f32[576,16]{1,0:T(8,128)S(1)} %broadcast_in_dim.3), dimensions={1} | concatenate | bytes 589824 | tf_op jit(solution)/shard_map/concatenate | solution.py:398
  20.2 0.0 collective-permute-done.3.other_ref
  20.2 0.0 copy-start.4
  20.2 0.6 %copy-done.4 = f32[24,128]{1,0:T(8,128)} copy-done((f32[24,128]{1,0:T(8,128)}, f32[24,128]{1,0:T(8,128)S(1)}, u32[]{:S(2)}) %copy-start.4) | copy-done | bytes 12312
  20.8 4.2 %shard_map.164.mine_ref = f32[24,128]{1,0:T(8,128)} custom-call(s32[6]{0:T(128)} %stack.43.where_ref, s32[2]{0:T(128)} %cond_ref.1, f32[8]{0:T(128)} %dose_ref.1, f32[48,128]{1,0:T(8,128)} %get-tuple-element.7.own_ref, f32[48,128]{1,0:T(8,128)} %copy-done.1, f32[48,128]{1,0:T(8,128)} %copy-done.2, f32[24,128]{1,0:T(8,128)} %copy-done.3, ...), custom_call_target="tpu_custom_call" | custom-call | flops 1000000 | bytes 1000000 | tf_op jit(solution)/shard_map/pallas_call | solution.py:323
  25.0 0.0 collective-permute-start.4
  25.0 1.4 %collective-permute-done.4.theirs_ref = f32[24,128]{1,0:T(8,128)S(1)} collective-permute-done((f32[24,128]{1,0:T(8,128)}, f32[24,128]{1,0:T(8,128)S(1)}, u32[]{:S(2)}, u32[]{:S(2)}) %collective-permute-start.4) | collective-permute-done | bytes 12320 | tf_op jit(solution)/shard_map/ppermute | solution.py:412
  26.3 0.0 copy-start.5
  26.3 0.6 %copy-done.5 = f32[24,128]{1,0:T(8,128)} copy-done((f32[24,128]{1,0:T(8,128)}, f32[24,128]{1,0:T(8,128)S(1)}, u32[]{:S(2)}) %copy-start.5) | copy-done | bytes 12312
  26.9 1.9 %shard_map.165 = f32[128,128]{1,0:T(8,128)} custom-call(f32[24,128]{1,0:T(8,128)} %shard_map.164.mine_ref, f32[24,128]{1,0:T(8,128)} %copy-done.5, bf16[256,256]{1,0:T(8,128)(2,1)} %constant.82.clone.cols_ref, bf16[128,144]{1,0:T(8,128)(2,1)} %constant.83.clone.rows_ref), custom_call_target="tpu_custom_call" | custom-call | flops 1000000 | bytes 1000000 | tf_op jit(solution)/shard_map/pallas_call | solution.py:323
  (6 shorter events, 0.1 us)
Async XLA Ops:
  2.9 3.0 %copy-start.6 = (s32[2]{0:T(128)S(1)}, s32[2]{0:T(128)}, u32[]{:S(2)}) copy-start(s32[2]{0:T(128)} %cond_ref.1) | copy-start | bytes 28
  2.9 8.7 %collective-permute-start = (f32[48,128]{1,0:T(8,128)}, f32[48,128]{1,0:T(8,128)S(1)}, u32[]{:S(2)}, u32[]{:S(2)}) collective-permute-start(f32[48,128]{1,0:T(8,128)} %get-tuple-element.8), channel_id=1, source_target_pairs={{0,8},{1,3},{2,10},{3,1},{4,12},{5,7},{6,14},{7,5},{8,0},{9,17},{1... | collective-permute-start | bytes 73736 | tf_op jit(solution)/shard_map/ppermute | solution.py:380
  11.6 1.3 %copy-start.1 = (f32[48,128]{1,0:T(8,128)}, f32[48,128]{1,0:T(8,128)S(1)}, u32[]{:S(2)}) copy-start(f32[48,128]{1,0:T(8,128)S(1)} %collective-permute-done.near_ref) | copy-start | bytes 73732
  11.6 1.3 %collective-permute-start.1 = (f32[48,128]{1,0:T(8,128)S(1)}, f32[48,128]{1,0:T(8,128)S(1)}, u32[]{:S(2)}, u32[]{:S(2)}) collective-permute-start(f32[48,128]{1,0:T(8,128)S(1)} %collective-permute-done.near_ref), channel_id=1, source_target_pairs={{0,1},{1,0},{2,3},{3,2},{4,5},{5,4},{6,7},{7,6},{8,9},{9,8},{10,11... | collective-permute-start | bytes 73736 | tf_op jit(solution)/shard_map/ppermute | solution.py:381
  11.7 1.2 %copy-start = (f32[48,128]{1,0:T(8,128)S(1)}, f32[48,128]{1,0:T(8,128)}, u32[]{:S(2)}) copy-start(f32[48,128]{1,0:T(8,128)} %get-tuple-element.7.own_ref) | copy-start | bytes 73732
  12.9 0.6 %copy-start.2 = (f32[48,128]{1,0:T(8,128)}, f32[48,128]{1,0:T(8,128)S(1)}, u32[]{:S(2)}) copy-start(f32[48,128]{1,0:T(8,128)S(1)} %collective-permute-done.1.far_ref) | copy-start | bytes 73732
  13.5 3.7 %collective-permute-start.2 = (f32[24,128]{1,0:T(8,128)S(1)}, f32[24,128]{1,0:T(8,128)S(1)}, u32[]{:S(2)}, u32[]{:S(2)}) collective-permute-start(f32[24,128]{1,0:T(8,128)S(1)} %slice_add_fusion), channel_id=1, source_target_pairs={{0,2},{1,9},{2,0},{3,5},{4,6},{5,3},{6,4},{7,15},{8,10},{9,1},{10,... | collective-permute-start | bytes 36872 | tf_op jit(solution)/shard_map/ppermute | solution.py:383
  17.2 0.6 %copy-start.3 = (f32[24,128]{1,0:T(8,128)}, f32[24,128]{1,0:T(8,128)S(1)}, u32[]{:S(2)}) copy-start(f32[24,128]{1,0:T(8,128)S(1)} %collective-permute-done.2.side_ref) | copy-start | bytes 36868
  17.2 3.0 %collective-permute-start.3 = (f32[24,128]{1,0:T(8,128)S(1)}, f32[24,128]{1,0:T(8,128)S(1)}, u32[]{:S(2)}, u32[]{:S(2)}) collective-permute-start(f32[24,128]{1,0:T(8,128)S(1)} %collective-permute-done.2.side_ref), channel_id=1, source_target_pairs={{0,1},{1,0},{2,3},{3,2},{4,5},{5,4},{6,7},{7,6},{8,9},{9,8},{10,11... | collective-permute-start | bytes 36872 | tf_op jit(solution)/shard_map/ppermute | solution.py:384
  20.2 0.6 %copy-start.4 = (f32[24,128]{1,0:T(8,128)}, f32[24,128]{1,0:T(8,128)S(1)}, u32[]{:S(2)}) copy-start(f32[24,128]{1,0:T(8,128)S(1)} %collective-permute-done.3.other_ref) | copy-start | bytes 36868
  25.0 1.4 %collective-permute-start.4 = (f32[24,128]{1,0:T(8,128)}, f32[24,128]{1,0:T(8,128)S(1)}, u32[]{:S(2)}, u32[]{:S(2)}) collective-permute-start(f32[24,128]{1,0:T(8,128)} %shard_map.164.mine_ref), channel_id=1, source_target_pairs={{0,1},{1,0},{2,3},{3,2},{4,5},{5,4},{6,7},{7,6},{8,9},{9,8},{10,11... | collective-permute-start | bytes 36872 | tf_op jit(solution)/shard_map/ppermute | solution.py:412
  26.3 0.6 %copy-start.5 = (f32[24,128]{1,0:T(8,128)}, f32[24,128]{1,0:T(8,128)S(1)}, u32[]{:S(2)}) copy-start(f32[24,128]{1,0:T(8,128)S(1)} %collective-permute-done.4.theirs_ref) | copy-start | bytes 36868

commit v2 on v1

--- a/solution.py
+++ b/solution.py
@@ -136,6 +136,12 @@
     return stacked(cols, 2), three(rows)
 
 
+def toward(at, core, size):
+    onward = lax.rem(at + core, 2) == 0
+    other = jnp.where(onward, at + 1, at - 1)
+    return onward, (other >= 0) & (other < size)
+
+
 def dot(left, right):
     return jnp.dot(left, right, preferred_element_type=F32)
 
@@ -180,7 +186,7 @@
     return jnp.concatenate([high, low, high], 0)
 
 
-def local_kernel(where_ref, mask_ref, col_ref, row_ref, own_ref, send_ref):
+def local_kernel(mesh_shape, mask_ref, col_ref, row_ref, own_ref, send_ref):
     tile = mask_ref.shape[0]
     high, mid, low = split(mask_ref[...], 3)
     left = jnp.concatenate([high, mid, low, high, mid, high], 1)
@@ -200,34 +206,51 @@
     own = result[:BAND]
     below = result[BAND : 2 * BAND]
     above = result[2 * BAND :]
-    down, valid = where_ref[0], where_ref[1]
-    chosen = jnp.where(down == 1, below, above)
-    chosen = jnp.where(valid == 1, chosen, 0.0)
+    down, valid = toward(lax.axis_index("row"), lax.axis_index("cond"), mesh_shape[0])
+    chosen = jnp.where(down, below, above)
+    chosen = jnp.where(valid, chosen, 0.0)
     own_ref[:BAND] = own[:, : 2 * HALF]
     own_ref[BAND:] = own[:, 2 * HALF :]
     send_ref[:BAND] = chosen[:, : 2 * HALF]
     send_ref[BAND:] = chosen[:, 2 * HALF :]
 
 
+def select_kernel(cond_ref, dose_ref, kernels_ref, out_ref, strength_ref, sems):
+    conds = cond_ref.shape[0]
+    copies = [
+        pltpu.make_async_copy(kernels_ref.at[cond_ref[c]], out_ref.at[c], sems.at[c])
+        for c in range(conds)
+    ]
+    for copy in copies:
+        copy.start()
+    for c in range(conds):
+        strength_ref[c] = jnp.full(strength_ref.shape[1:], dose_ref[cond_ref[c]], F32)
+    for copy in copies:
+        copy.wait()
+
+
 def field_kernel(
-    where_ref, cond_ref, dose_ref, own_ref, near_ref, far_ref, side_ref, other_ref, ker_a_ref,
+    mesh_shape, strength_ref, own_ref, near_ref, far_ref, side_ref, other_ref, ker_a_ref,
     ker_b_ref, target_ref, to_cols_ref, to_rows_ref, spread_cols_ref, spread_ref,
     gather_rows_ref, gather_cols_ref, from_rows_ref, from_cols_ref, out_ref, cols_ref, field_ref,
 ):
-    conds = cond_ref.shape[0]
+    conds = strength_ref.shape[0]
     count = 2 * BAND
     total = ker_a_ref.shape[0] // BAND
     per = total // conds
     tile = target_ref.shape[0]
 
-    def half(value, first, valid):
-        keep = (lane_ids(value.shape) < HALF) == (first == 1)
-        kept = jnp.where(keep & (valid == 1), value, 0.0)
+    col, core = lax.axis_index("col"), lax.axis_index("cond")
+
+    def half(value, core):
+        onward, valid = toward(col, core, mesh_shape[1])
+        low_half = lane_ids(value.shape) < HALF
+        kept = jnp.where(onward, jnp.where(low_half, 0.0, value), jnp.where(low_half, value, 0.0))
+        kept = jnp.where(valid, kept, 0.0)
         return kept + pltpu.roll(kept, HALF, 1)
 
     spectrum = own_ref[BAND:] + near_ref[BAND:] + far_ref[BAND:]
-    spectrum += half(side_ref[...], where_ref[2], where_ref[3])
-    spectrum += half(other_ref[...], where_ref[4], where_ref[5])
+    spectrum += half(side_ref[...], core) + half(other_ref[...], 1 - core)
     lane = lane_ids(spectrum.shape) % HALF
     real = jnp.where(lane < BAND, spectrum, 0.0)
     imag = jnp.where(lane >= BAND, spectrum, 0.0)
@@ -265,7 +288,7 @@
     norm = 1.0 / (per * BAND * BAND)
     slopes = []
     for c in range(conds):
-        strength = dose_ref[cond_ref[c]]
+        strength = strength_ref[c][:1]
         intensity = image[:, c * tile : (c + 1) * tile] * norm
         resist = jax.nn.sigmoid(STEEP * (strength * intensity - THRESH))
         slope = (resist - goal) * resist * (1.0 - resist)
@@ -317,7 +340,7 @@
 SMEM = pl.BlockSpec(memory_space=pltpu.SMEM)
 
 
-def call(body, outs, specs, args, scratch=(), flops=1000000):
+def call(body, outs, specs, args, scratch=(), flops=1000000, grant=8):
     shapes = [jax.ShapeDtypeStruct(shape, F32) for shape in outs]
     one = len(outs) == 1
     return pl.pallas_call(
@@ -326,6 +349,7 @@
         in_specs=specs,
         out_specs=VMEM if one else [VMEM] * len(outs),
         scratch_shapes=list(scratch),
+        compiler_params=pltpu.CompilerParams(vmem_limit_bytes=grant * 2**20),
         cost_estimate=pl.CostEstimate(flops=flops, bytes_accessed=1000000, transcendentals=0),
     )(*args)
 
@@ -354,27 +378,14 @@
     return out
 
 
-def toward(at, core, size):
-    onward = (at + core) % 2 == 0
-    other = jnp.where(onward, at + 1, at - 1)
-    valid = (other >= 0) & (other < size)
-    return onward.astype(jnp.int32), valid.astype(jnp.int32)
-
-
 def shards(mesh_shape, mask, target, cond_index, kernels, dose):
     tile = mask.shape[0]
     window = tile + 2 * MARGIN
-    rows, cols, cores = mesh_shape
-    row, col, core = (lax.axis_index(name) for name in AXES)
-    down, valid = toward(row, core, rows)
-    right, side_valid = toward(col, core, cols)
-    other_right, other_valid = toward(col, 1 - core, cols)
-    where = jnp.stack([down, valid, 1 - right, side_valid, 1 - other_right, other_valid])
-
     col_table, row_table = local_tables(tile, window)
     block = (2 * BAND, 2 * HALF)
     own, send = call(
-        local_kernel, [block, block], [SMEM, VMEM, VMEM, VMEM], (where, mask, col_table, row_table)
+        functools.partial(local_kernel, mesh_shape), [block] * 2, [VMEM] * 3,
+        (mask, col_table, row_table),
     )
     swap = [(0, 1), (1, 0)]
     near = lax.ppermute(send, AXES, swaps(mesh_shape, 0))
@@ -385,24 +396,24 @@
 
     conds = cond_index.shape[0]
     count = kernels.shape[2]
-    chosen = [
-        lax.dynamic_index_in_dim(kernels, cond_index[c], 0, keepdims=False).reshape(
-            2, count * BAND, BAND
-        )
-        for c in range(conds)
-    ]
-    real = jnp.concatenate([value[0] for value in chosen], 0)
-    imag = jnp.concatenate([value[1] for value in chosen], 0)
+    chosen, strength = call(
+        select_kernel, [(conds, count, 2, BAND * BAND), (conds, 8, tile)],
+        [SMEM, SMEM, pl.BlockSpec(memory_space=pl.ANY)],
+        (cond_index, dose, jnp.transpose(kernels, (0, 2, 1, 3))),
+        scratch=[pltpu.SemaphoreType.DMA((conds,))],
+    )
+    real = chosen[:, :, 0].reshape(conds * count * BAND, BAND)
+    imag = chosen[:, :, 1].reshape(conds * count * BAND, BAND)
     gap = jnp.zeros((real.shape[0], HALF - 2 * BAND), F32)
     ker_a = jnp.concatenate([real, imag, gap] * 2, 1)
     ker_b = jnp.concatenate([-imag, real, gap] * 2, 1)
 
     total = conds * count
     cotangent = call(
-        field_kernel,
+        functools.partial(field_kernel, mesh_shape),
         [(BAND, 2 * HALF)],
-        [SMEM] * 3 + [VMEM] * 16,
-        (where, cond_index, dose, own, near, far, side, other, ker_a, ker_b, target)
+        [VMEM] * 17,
+        (strength, own, near, far, side, other, ker_a, ker_b, target)
         + field_tables(tile, window),
         scratch=[
             pltpu.VMEM((total * BAND, 4 * HALF), F32),

time: 29.2 us -> 20.5 us (0.70)
  Pallas kernels: 8.34 us -> 4.54 us
  between operations: 3.87 us -> 0.19 us
  local copies, waits for them, and re-layouts: 7.69 us -> 4.85 us
  starting transfers between devices: 4.62 us -> 5.86 us
  waiting for transfers between devices: 4.3 us -> 4.76 us
    pallas_call x3 -> x4, Pallas kernels: 8.34 us -> 4.54 us  [call(): pl.pallas_call(body, out_shape=shapes[0] if one else shapes, in_specs=spe...]
    ppermute x1, waiting for transfers between devices: 0.01 us -> 1.81 us  [shards(): near = lax.ppermute(send, AXES, swaps(mesh_shape, 0))]
    slice x2 -> x1, local copies, waits for them, and re-layouts: 1.85 us -> 0.32 us  [shards(): imag = chosen[:, :, 1].reshape(conds * count * BAND, BAND)]
    ppermute x1, waiting for transfers between devices: 1.88 us -> 0.93 us  [shards(): side = lax.ppermute(message, AXES, swaps(mesh_shape, 1))]
    unnamed x16 -> x34, local copies, waits for them, and re-layouts: 2.39 us -> 3.26 us
    concatenate x1, local copies, waits for them, and re-layouts: 1.17 us -> 0.48 us  [shards(): ker_b = jnp.concatenate([-imag, real, gap] * 2, 1)]
    ppermute x1, starting transfers between devices: 1.58 us -> 2.25 us  [shards(): side = lax.ppermute(message, AXES, swaps(mesh_shape, 1))]
    concatenate x1, local copies, waits for them, and re-layouts: 1.16 us -> 0.48 us  [shards(): ker_a = jnp.concatenate([real, imag, gap] * 2, 1)]
  transfers between devices with their start and end apart: 5 -> 5, of which waited for: 3 -> 4; matrix products, arithmetic and copies ran while one was open for 16% -> 8% of each run, Pallas kernels for 0% -> 4%
where the time goes in v2:
time: 20.5 us; the launch traced here: 20.2 us
  starting transfers between devices  5.86 us (29%)
  local copies, waits for them, and re-layouts  4.85 us (24%)
  waiting for transfers between devices  4.76 us (23%)
  Pallas kernels  4.54 us (22%)
    pallas_call x4, Pallas kernels, call(): pl.pallas_call(body, out_shape=shapes[0] if one else shapes, in_specs=spe...  4.54 us
    unnamed x34, local copies, waits for them, and re-layouts  3.26 us
    ppermute x1, starting transfers between devices, shards(): near = lax.ppermute(send, AXES, swaps(mesh_shape, 0))  3.03 us
    ppermute x1, starting transfers between devices, shards(): side = lax.ppermute(message, AXES, swaps(mesh_shape, 1))  2.25 us
    ppermute x1, waiting for transfers between devices, shards(): near = lax.ppermute(send, AXES, swaps(mesh_shape, 0))  1.81 us
    ppermute x1, waiting for transfers between devices, shards(): far = lax.ppermute(near, 'cond', swap)  1.19 us
    ppermute x1, waiting for transfers between devices, shards(): side = lax.ppermute(message, AXES, swaps(mesh_shape, 1))  0.93 us
    ppermute x1, waiting for transfers between devices, shards(): theirs = lax.ppermute(cotangent, 'cond', swap)  0.83 us
  transfers between devices with their start and end apart: 5, of which 4 were waited for; matrix products, arithmetic and copies ran while one was open for 8% of the time, Pallas kernels for 4%

profile of v2, /device:TPU:0, one launch (start us, length us, event | category | flops | bytes accessed | tf_op | source)
XLA Modules:
  0.0 20.2 jit_solution(5333655351745011127)
XLA Ops:
  0.0 0.0 copy-start
  0.0 0.0 copy-start.1
  0.0 1.0 %copy-done.1 = bf16[144,768]{1,0:T(8,128)(2,1)S(1)} copy-done((bf16[144,768]{1,0:T(8,128)(2,1)S(1)}, bf16[144,768]{1,0:T(8,128)(2,1)}, u32[]{:S(2)}) %copy-start.1) | copy-done | bytes 221208
  1.0 0.0 copy-start.2
  1.0 0.9 %copy-done.2 = bf16[384,256]{1,0:T(8,128)(2,1)S(1)} copy-done((bf16[384,256]{1,0:T(8,128)(2,1)S(1)}, bf16[384,256]{1,0:T(8,128)(2,1)}, u32[]{:S(2)}) %copy-start.2) | copy-done | bytes 196632
  1.9 0.0 copy-start.10
  1.9 0.8 %copy-done.10 = f32[128,128]{1,0:T(8,128)S(1)} copy-done((f32[128,128]{1,0:T(8,128)S(1)}, f32[128,128]{1,0:T(8,128)}, u32[]{:S(2)}) %copy-start.10) | copy-done | bytes 65560
  2.8 0.6 %shard_map.164 = (f32[48,128]{1,0:T(8,128)S(1)}, f32[48,128]{1,0:T(8,128)S(1)}) custom-call(f32[128,128]{1,0:T(8,128)S(1)} %copy-done.10, bf16[384,256]{1,0:T(8,128)(2,1)S(1)} %copy-done.2, bf16[144,768]{1,0:T(8,128)(2,1)S(1)} %copy-done.1), custom_call_target="tpu_custom_call" | custom-call | flops 1000000 | bytes 1000000 | tf_op jit(solution)/shard_map/pallas_call | solution.py:346
  3.4 3.0 %collective-permute-start = (f32[48,128]{1,0:T(8,128)S(1)}, f32[48,128]{1,0:T(8,128)S(1)}, u32[]{:S(2)}, u32[]{:S(2)}) collective-permute-start(f32[48,128]{1,0:T(8,128)S(1)} %get-tuple-element.11), channel_id=1, source_target_pairs={{0,8},{1,3},{2,10},{3,1},{4,12},{5,7},{6,14},{7,5},{8,0},{9,17},{1... | collective-permute-start | bytes 73736 | tf_op jit(solution)/shard_map/ppermute | solution.py:391
  6.4 1.8 %collective-permute-done.near_ref = f32[48,128]{1,0:T(8,128)S(1)} collective-permute-done((f32[48,128]{1,0:T(8,128)S(1)}, f32[48,128]{1,0:T(8,128)S(1)}, u32[]{:S(2)}, u32[]{:S(2)}) %collective-permute-start) | collective-permute-done | bytes 24608 | tf_op jit(solution)/shard_map/ppermute | solution.py:391
  8.2 0.0 collective-permute-start.1
  8.2 1.2 %collective-permute-done.1.far_ref = f32[48,128]{1,0:T(8,128)S(1)} collective-permute-done((f32[48,128]{1,0:T(8,128)S(1)}, f32[48,128]{1,0:T(8,128)S(1)}, u32[]{:S(2)}, u32[]{:S(2)}) %collective-permute-start.1) | collective-permute-done | bytes 24608 | tf_op jit(solution)/shard_map/ppermute | solution.py:392
  9.4 0.0 copy-start.15
  9.4 0.0 copy-start.16
  9.4 2.3 %collective-permute-start.2 = (f32[24,128]{1,0:T(8,128)S(1)}, f32[24,128]{1,0:T(8,128)S(1)}, u32[]{:S(2)}, u32[]{:S(2)}) collective-permute-start(f32[24,128]{1,0:T(8,128)S(1)} %slice_add_fusion), channel_id=1, source_target_pairs={{0,2},{1,9},{2,0},{3,5},{4,6},{5,3},{6,4},{7,15},{8,10},{9,1},{10,... | collective-permute-start | bytes 36872 | tf_op jit(solution)/shard_map/ppermute | solution.py:394
  11.7 0.0 copy-done
  11.7 0.0 copy-done.15
  11.7 0.0 copy-done.16
  11.7 0.7 %shard_map.163 = (f32[2,12,2,576]{3,2,1,0:T(2,128)S(1)}, f32[2,8,128]{2,1,0:T(8,128)S(1)}) custom-call(s32[2]{0:T(128)S(1)} %copy-done.15, f32[8]{0:T(128)S(1)} %copy-done.16, f32[8,12,2,576]{3,2,1,0:T(2,128)S(1)} %bitcast.1), custom_call_target="tpu_custom_call" | custom-call | flops 1000000 | bytes 1000000 | tf_op jit(solution)/shard_map/pallas_call | solution.py:346
  12.4 0.9 %collective-permute-done.2.side_ref = f32[24,128]{1,0:T(8,128)S(1)} collective-permute-done((f32[24,128]{1,0:T(8,128)S(1)}, f32[24,128]{1,0:T(8,128)S(1)}, u32[]{:S(2)}, u32[]{:S(2)}) %collective-permute-start.2) | collective-permute-done | bytes 12320 | tf_op jit(solution)/shard_map/ppermute | solution.py:394
  13.3 0.0 collective-permute-start.3
  13.3 0.3 %slice_reduce_fusion = (f32[2,12,576]{2,1,0:T(8,128)S(1)}, f32[2,12,576]{2,1,0:T(8,128)S(1)}) fusion(f32[2,12,2,576]{3,2,1,0:T(2,128)S(1)} %get-tuple-element.12), kind=kLoop, calls=%fused_computation | loop fusion | bytes 221184 | tf_op jit(solution)/shard_map/slice | solution.py:406
  13.7 0.1 reshape_squeeze.7
  13.8 0.1 reshape_squeeze.6
  14.0 0.5 %concatenate.6.ker_a_ref = f32[576,128]{1,0:T(8,128)S(1)} concatenate(f32[576,24]{1,0:T(8,128)S(1)} %reshape_squeeze.6, f32[576,24]{1,0:T(8,128)S(1)} %reshape_squeeze.7, f32[576,16]{1,0:T(8,128)S(1)} %broadcast_in_dim.3, f32[576,24]{1,0:T(8,128)S(1)} %reshape_squeeze.6, f32[576,24]{1,0:T(8,128)S(1)} %reshape_squeeze.7, f32[576,16]{1,0:T(8,128)S(1)} %broadcast_in_dim.3), dimensions={1} | concatenate | bytes 589824 | tf_op jit(solution)/shard_map/concatenate | solution.py:408
  14.5 0.0 copy-start.3
  14.5 0.0 copy-start.5
  14.5 0.0 copy-start.6
  14.6 0.0 copy-start.7
  14.6 0.0 copy-start.8
  14.6 0.0 copy-start.11
  14.6 0.0 copy-start.12
  14.6 0.0 copy-start.13
  14.6 0.0 copy-start.14
  14.6 0.5 %concatenate.7.ker_b_ref = f32[576,128]{1,0:T(8,128)S(1)} concatenate(f32[576,24]{1,0:T(8,128)S(1)} %neg.3, f32[576,24]{1,0:T(8,128)S(1)} %reshape_squeeze.6, f32[576,16]{1,0:T(8,128)S(1)} %broadcast_in_dim.3, f32[576,24]{1,0:T(8,128)S(1)} %neg.3, f32[576,24]{1,0:T(8,128)S(1)} %reshape_squeeze.6, f32[576,16]{1,0:T(8,128)S(1)} %broadcast_in_dim.3), dimensions={1} | concatenate | bytes 589824 | tf_op jit(solution)/shard_map/concatenate | solution.py:409
  15.1 0.0 collective-permute-done.3.other_ref
  15.1 0.3 %copy-done.3 = bf16[256,256]{1,0:T(8,128)(2,1)S(1)} copy-done((bf16[256,256]{1,0:T(8,128)(2,1)S(1)}, bf16[256,256]{1,0:T(8,128)(2,1)}, u32[]{:S(2)}) %copy-start.3) | copy-done | bytes 131096
  15.4 0.1 copy-done.5
  15.5 0.0 copy-done.6
  15.5 0.0 copy-done.7
  15.5 0.0 copy-done.8
  15.6 0.0 copy-done.11
  15.6 0.0 copy-done.12
  15.6 0.0 copy-done.13
  15.6 0.0 copy-done.14
  15.6 0.0 copy-start.4
  15.6 0.0 copy-start.9
  15.6 2.3 %shard_map.165.mine_ref = f32[24,128]{1,0:T(8,128)S(1)} custom-call(f32[2,8,128]{2,1,0:T(8,128)S(1)} %get-tuple-element.9.strength_ref, f32[48,128]{1,0:T(8,128)S(1)} %get-tuple-element.10.own_ref, f32[48,128]{1,0:T(8,128)S(1)} %collective-permute-done.near_ref, f32[48,128]{1,0:T(8,128)S(1)} %collective-permute-done.1.far_ref, ...), custom_call_target="tpu_custom_call" | custom-call | flops 1000000 | bytes 1000000 | tf_op jit(solution)/shard_map/pallas_call | solution.py:346
  17.9 0.6 %collective-permute-start.4 = (f32[24,128]{1,0:T(8,128)S(1)}, f32[24,128]{1,0:T(8,128)S(1)}, u32[]{:S(2)}, u32[]{:S(2)}) collective-permute-start(f32[24,128]{1,0:T(8,128)S(1)} %shard_map.165.mine_ref), channel_id=1, source_target_pairs={{0,1},{1,0},{2,3},{3,2},{4,5},{5,4},{6,7},{7,6},{8,9},{9,8},{10,11... | collective-permute-start | bytes 36872 | tf_op jit(solution)/shard_map/ppermute | solution.py:423
  18.4 0.8 %collective-permute-done.4.theirs_ref = f32[24,128]{1,0:T(8,128)S(1)} collective-permute-done((f32[24,128]{1,0:T(8,128)S(1)}, f32[24,128]{1,0:T(8,128)S(1)}, u32[]{:S(2)}, u32[]{:S(2)}) %collective-permute-start.4) | collective-permute-done | bytes 12320 | tf_op jit(solution)/shard_map/ppermute | solution.py:423
  19.3 0.0 copy-done.4
  19.3 0.0 copy-done.9
  19.3 1.0 %shard_map.166 = f32[128,128]{1,0:T(8,128)} custom-call(f32[24,128]{1,0:T(8,128)S(1)} %shard_map.165.mine_ref, f32[24,128]{1,0:T(8,128)S(1)} %collective-permute-done.4.theirs_ref, bf16[256,256]{1,0:T(8,128)(2,1)S(1)} %copy-done.4, bf16[128,144]{1,0:T(8,128)(2,1)S(1)} %copy-done.9), custom_call_target="tpu_custom_call" | custom-call | flops 1000000 | bytes 1000000 | tf_op jit(solution)/shard_map/pallas_call | solution.py:346
  (3 shorter events, 0.0 us)
Async XLA Ops:
  0.0 11.7 %copy-start = (f32[8,2,12,576]{3,1,2,0:T(2,128)S(1)}, f32[8,2,12,576]{3,1,2,0:T(2,128)}, u32[]{:S(2)}) copy-start(f32[8,2,12,576]{3,1,2,0:T(2,128)} %param.20) | copy-start | bytes 1327108
  0.0 1.0 %copy-start.1 = (bf16[144,768]{1,0:T(8,128)(2,1)S(1)}, bf16[144,768]{1,0:T(8,128)(2,1)}, u32[]{:S(2)}) copy-start(bf16[144,768]{1,0:T(8,128)(2,1)} %constant.27.clone.row_ref) | copy-start | bytes 663556
  1.0 0.9 %copy-start.2 = (bf16[384,256]{1,0:T(8,128)(2,1)S(1)}, bf16[384,256]{1,0:T(8,128)(2,1)}, u32[]{:S(2)}) copy-start(bf16[384,256]{1,0:T(8,128)(2,1)} %constant.26.clone.col_ref) | copy-start | bytes 589828
  1.9 0.8 %copy-start.10 = (f32[128,128]{1,0:T(8,128)S(1)}, f32[128,128]{1,0:T(8,128)}, u32[]{:S(2)}) copy-start(f32[128,128]{1,0:T(8,128)} %mask_ref.1) | copy-start | bytes 196612
  3.4 4.8 %collective-permute-start = (f32[48,128]{1,0:T(8,128)S(1)}, f32[48,128]{1,0:T(8,128)S(1)}, u32[]{:S(2)}, u32[]{:S(2)}) collective-permute-start(f32[48,128]{1,0:T(8,128)S(1)} %get-tuple-element.11), channel_id=1, source_target_pairs={{0,8},{1,3},{2,10},{3,1},{4,12},{5,7},{6,14},{7,5},{8,0},{9,17},{1... | collective-permute-start | bytes 73736 | tf_op jit(solution)/shard_map/ppermute | solution.py:391
  8.2 1.2 %collective-permute-start.1 = (f32[48,128]{1,0:T(8,128)S(1)}, f32[48,128]{1,0:T(8,128)S(1)}, u32[]{:S(2)}, u32[]{:S(2)}) collective-permute-start(f32[48,128]{1,0:T(8,128)S(1)} %collective-permute-done.near_ref), channel_id=1, source_target_pairs={{0,1},{1,0},{2,3},{3,2},{4,5},{5,4},{6,7},{7,6},{8,9},{9,8},{10,11... | collective-permute-start | bytes 73736 | tf_op jit(solution)/shard_map/ppermute | solution.py:392
  9.4 2.3 %copy-start.15 = (s32[2]{0:T(128)S(1)}, s32[2]{0:T(128)}, u32[]{:S(2)}) copy-start(s32[2]{0:T(128)} %cond_ref.1) | copy-start | bytes 28
  9.4 2.3 %copy-start.16 = (f32[8]{0:T(128)S(1)}, f32[8]{0:T(128)}, u32[]{:S(2)}) copy-start(f32[8]{0:T(128)} %dose_ref.1) | copy-start | bytes 100
  9.4 3.9 %collective-permute-start.2 = (f32[24,128]{1,0:T(8,128)S(1)}, f32[24,128]{1,0:T(8,128)S(1)}, u32[]{:S(2)}, u32[]{:S(2)}) collective-permute-start(f32[24,128]{1,0:T(8,128)S(1)} %slice_add_fusion), channel_id=1, source_target_pairs={{0,2},{1,9},{2,0},{3,5},{4,6},{5,3},{6,4},{7,15},{8,10},{9,1},{10,... | collective-permute-start | bytes 36872 | tf_op jit(solution)/shard_map/ppermute | solution.py:394
  13.3 1.8 %collective-permute-start.3 = (f32[24,128]{1,0:T(8,128)S(1)}, f32[24,128]{1,0:T(8,128)S(1)}, u32[]{:S(2)}, u32[]{:S(2)}) collective-permute-start(f32[24,128]{1,0:T(8,128)S(1)} %collective-permute-done.2.side_ref), channel_id=1, source_target_pairs={{0,1},{1,0},{2,3},{3,2},{4,5},{5,4},{6,7},{7,6},{8,9},{9,8},{10,11... | collective-permute-start | bytes 36872 | tf_op jit(solution)/shard_map/ppermute | solution.py:395
  14.5 0.9 %copy-start.3 = (bf16[256,256]{1,0:T(8,128)(2,1)S(1)}, bf16[256,256]{1,0:T(8,128)(2,1)}, u32[]{:S(2)}) copy-start(bf16[256,256]{1,0:T(8,128)(2,1)} %constant.35.clone.from_cols_ref) | copy-start | bytes 393220
  14.5 1.0 %copy-start.5 = (bf16[128,288]{1,0:T(8,128)(2,1)S(1)}, bf16[128,288]{1,0:T(8,128)(2,1)}, u32[]{:S(2)}) copy-start(bf16[128,288]{1,0:T(8,128)(2,1)} %constant.31.clone.spread_ref) | copy-start | bytes 221188
  14.5 1.0 %copy-start.6 = (bf16[192,256]{1,0:T(8,128)(2,1)S(1)}, bf16[192,256]{1,0:T(8,128)(2,1)}, u32[]{:S(2)}) copy-start(bf16[192,256]{1,0:T(8,128)(2,1)} %constant.28.clone.to_cols_ref) | copy-start | bytes 294916
  14.6 1.0 %copy-start.7 = (s32[128,128]{1,0:T(8,128)S(1)}, s32[128,128]{1,0:T(8,128)}, u32[]{:S(2)}) copy-start(s32[128,128]{1,0:T(8,128)} %target_ref.1) | copy-start | bytes 196612
  14.6 1.0 %copy-start.8 = (bf16[256,128]{1,0:T(8,128)(2,1)S(1)}, bf16[256,128]{1,0:T(8,128)(2,1)}, u32[]{:S(2)}) copy-start(bf16[256,128]{1,0:T(8,128)(2,1)} %constant.33.clone.gather_cols_ref) | copy-start | bytes 196612
  14.6 1.0 %copy-start.11 = (bf16[192,128]{1,0:T(8,128)(2,1)S(1)}, bf16[192,128]{1,0:T(8,128)(2,1)}, u32[]{:S(2)}) copy-start(bf16[192,128]{1,0:T(8,128)(2,1)} %constant.30.clone.spread_cols_ref) | copy-start | bytes 147460
  14.6 1.0 %copy-start.12 = (bf16[48,384]{1,0:T(8,128)(2,1)S(1)}, bf16[48,384]{1,0:T(8,128)(2,1)}, u32[]{:S(2)}) copy-start(bf16[48,384]{1,0:T(8,128)(2,1)} %constant.32.clone.gather_rows_ref) | copy-start | bytes 110596
  14.6 1.0 %copy-start.13 = (bf16[48,288]{1,0:T(8,128)(2,1)S(1)}, bf16[48,288]{1,0:T(8,128)(2,1)}, u32[]{:S(2)}) copy-start(bf16[48,288]{1,0:T(8,128)(2,1)} %constant.29.clone.to_rows_ref) | copy-start | bytes 82948
  14.6 0.9 %copy-start.14 = (bf16[48,144]{1,0:T(8,128)(2,1)S(1)}, bf16[48,144]{1,0:T(8,128)(2,1)}, u32[]{:S(2)}) copy-start(bf16[48,144]{1,0:T(8,128)(2,1)} %constant.34.clone.from_rows_ref) | copy-start | bytes 41476
  15.6 3.7 %copy-start.4 = (bf16[256,256]{1,0:T(8,128)(2,1)S(1)}, bf16[256,256]{1,0:T(8,128)(2,1)}, u32[]{:S(2)}) copy-start(bf16[256,256]{1,0:T(8,128)(2,1)} %constant.36.clone.cols_ref) | copy-start | bytes 393220
  15.6 3.7 %copy-start.9 = (bf16[128,144]{1,0:T(8,128)(2,1)S(1)}, bf16[128,144]{1,0:T(8,128)(2,1)}, u32[]{:S(2)}) copy-start(bf16[128,144]{1,0:T(8,128)(2,1)} %constant.37.clone.rows_ref) | copy-start | bytes 110596
  17.9 1.4 %collective-permute-start.4 = (f32[24,128]{1,0:T(8,128)S(1)}, f32[24,128]{1,0:T(8,128)S(1)}, u32[]{:S(2)}, u32[]{:S(2)}) collective-permute-start(f32[24,128]{1,0:T(8,128)S(1)} %shard_map.165.mine_ref), channel_id=1, source_target_pairs={{0,1},{1,0},{2,3},{3,2},{4,5},{5,4},{6,7},{7,6},{8,9},{9,8},{10,11... | collective-permute-start | bytes 36872 | tf_op jit(solution)/shard_map/ppermute | solution.py:423

commit v3 on v2

--- a/solution.py
+++ b/solution.py
@@ -91,7 +91,13 @@
     cos, sin = np.cos(phase), np.sin(phase)
     real_rows = lanes((0, cos), (HALF, sin), (2 * HALF, -sin), (3 * HALF, cos))
     imag_rows = lanes((0, -sin), (HALF, cos), (2 * HALF, -cos), (3 * HALF, -sin))
-    to_cols = rows_at(HALF, (0, real_rows), (BAND, imag_rows))
+    to_cols = rows_at(
+        2 * HALF,
+        (0, real_rows),
+        (BAND, imag_rows),
+        (HALF, imag_rows),
+        (HALF + BAND, -real_rows),
+    )
     to_rows = np.concatenate([cos.T, sin.T], 1)
     where = (np.arange(tile)[:, None] + MARGIN) / window - points[None, :] / count
     spread = np.ones((tile, count))
@@ -105,8 +111,7 @@
     c, s = cos.T, sin.T
 
     def both(real_part, imag_part):
-        block = np.concatenate([real_part, imag_part], 1)
-        return lanes((0, block), (HALF, block))
+        return lanes((0, real_part), (BAND, imag_part), (HALF, imag_part), (HALF + BAND, -real_part))
 
     blocks = [both(c, -s), both(s, c), both(-s, -c), both(c, -s)]
     empty = np.zeros((HALF - count, 2 * HALF))
@@ -186,8 +191,22 @@
     return jnp.concatenate([high, low, high], 0)
 
 
-def local_kernel(mesh_shape, mask_ref, col_ref, row_ref, own_ref, send_ref):
+def fetch(sources, targets, sems):
+    copies = [
+        pltpu.make_async_copy(source, target, sems.at[at])
+        for at, (source, target) in enumerate(zip(sources, targets))
+    ]
+    for copy in copies:
+        copy.start()
+    return copies
+
+
+def local_kernel(
+    mesh_shape, mask_hbm, col_hbm, row_hbm, own_ref, send_ref, mask_ref, col_ref, row_ref, sems
+):
     tile = mask_ref.shape[0]
+    for copy in fetch((mask_hbm, col_hbm, row_hbm), (mask_ref, col_ref, row_ref), sems):
+        copy.wait()
     high, mid, low = split(mask_ref[...], 3)
     left = jnp.concatenate([high, mid, low, high, mid, high], 1)
     ch, cm, cl = col_ref[:tile], col_ref[tile : 2 * tile], col_ref[2 * tile :]
@@ -215,14 +234,17 @@
     send_ref[BAND:] = chosen[:, 2 * HALF :]
 
 
-def select_kernel(cond_ref, dose_ref, kernels_ref, out_ref, strength_ref, sems):
+def fetch_kernel(cond_ref, dose_ref, kernels_hbm, *refs):
+    sems = refs[-1]
+    count = (len(refs) - 3) // 2
+    chosen_ref, strength_ref = refs[count : count + 2]
     conds = cond_ref.shape[0]
-    copies = [
-        pltpu.make_async_copy(kernels_ref.at[cond_ref[c]], out_ref.at[c], sems.at[c])
-        for c in range(conds)
-    ]
-    for copy in copies:
-        copy.start()
+    chosen = [kernels_hbm.at[cond_ref[c]] for c in range(conds)]
+    copies = fetch(
+        chosen + list(refs[:count]),
+        [chosen_ref.at[c] for c in range(conds)] + list(refs[count + 2 : -1]),
+        sems,
+    )
     for c in range(conds):
         strength_ref[c] = jnp.full(strength_ref.shape[1:], dose_ref[cond_ref[c]], F32)
     for copy in copies:
@@ -230,13 +252,13 @@
 
 
 def field_kernel(
-    mesh_shape, strength_ref, own_ref, near_ref, far_ref, side_ref, other_ref, ker_a_ref,
-    ker_b_ref, target_ref, to_cols_ref, to_rows_ref, spread_cols_ref, spread_ref,
+    mesh_shape, strength_ref, own_ref, near_ref, far_ref, side_ref, other_ref,
+    kernels_ref, target_ref, to_cols_ref, to_rows_ref, spread_cols_ref, spread_ref,
     gather_rows_ref, gather_cols_ref, from_rows_ref, from_cols_ref, out_ref, cols_ref, field_ref,
 ):
     conds = strength_ref.shape[0]
     count = 2 * BAND
-    total = ker_a_ref.shape[0] // BAND
+    total = kernels_ref.shape[0] // BAND
     per = total // conds
     tile = target_ref.shape[0]
 
@@ -252,15 +274,23 @@
     spectrum = own_ref[BAND:] + near_ref[BAND:] + far_ref[BAND:]
     spectrum += half(side_ref[...], core) + half(other_ref[...], 1 - core)
     lane = lane_ids(spectrum.shape) % HALF
-    real = jnp.where(lane < BAND, spectrum, 0.0)
-    imag = jnp.where(lane >= BAND, spectrum, 0.0)
-    real = real + pltpu.roll(real, BAND, 1)
-    imag = imag + pltpu.roll(imag, 2 * HALF - BAND, 1)
-
-    ker_a = ker_a_ref[...].reshape(total, BAND, 2 * HALF)
-    ker_b = ker_b_ref[...].reshape(total, BAND, 2 * HALF)
-    product = (ker_a * real[None] + ker_b * imag[None]).reshape(total * BAND, 2 * HALF)
-    cols_ref[...] = dot(doubled(product), doubled_weights(to_cols_ref))
+    onto_next = jnp.where(lane < BAND, spectrum, 0.0)
+    onto_last = jnp.where(lane >= BAND, spectrum, 0.0)
+    spectrum = jnp.where(
+        lane_ids(spectrum.shape) < HALF,
+        onto_next + pltpu.roll(onto_next, BAND, 1),
+        onto_last + pltpu.roll(onto_last, 2 * HALF - BAND, 1),
+    )
+
+    kernels = kernels_ref[...].reshape(total, BAND, 2 * HALF)
+    product = (kernels * spectrum[None]).reshape(total * BAND, 2 * HALF)
+    high, mid, low = split(product, 3)
+    size = 2 * HALF
+    wh, wm, wl = to_cols_ref[:size], to_cols_ref[size : 2 * size], to_cols_ref[2 * size :]
+    cols_ref[...] = dot(
+        jnp.concatenate([high, mid, low, high, mid, high], 1),
+        jnp.concatenate([wh, wh, wh, wm, wm, wl], 0),
+    )
 
     sums = [jnp.zeros((count, 2 * HALF), F32) for _ in range(conds)]
     to_rows = to_rows_ref[...]
@@ -321,9 +351,7 @@
     first = dot(high, weights)
     back = first[:, : 2 * HALF] + first[:, 2 * HALF :] + dot(low, weights[:, : 2 * HALF])
     back = back.reshape(total, BAND, 2 * HALF)
-    sum_a = jnp.sum(ker_a_ref[...].reshape(total, BAND, 2 * HALF) * back, axis=0)
-    sum_b = jnp.sum(ker_b_ref[...].reshape(total, BAND, 2 * HALF) * back, axis=0)
-    out_ref[...] = jnp.where(lane_ids(sum_a.shape) < HALF, sum_a, sum_b)
+    out_ref[...] = jnp.sum(kernels_ref[...].reshape(total, BAND, 2 * HALF) * back, axis=0)
 
 
 def adjoint_kernel(mine_ref, theirs_ref, cols_ref, rows_ref, out_ref):
@@ -338,11 +366,18 @@
 
 VMEM = pl.BlockSpec(memory_space=pltpu.VMEM)
 SMEM = pl.BlockSpec(memory_space=pltpu.SMEM)
+HBM = pl.BlockSpec(memory_space=pltpu.HBM)
 
 
 def call(body, outs, specs, args, scratch=(), flops=1000000, grant=8):
-    shapes = [jax.ShapeDtypeStruct(shape, F32) for shape in outs]
+    shapes = [
+        shape if hasattr(shape, "dtype") else jax.ShapeDtypeStruct(shape, F32) for shape in outs
+    ]
     one = len(outs) == 1
+    args = [
+        pltpu.with_memory_space_constraint(value, pltpu.HBM) if spec is HBM else value
+        for spec, value in zip(specs, args)
+    ]
     return pl.pallas_call(
         body,
         out_shape=shapes[0] if one else shapes,
@@ -384,37 +419,46 @@
     col_table, row_table = local_tables(tile, window)
     block = (2 * BAND, 2 * HALF)
     own, send = call(
-        functools.partial(local_kernel, mesh_shape), [block] * 2, [VMEM] * 3,
+        functools.partial(local_kernel, mesh_shape), [block] * 2, [HBM] * 3,
         (mask, col_table, row_table),
+        scratch=[
+            pltpu.VMEM(mask.shape, F32),
+            pltpu.VMEM(col_table.shape, BF),
+            pltpu.VMEM(row_table.shape, BF),
+            pltpu.SemaphoreType.DMA((3,)),
+        ],
     )
     swap = [(0, 1), (1, 0)]
     near = lax.ppermute(send, AXES, swaps(mesh_shape, 0))
+
+    conds = cond_index.shape[0]
+    count = kernels.shape[2]
+    later = (target,) + field_tables(tile, window) + adjoint_tables(tile, window)
+    chosen, strength, *later = call(
+        fetch_kernel,
+        [(conds, count, 2, BAND * BAND), (conds, 8, tile)]
+        + [jax.ShapeDtypeStruct(value.shape, value.dtype) for value in later],
+        [SMEM] * 2 + [HBM] * (1 + len(later)),
+        (cond_index, dose, jnp.transpose(kernels, (0, 2, 1, 3))) + later,
+        scratch=[pltpu.SemaphoreType.DMA((conds + len(later),))],
+    )
+    near, chosen, strength, later = lax.optimization_barrier((near, chosen, strength, later))
     far = lax.ppermute(near, "cond", swap)
+    real = chosen[:, :, 0].reshape(conds * count * BAND, BAND)
+    imag = chosen[:, :, 1].reshape(conds * count * BAND, BAND)
+    gap = jnp.zeros((real.shape[0], HALF - 2 * BAND), F32)
+    arranged = jnp.concatenate([real, imag, gap] * 2, 1)
+    far, arranged = lax.optimization_barrier((far, arranged))
     message = own[:BAND] + near[:BAND] + far[:BAND]
     side = lax.ppermute(message, AXES, swaps(mesh_shape, 1))
     other = lax.ppermute(side, "cond", swap)
-
-    conds = cond_index.shape[0]
-    count = kernels.shape[2]
-    chosen, strength = call(
-        select_kernel, [(conds, count, 2, BAND * BAND), (conds, 8, tile)],
-        [SMEM, SMEM, pl.BlockSpec(memory_space=pl.ANY)],
-        (cond_index, dose, jnp.transpose(kernels, (0, 2, 1, 3))),
-        scratch=[pltpu.SemaphoreType.DMA((conds,))],
-    )
-    real = chosen[:, :, 0].reshape(conds * count * BAND, BAND)
-    imag = chosen[:, :, 1].reshape(conds * count * BAND, BAND)
-    gap = jnp.zeros((real.shape[0], HALF - 2 * BAND), F32)
-    ker_a = jnp.concatenate([real, imag, gap] * 2, 1)
-    ker_b = jnp.concatenate([-imag, real, gap] * 2, 1)
 
     total = conds * count
     cotangent = call(
         functools.partial(field_kernel, mesh_shape),
         [(BAND, 2 * HALF)],
-        [VMEM] * 17,
-        (strength, own, near, far, side, other, ker_a, ker_b, target)
-        + field_tables(tile, window),
+        [VMEM] * 16,
+        (strength, own, near, far, side, other, arranged, *later[:-2]),
         scratch=[
             pltpu.VMEM((total * BAND, 4 * HALF), F32),
             pltpu.VMEM((total // 2, 2 * BAND, 4 * HALF), F32),
@@ -422,7 +466,7 @@
     )
     theirs = lax.ppermute(cotangent, "cond", swap)
     return call(
-        adjoint_kernel, [(tile, tile)], [VMEM] * 4, (cotangent, theirs) + adjoint_tables(tile, window)
+        adjoint_kernel, [(tile, tile)], [VMEM] * 4, (cotangent, theirs, *later[-2:])
     )
 
 

time: 20.5 us -> 17.8 us (0.87)
  local copies, waits for them, and re-layouts: 4.85 us -> 1.13 us
  Pallas kernels: 4.54 us -> 7.07 us
  waiting for transfers between devices: 4.76 us -> 3.96 us
  starting transfers between devices: 5.86 us -> 5.35 us
    unnamed x34 -> x4, local copies, waits for them, and re-layouts: 3.26 us -> 0.01 us
    pallas_call x4, Pallas kernels: 4.54 us -> 7.07 us  [call(): pl.pallas_call(body, out_shape=shapes[0] if one else shapes, in_specs=spe...]
    ppermute x1, waiting for transfers between devices: 1.81 us -> 0.01 us  [shards(): near = lax.ppermute(send, AXES, swaps(mesh_shape, 0))]
    ppermute x1, waiting for transfers between devices: 0.01 us -> 1.18 us  [shards(): other = lax.ppermute(side, 'cond', swap)]
    ppermute x1, waiting for transfers between devices: 1.19 us -> 0.03 us  [shards(): far = lax.ppermute(near, 'cond', swap)]
    ppermute x1, waiting for transfers between devices: 0.93 us -> 1.74 us  [shards(): side = lax.ppermute(message, AXES, swaps(mesh_shape, 1))]
    concatenate x2 -> x1, local copies, waits for them, and re-layouts: 0.96 us -> 0.48 us  [shards(): arranged = jnp.concatenate([real, imag, gap] * 2, 1)]
    ppermute x1, starting transfers between devices: 0.57 us -> 0.23 us  [shards(): theirs = lax.ppermute(cotangent, 'cond', swap)]
  transfers between devices with their start and end apart: 5 -> 5, of which waited for: 4 -> 3; matrix products, arithmetic and copies ran while one was open for 8% -> 6% of each run, Pallas kernels for 4% -> 11%
where the time goes in v3:
time: 17.8 us; the launch traced here: 17.6 us
  Pallas kernels  7.07 us (40%)
  starting transfers between devices  5.35 us (30%)
  waiting for transfers between devices  3.96 us (22%)
  local copies, waits for them, and re-layouts  1.13 us (6%)
    pallas_call x4, Pallas kernels, call(): pl.pallas_call(body, out_shape=shapes[0] if one else shapes, in_specs=spe...  7.07 us
    ppermute x1, starting transfers between devices, shards(): near = lax.ppermute(send, AXES, swaps(mesh_shape, 0))  3.03 us
    ppermute x1, starting transfers between devices, shards(): side = lax.ppermute(message, AXES, swaps(mesh_shape, 1))  2.01 us
    ppermute x1, waiting for transfers between devices, shards(): side = lax.ppermute(message, AXES, swaps(mesh_shape, 1))  1.74 us
    ppermute x1, waiting for transfers between devices, shards(): other = lax.ppermute(side, 'cond', swap)  1.18 us
    ppermute x1, waiting for transfers between devices, shards(): theirs = lax.ppermute(cotangent, 'cond', swap)  1.01 us
    concatenate x1, local copies, waits for them, and re-layouts, shards(): arranged = jnp.concatenate([real, imag, gap] * 2, 1)  0.48 us
  transfers between devices with their start and end apart: 5, of which 3 were waited for; matrix products, arithmetic and copies ran while one was open for 6% of the time, Pallas kernels for 11%

profile of v3, /device:TPU:0, one launch (start us, length us, event | category | flops | bytes accessed | tf_op | source)
XLA Modules:
  0.0 17.6 jit_solution(8075409012327213972)
XLA Ops:
  0.0 1.7 %shard_map.163 = (f32[48,128]{1,0:T(8,128)S(1)}, f32[48,128]{1,0:T(8,128)S(1)}) custom-call(f32[128,128]{1,0:T(8,128)} %mask_hbm.1, bf16[384,256]{1,0:T(8,128)(2,1)} %constant.26.clone.col_hbm, bf16[144,768]{1,0:T(8,128)(2,1)} %constant.27.clone.row_hbm), custom_call_target="tpu_custom_call" | custom-call | flops 1000000 | bytes 1000000 | tf_op jit(solution)/shard_map/pallas_call | solution.py:381
  1.7 0.0 copy-start
  1.7 0.0 copy-start.1
  1.7 3.0 %collective-permute-start = (f32[48,128]{1,0:T(8,128)S(1)}, f32[48,128]{1,0:T(8,128)S(1)}, u32[]{:S(2)}, u32[]{:S(2)}) collective-permute-start(f32[48,128]{1,0:T(8,128)S(1)} %get-tuple-element.36), channel_id=1, source_target_pairs={{0,8},{1,3},{2,10},{3,1},{4,12},{5,7},{6,14},{7,5},{8,0},{9,17},{1... | collective-permute-start | bytes 73736 | tf_op jit(solution)/shard_map/ppermute | solution.py:432
  4.7 0.0 copy-done
  4.7 0.0 copy-done.1
  4.8 1.9 %shard_map.164 = (f32[2,12,2,576]{3,2,1,0:T(2,128)S(1)}, f32[2,8,128]{2,1,0:T(8,128)S(1)}, s32[128,128]{1,0:T(8,128)S(1)}, bf16[384,256]{1,0:T(8,128)(2,1)S(1)},...) custom-call(s32[2]{0:T(128)S(1)} %copy-done, ...), custom_call_target="tpu_custom_call" | custom-call | flops 1000000 | bytes 1000000 | tf_op jit(solution)/shard_map/pallas_call | solution.py:381
  6.7 0.0 collective-permute-done.near_ref
  6.7 0.1 collective-permute-start.1
  6.8 0.3 %slice_reduce_fusion = (f32[2,12,576]{2,1,0:T(8,128)S(1)}, f32[2,12,576]{2,1,0:T(8,128)S(1)}) fusion(f32[2,12,2,576]{3,2,1,0:T(2,128)S(1)} %get-tuple-element.53), kind=kLoop, calls=%fused_computation | loop fusion | bytes 221184 | tf_op jit(solution)/shard_map/slice | solution.py:448
  7.1 0.1 reshape_squeeze.6
  7.3 0.1 reshape_squeeze.7
  7.5 0.5 %concatenate.3.kernels_ref = f32[576,128]{1,0:T(8,128)S(1)} concatenate(f32[576,24]{1,0:T(8,128)S(1)} %reshape_squeeze.6, f32[576,24]{1,0:T(8,128)S(1)} %reshape_squeeze.7, f32[576,16]{1,0:T(8,128)S(1)} %broadcast_in_dim.3, f32[576,24]{1,0:T(8,128)S(1)} %reshape_squeeze.6, f32[576,24]{1,0:T(8,128)S(1)} %reshape_squeeze.7, f32[576,16]{1,0:T(8,128)S(1)} %broadcast_in_dim.3), dimensions={1} | concatenate | bytes 589824 | tf_op jit(solution)/shard_map/concatenate | solution.py:450
  7.9 0.0 collective-permute-done.1.far_ref
  8.0 2.0 %collective-permute-start.2 = (f32[24,128]{1,0:T(8,128)S(1)}, f32[24,128]{1,0:T(8,128)S(1)}, u32[]{:S(2)}, u32[]{:S(2)}) collective-permute-start(f32[24,128]{1,0:T(8,128)S(1)} %slice_add_fusion), channel_id=1, source_target_pairs={{0,2},{1,9},{2,0},{3,5},{4,6},{5,3},{6,4},{7,15},{8,10},{9,1},{10,... | collective-permute-start | bytes 36872 | tf_op jit(solution)/shard_map/ppermute | solution.py:453
  10.0 1.7 %collective-permute-done.2.side_ref = f32[24,128]{1,0:T(8,128)S(1)} collective-permute-done((f32[24,128]{1,0:T(8,128)S(1)}, f32[24,128]{1,0:T(8,128)S(1)}, u32[]{:S(2)}, u32[]{:S(2)}) %collective-permute-start.2) | collective-permute-done | bytes 12320 | tf_op jit(solution)/shard_map/ppermute | solution.py:453
  11.7 0.0 collective-permute-start.3
  11.7 1.2 %collective-permute-done.3.other_ref = f32[24,128]{1,0:T(8,128)S(1)} collective-permute-done((f32[24,128]{1,0:T(8,128)S(1)}, f32[24,128]{1,0:T(8,128)S(1)}, u32[]{:S(2)}, u32[]{:S(2)}) %collective-permute-start.3) | collective-permute-done | bytes 12320 | tf_op jit(solution)/shard_map/ppermute | solution.py:454
  12.9 2.5 %shard_map.165.mine_ref = f32[24,128]{1,0:T(8,128)S(1)} custom-call(f32[2,8,128]{2,1,0:T(8,128)S(1)} %get-tuple-element.50.strength_ref, f32[48,128]{1,0:T(8,128)S(1)} %get-tuple-element.51.own_ref, f32[48,128]{1,0:T(8,128)S(1)} %collective-permute-done.near_ref, f32[48,128]{1,0:T(8,128)S(1)} %collective-permute-done.1.far_ref, ...), custom_call_target="tpu_custom_call" | custom-call | flops 1000000 | bytes 1000000 | tf_op jit(solution)/shard_map/pallas_call | solution.py:381
  15.4 0.2 %collective-permute-start.4 = (f32[24,128]{1,0:T(8,128)S(1)}, f32[24,128]{1,0:T(8,128)S(1)}, u32[]{:S(2)}, u32[]{:S(2)}) collective-permute-start(f32[24,128]{1,0:T(8,128)S(1)} %shard_map.165.mine_ref), channel_id=1, source_target_pairs={{0,1},{1,0},{2,3},{3,2},{4,5},{5,4},{6,7},{7,6},{8,9},{9,8},{10,11... | collective-permute-start | bytes 36872 | tf_op jit(solution)/shard_map/ppermute | solution.py:467
  15.6 1.0 %collective-permute-done.4.theirs_ref = f32[24,128]{1,0:T(8,128)S(1)} collective-permute-done((f32[24,128]{1,0:T(8,128)S(1)}, f32[24,128]{1,0:T(8,128)S(1)}, u32[]{:S(2)}, u32[]{:S(2)}) %collective-permute-start.4) | collective-permute-done | bytes 12320 | tf_op jit(solution)/shard_map/ppermute | solution.py:467
  16.6 1.0 %shard_map.166 = f32[128,128]{1,0:T(8,128)} custom-call(f32[24,128]{1,0:T(8,128)S(1)} %shard_map.165.mine_ref, f32[24,128]{1,0:T(8,128)S(1)} %collective-permute-done.4.theirs_ref, bf16[256,256]{1,0:T(8,128)(2,1)S(1)} %get-tuple-element.65.cols_ref, bf16[128,144]{1,0:T(8,128)(2,1)S(1)} %get-tuple-element.66.rows_ref), custom_call_target="tpu_custom_call" | custom-call | flops 1000000 | bytes 1000000 | tf_op jit(solution)/shard_map/pallas_call | solution.py:381
  (2 shorter events, 0.0 us)
Async XLA Ops:
  1.7 3.1 %copy-start = (s32[2]{0:T(128)S(1)}, s32[2]{0:T(128)}, u32[]{:S(2)}) copy-start(s32[2]{0:T(128)} %cond_ref.1) | copy-start | bytes 28
  1.7 3.1 %copy-start.1 = (f32[8]{0:T(128)S(1)}, f32[8]{0:T(128)}, u32[]{:S(2)}) copy-start(f32[8]{0:T(128)} %dose_ref.1) | copy-start | bytes 100
  1.7 5.0 %collective-permute-start = (f32[48,128]{1,0:T(8,128)S(1)}, f32[48,128]{1,0:T(8,128)S(1)}, u32[]{:S(2)}, u32[]{:S(2)}) collective-permute-start(f32[48,128]{1,0:T(8,128)S(1)} %get-tuple-element.36), channel_id=1, source_target_pairs={{0,8},{1,3},{2,10},{3,1},{4,12},{5,7},{6,14},{7,5},{8,0},{9,17},{1... | collective-permute-start | bytes 73736 | tf_op jit(solution)/shard_map/ppermute | solution.py:432
  6.7 1.3 %collective-permute-start.1 = (f32[48,128]{1,0:T(8,128)S(1)}, f32[48,128]{1,0:T(8,128)S(1)}, u32[]{:S(2)}, u32[]{:S(2)}) collective-permute-start(f32[48,128]{1,0:T(8,128)S(1)} %collective-permute-done.near_ref), channel_id=1, source_target_pairs={{0,1},{1,0},{2,3},{3,2},{4,5},{5,4},{6,7},{7,6},{8,9},{9,8},{10,11... | collective-permute-start | bytes 73736 | tf_op jit(solution)/shard_map/ppermute | solution.py:446
  8.0 3.8 %collective-permute-start.2 = (f32[24,128]{1,0:T(8,128)S(1)}, f32[24,128]{1,0:T(8,128)S(1)}, u32[]{:S(2)}, u32[]{:S(2)}) collective-permute-start(f32[24,128]{1,0:T(8,128)S(1)} %slice_add_fusion), channel_id=1, source_target_pairs={{0,2},{1,9},{2,0},{3,5},{4,6},{5,3},{6,4},{7,15},{8,10},{9,1},{10,... | collective-permute-start | bytes 36872 | tf_op jit(solution)/shard_map/ppermute | solution.py:453
  11.7 1.2 %collective-permute-start.3 = (f32[24,128]{1,0:T(8,128)S(1)}, f32[24,128]{1,0:T(8,128)S(1)}, u32[]{:S(2)}, u32[]{:S(2)}) collective-permute-start(f32[24,128]{1,0:T(8,128)S(1)} %collective-permute-done.2.side_ref), channel_id=1, source_target_pairs={{0,1},{1,0},{2,3},{3,2},{4,5},{5,4},{6,7},{7,6},{8,9},{9,8},{10,11... | collective-permute-start | bytes 36872 | tf_op jit(solution)/shard_map/ppermute | solution.py:454
  15.4 1.2 %collective-permute-start.4 = (f32[24,128]{1,0:T(8,128)S(1)}, f32[24,128]{1,0:T(8,128)S(1)}, u32[]{:S(2)}, u32[]{:S(2)}) collective-permute-start(f32[24,128]{1,0:T(8,128)S(1)} %shard_map.165.mine_ref), channel_id=1, source_target_pairs={{0,1},{1,0},{2,3},{3,2},{4,5},{5,4},{6,7},{7,6},{8,9},{9,8},{10,11... | collective-permute-start | bytes 36872 | tf_op jit(solution)/shard_map/ppermute | solution.py:467

commit v4 on v3

--- a/solution.py
+++ b/solution.py
@@ -75,13 +75,11 @@
         phase = angles(places + shift, frequencies(), window)
         cols += [(at, np.cos(phase)), (at + BAND, -np.sin(phase))]
     col_table = lanes(*cols) / window
-    real, imag = [], []
+    row_table = []
     for shift in (MARGIN, 0, 2 * MARGIN):
         phase = angles(frequencies(), places + shift, window)
-        real.append(np.cos(phase))
-        imag.append(-np.sin(phase))
-    row_table = np.concatenate(real + imag, 0)
-    return stacked(col_table, 3), six(row_table)
+        row_table += [np.cos(phase), -np.sin(phase)]
+    return stacked(col_table, 2), three(np.concatenate(row_table, 0))
 
 
 def field_tables(tile, window):
@@ -201,54 +199,60 @@
     return copies
 
 
-def local_kernel(
-    mesh_shape, mask_hbm, col_hbm, row_hbm, own_ref, send_ref, mask_ref, col_ref, row_ref, sems
-):
-    tile = mask_ref.shape[0]
-    for copy in fetch((mask_hbm, col_hbm, row_hbm), (mask_ref, col_ref, row_ref), sems):
-        copy.wait()
-    high, mid, low = split(mask_ref[...], 3)
-    left = jnp.concatenate([high, mid, low, high, mid, high], 1)
-    ch, cm, cl = col_ref[:tile], col_ref[tile : 2 * tile], col_ref[2 * tile :]
-    right = jnp.concatenate([ch, ch, ch, cm, cm, cl], 0)
-    partial = dot(left, right)
-    both = dot(row_ref[...], six_right(partial))
-    top, bottom = both[: 3 * BAND], both[3 * BAND :]
+def local_spectrum(tile_value, col_ref, row_table):
+    size = col_ref.shape[0] // 2
+    high, low = split(tile_value, 2)
+    ch, cl = col_ref[:size], col_ref[size:]
+    partial = dot(jnp.concatenate([high, low, high], 1), jnp.concatenate([ch, ch, cl], 0))
+    both = dot(row_table, three_right(partial))
+    top, bottom = both[:BAND], both[BAND:]
     lane = lane_ids(top.shape) % HALF
-    width = top.shape[1]
     turned = jnp.where(
         lane < BAND,
-        -pltpu.roll(bottom, width - BAND, 1),
+        -pltpu.roll(bottom, top.shape[1] - BAND, 1),
         jnp.where(lane < 2 * BAND, pltpu.roll(bottom, BAND, 1), 0.0),
     )
     result = top + turned
-    own = result[:BAND]
-    below = result[BAND : 2 * BAND]
-    above = result[2 * BAND :]
-    down, valid = toward(lax.axis_index("row"), lax.axis_index("cond"), mesh_shape[0])
-    chosen = jnp.where(down, below, above)
-    chosen = jnp.where(valid, chosen, 0.0)
-    own_ref[:BAND] = own[:, : 2 * HALF]
-    own_ref[BAND:] = own[:, 2 * HALF :]
-    send_ref[:BAND] = chosen[:, : 2 * HALF]
-    send_ref[BAND:] = chosen[:, 2 * HALF :]
-
-
-def fetch_kernel(cond_ref, dose_ref, kernels_hbm, *refs):
-    sems = refs[-1]
-    count = (len(refs) - 3) // 2
-    chosen_ref, strength_ref = refs[count : count + 2]
-    conds = cond_ref.shape[0]
-    chosen = [kernels_hbm.at[cond_ref[c]] for c in range(conds)]
-    copies = fetch(
-        chosen + list(refs[:count]),
-        [chosen_ref.at[c] for c in range(conds)] + list(refs[count + 2 : -1]),
-        sems,
-    )
+    return jnp.concatenate([result[:, : 2 * HALF], result[:, 2 * HALF :]], 0)
+
+
+def open_kernel(*refs):
+    cond_hbm, dose_hbm, mask_hbm, kernels_hbm = refs[:4]
+    cond_ref, dose_ref, mask_ref, sems = refs[-4:]
+    count = (len(refs) - 11) // 2
+    sources, targets = refs[4 : 4 + count], refs[7 + count : 7 + 2 * count]
+    own_ref, chosen_ref, strength_ref = refs[4 + count : 7 + count]
+    conds = cond_hbm.shape[0]
+    copies = []
+
+    def start(source, target):
+        copy = pltpu.make_async_copy(source, target, sems.at[len(copies)])
+        copy.start()
+        copies.append(copy)
+        return copy
+
+    scalars = [start(cond_hbm, cond_ref), start(dose_hbm, dose_ref)]
+    first = [start(mask_hbm, mask_ref)]
+    first += [start(source, target) for source, target in zip(sources[:2], targets[:2])]
+    for copy in scalars:
+        copy.wait()
+    rest = [start(kernels_hbm.at[cond_ref[c]], chosen_ref.at[c]) for c in range(conds)]
+    rest += [start(source, target) for source, target in zip(sources[2:], targets[2:])]
     for c in range(conds):
         strength_ref[c] = jnp.full(strength_ref.shape[1:], dose_ref[cond_ref[c]], F32)
-    for copy in copies:
+    for copy in first:
         copy.wait()
+    col_ref, row_ref = targets[:2]
+    own_ref[...] = local_spectrum(mask_ref[...], col_ref, row_ref[: 2 * BAND])
+    for copy in rest:
+        copy.wait()
+
+
+def near_kernel(mesh_shape, tile_ref, col_ref, row_ref, out_ref):
+    down, valid = toward(lax.axis_index("row"), lax.axis_index("cond"), mesh_shape[0])
+    at = pl.multiple_of(jnp.where(down, 4 * BAND, 2 * BAND), 2 * BAND)
+    share = local_spectrum(tile_ref[...], col_ref, row_ref[pl.ds(at, 2 * BAND)])
+    out_ref[...] = jnp.where(valid, share, 0.0)
 
 
 def field_kernel(
@@ -416,33 +420,34 @@
 def shards(mesh_shape, mask, target, cond_index, kernels, dose):
     tile = mask.shape[0]
     window = tile + 2 * MARGIN
-    col_table, row_table = local_tables(tile, window)
-    block = (2 * BAND, 2 * HALF)
-    own, send = call(
-        functools.partial(local_kernel, mesh_shape), [block] * 2, [HBM] * 3,
-        (mask, col_table, row_table),
-        scratch=[
-            pltpu.VMEM(mask.shape, F32),
-            pltpu.VMEM(col_table.shape, BF),
-            pltpu.VMEM(row_table.shape, BF),
-            pltpu.SemaphoreType.DMA((3,)),
-        ],
-    )
     swap = [(0, 1), (1, 0)]
-    near = lax.ppermute(send, AXES, swaps(mesh_shape, 0))
-
     conds = cond_index.shape[0]
     count = kernels.shape[2]
-    later = (target,) + field_tables(tile, window) + adjoint_tables(tile, window)
-    chosen, strength, *later = call(
-        fetch_kernel,
-        [(conds, count, 2, BAND * BAND), (conds, 8, tile)]
-        + [jax.ShapeDtypeStruct(value.shape, value.dtype) for value in later],
-        [SMEM] * 2 + [HBM] * (1 + len(later)),
-        (cond_index, dose, jnp.transpose(kernels, (0, 2, 1, 3))) + later,
-        scratch=[pltpu.SemaphoreType.DMA((conds + len(later),))],
-    )
-    near, chosen, strength, later = lax.optimization_barrier((near, chosen, strength, later))
+    block = (2 * BAND, 2 * HALF)
+    beside = lax.ppermute(mask, AXES, swaps(mesh_shape, 0))
+    fetched = local_tables(tile, window) + (target,)
+    fetched += field_tables(tile, window) + adjoint_tables(tile, window)
+    own, chosen, strength, *fetched = call(
+        open_kernel,
+        [block, (conds, count, 2, BAND * BAND), (conds, 8, tile)]
+        + [jax.ShapeDtypeStruct(value.shape, value.dtype) for value in fetched],
+        [HBM] * (4 + len(fetched)),
+        (cond_index, dose, mask, jnp.transpose(kernels, (0, 2, 1, 3))) + fetched,
+        scratch=[
+            pltpu.SMEM(cond_index.shape, jnp.int32),
+            pltpu.SMEM(dose.shape, F32),
+            pltpu.VMEM(mask.shape, F32),
+            pltpu.SemaphoreType.DMA((3 + conds + len(fetched),)),
+        ],
+    )
+    beside, own, chosen, strength, fetched = lax.optimization_barrier(
+        (beside, own, chosen, strength, fetched)
+    )
+    col_table, row_table, *later = fetched
+    near = call(
+        functools.partial(near_kernel, mesh_shape), [block], [VMEM] * 3,
+        (beside, col_table, row_table),
+    )
     far = lax.ppermute(near, "cond", swap)
     real = chosen[:, :, 0].reshape(conds * count * BAND, BAND)
     imag = chosen[:, :, 1].reshape(conds * count * BAND, BAND)

time: 17.8 us -> 17.5 us (0.983)
  Pallas kernels: 7.07 us -> 5.97 us
  waiting for transfers between devices: 3.96 us -> 4.56 us
  starting transfers between devices: 5.35 us -> 5.62 us
    pallas_call x4, Pallas kernels: 7.07 us -> 5.97 us  [call(): pl.pallas_call(body, out_shape=shapes[0] if one else shapes, in_specs=spe...]
    ppermute x1, waiting for transfers between devices: 0.01 us -> 0.68 us  [shards(): beside = lax.ppermute(mask, AXES, swaps(mesh_shape, 0))]
    ppermute x1, starting transfers between devices: 2.01 us -> 2.34 us  [shards(): side = lax.ppermute(message, AXES, swaps(mesh_shape, 1))]
  transfers between devices with their start and end apart: 5 -> 5, of which waited for: 3 -> 4; matrix products, arithmetic and copies ran while one was open for 6% -> 6% of each run, Pallas kernels for 11% -> 12%
where the time goes in v4:
time: 17.5 us; the launch traced here: 17.3 us
  Pallas kernels  5.97 us (34%)
  starting transfers between devices  5.62 us (32%)
  waiting for transfers between devices  4.56 us (26%)
  local copies, waits for them, and re-layouts  1.12 us (6%)
    pallas_call x4, Pallas kernels, call(): pl.pallas_call(body, out_shape=shapes[0] if one else shapes, in_specs=spe...  5.97 us
    ppermute x1, starting transfers between devices, shards(): beside = lax.ppermute(mask, AXES, swaps(mesh_shape, 0))  2.97 us
    ppermute x1, starting transfers between devices, shards(): side = lax.ppermute(message, AXES, swaps(mesh_shape, 1))  2.34 us
    ppermute x1, waiting for transfers between devices, shards(): side = lax.ppermute(message, AXES, swaps(mesh_shape, 1))  1.67 us
    ppermute x1, waiting for transfers between devices, shards(): other = lax.ppermute(side, 'cond', swap)  1.18 us
    ppermute x1, waiting for transfers between devices, shards(): theirs = lax.ppermute(cotangent, 'cond', swap)  1 us
    ppermute x1, waiting for transfers between devices, shards(): beside = lax.ppermute(mask, AXES, swaps(mesh_shape, 0))  0.68 us
    concatenate x1, local copies, waits for them, and re-layouts, shards(): arranged = jnp.concatenate([real, imag, gap] * 2, 1)  0.48 us
  transfers between devices with their start and end apart: 5, of which 4 were waited for; matrix products, arithmetic and copies ran while one was open for 6% of the time, Pallas kernels for 12%

profile of v4, /device:TPU:0, one launch (start us, length us, event | category | flops | bytes accessed | tf_op | source)
XLA Modules:
  0.0 17.3 jit_solution(9308089655374576998)
XLA Ops:
  0.0 3.0 %collective-permute-start = (f32[128,128]{1,0:T(8,128)}, f32[128,128]{1,0:T(8,128)S(1)}, u32[]{:S(2)}, u32[]{:S(2)}) collective-permute-start(f32[128,128]{1,0:T(8,128)} %refs_2_.1), channel_id=1, source_target_pairs={{0,8},{1,3},{2,10},{3,1},{4,12},{5,7},{6,14},{7,5},{8,0},{9,17},{1... | collective-permute-start | bytes 196616 | tf_op jit(solution)/shard_map/ppermute | solution.py:427
  3.0 2.1 %shard_map.163 = (f32[48,128]{1,0:T(8,128)S(1)}, f32[2,12,2,576]{3,2,1,0:T(2,128)S(1)}, f32[2,8,128]{2,1,0:T(8,128)S(1)}, bf16[256,256]{1,0:T(8,128)(2,1)S(1)}, ...) custom-call(s32[2]{0:T(128)} %refs_0_.1, ...), custom_call_target="tpu_custom_call" | custom-call | flops 1000000 | bytes 1000000 | tf_op jit(solution)/shard_map/pallas_call | solution.py:385
  5.1 0.7 %collective-permute-done.tile_ref = f32[128,128]{1,0:T(8,128)S(1)} collective-permute-done((f32[128,128]{1,0:T(8,128)}, f32[128,128]{1,0:T(8,128)S(1)}, u32[]{:S(2)}, u32[]{:S(2)}) %collective-permute-start) | collective-permute-done | bytes 65568 | tf_op jit(solution)/shard_map/ppermute | solution.py:427
  5.8 0.4 %shard_map.164.near_ref = f32[48,128]{1,0:T(8,128)S(1)} custom-call(f32[128,128]{1,0:T(8,128)S(1)} %collective-permute-done.tile_ref, bf16[256,256]{1,0:T(8,128)(2,1)S(1)} %get-tuple-element.59.col_ref, bf16[144,384]{1,0:T(8,128)(2,1)S(1)} %get-tuple-element.60.row_ref), custom_call_target="tpu_custom_call" | custom-call | flops 1000000 | bytes 1000000 | tf_op jit(solution)/shard_map/pallas_call | solution.py:385
  6.2 0.1 collective-permute-start.1
  6.3 0.3 %slice_reduce_fusion = (f32[2,12,576]{2,1,0:T(8,128)S(1)}, f32[2,12,576]{2,1,0:T(8,128)S(1)}) fusion(f32[2,12,2,576]{3,2,1,0:T(2,128)S(1)} %get-tuple-element.61), kind=kLoop, calls=%fused_computation | loop fusion | bytes 221184 | tf_op jit(solution)/shard_map/slice | solution.py:453
  6.6 0.1 reshape_squeeze.7
  6.7 0.1 reshape_squeeze.6
  6.9 0.5 %concatenate.3.kernels_ref = f32[576,128]{1,0:T(8,128)S(1)} concatenate(f32[576,24]{1,0:T(8,128)S(1)} %reshape_squeeze.6, f32[576,24]{1,0:T(8,128)S(1)} %reshape_squeeze.7, f32[576,16]{1,0:T(8,128)S(1)} %broadcast_in_dim.3, f32[576,24]{1,0:T(8,128)S(1)} %reshape_squeeze.6, f32[576,24]{1,0:T(8,128)S(1)} %reshape_squeeze.7, f32[576,16]{1,0:T(8,128)S(1)} %broadcast_in_dim.3), dimensions={1} | concatenate | bytes 589824 | tf_op jit(solution)/shard_map/concatenate | solution.py:455
  7.4 0.0 collective-permute-done.1.far_ref
  7.4 2.3 %collective-permute-start.2 = (f32[24,128]{1,0:T(8,128)S(1)}, f32[24,128]{1,0:T(8,128)S(1)}, u32[]{:S(2)}, u32[]{:S(2)}) collective-permute-start(f32[24,128]{1,0:T(8,128)S(1)} %fusion), channel_id=1, source_target_pairs={{0,2},{1,9},{2,0},{3,5},{4,6},{5,3},{6,4},{7,15},{8,10},{9,1},{10,... | collective-permute-start | bytes 36872 | tf_op jit(solution)/shard_map/ppermute | solution.py:458
  9.8 1.7 %collective-permute-done.2.side_ref = f32[24,128]{1,0:T(8,128)S(1)} collective-permute-done((f32[24,128]{1,0:T(8,128)S(1)}, f32[24,128]{1,0:T(8,128)S(1)}, u32[]{:S(2)}, u32[]{:S(2)}) %collective-permute-start.2) | collective-permute-done | bytes 12320 | tf_op jit(solution)/shard_map/ppermute | solution.py:458
  11.5 0.0 collective-permute-start.3
  11.5 1.2 %collective-permute-done.3.other_ref = f32[24,128]{1,0:T(8,128)S(1)} collective-permute-done((f32[24,128]{1,0:T(8,128)S(1)}, f32[24,128]{1,0:T(8,128)S(1)}, u32[]{:S(2)}, u32[]{:S(2)}) %collective-permute-start.3) | collective-permute-done | bytes 12320 | tf_op jit(solution)/shard_map/ppermute | solution.py:459
  12.6 2.5 %shard_map.165.mine_ref = f32[24,128]{1,0:T(8,128)S(1)} custom-call(f32[2,8,128]{2,1,0:T(8,128)S(1)} %get-tuple-element.56.strength_ref, f32[48,128]{1,0:T(8,128)S(1)} %get-tuple-element.57.own_ref, f32[48,128]{1,0:T(8,128)S(1)} %shard_map.164.near_ref, f32[48,128]{1,0:T(8,128)S(1)} %collective-permute-done.1.far_ref, ...), custom_call_target="tpu_custom_call" | custom-call | flops 1000000 | bytes 1000000 | tf_op jit(solution)/shard_map/pallas_call | solution.py:385
  15.1 0.2 %collective-permute-start.4 = (f32[24,128]{1,0:T(8,128)S(1)}, f32[24,128]{1,0:T(8,128)S(1)}, u32[]{:S(2)}, u32[]{:S(2)}) collective-permute-start(f32[24,128]{1,0:T(8,128)S(1)} %shard_map.165.mine_ref), channel_id=1, source_target_pairs={{0,1},{1,0},{2,3},{3,2},{4,5},{5,4},{6,7},{7,6},{8,9},{9,8},{10,11... | collective-permute-start | bytes 36872 | tf_op jit(solution)/shard_map/ppermute | solution.py:472
  15.4 1.0 %collective-permute-done.4.theirs_ref = f32[24,128]{1,0:T(8,128)S(1)} collective-permute-done((f32[24,128]{1,0:T(8,128)S(1)}, f32[24,128]{1,0:T(8,128)S(1)}, u32[]{:S(2)}, u32[]{:S(2)}) %collective-permute-start.4) | collective-permute-done | bytes 12320 | tf_op jit(solution)/shard_map/ppermute | solution.py:472
  16.4 1.0 %shard_map.166 = f32[128,128]{1,0:T(8,128)} custom-call(f32[24,128]{1,0:T(8,128)S(1)} %shard_map.165.mine_ref, f32[24,128]{1,0:T(8,128)S(1)} %collective-permute-done.4.theirs_ref, bf16[256,256]{1,0:T(8,128)(2,1)S(1)} %get-tuple-element.73.cols_ref, bf16[128,144]{1,0:T(8,128)(2,1)S(1)} %get-tuple-element.74.rows_ref), custom_call_target="tpu_custom_call" | custom-call | flops 1000000 | bytes 1000000 | tf_op jit(solution)/shard_map/pallas_call | solution.py:385
  (2 shorter events, 0.0 us)
Async XLA Ops:
  0.0 5.8 %collective-permute-start = (f32[128,128]{1,0:T(8,128)}, f32[128,128]{1,0:T(8,128)S(1)}, u32[]{:S(2)}, u32[]{:S(2)}) collective-permute-start(f32[128,128]{1,0:T(8,128)} %refs_2_.1), channel_id=1, source_target_pairs={{0,8},{1,3},{2,10},{3,1},{4,12},{5,7},{6,14},{7,5},{8,0},{9,17},{1... | collective-permute-start | bytes 196616 | tf_op jit(solution)/shard_map/ppermute | solution.py:427
  6.2 1.3 %collective-permute-start.1 = (f32[48,128]{1,0:T(8,128)S(1)}, f32[48,128]{1,0:T(8,128)S(1)}, u32[]{:S(2)}, u32[]{:S(2)}) collective-permute-start(f32[48,128]{1,0:T(8,128)S(1)} %shard_map.164.near_ref), channel_id=1, source_target_pairs={{0,1},{1,0},{2,3},{3,2},{4,5},{5,4},{6,7},{7,6},{8,9},{9,8},{10,11... | collective-permute-start | bytes 73736 | tf_op jit(solution)/shard_map/ppermute | solution.py:451
  7.4 4.0 %collective-permute-start.2 = (f32[24,128]{1,0:T(8,128)S(1)}, f32[24,128]{1,0:T(8,128)S(1)}, u32[]{:S(2)}, u32[]{:S(2)}) collective-permute-start(f32[24,128]{1,0:T(8,128)S(1)} %fusion), channel_id=1, source_target_pairs={{0,2},{1,9},{2,0},{3,5},{4,6},{5,3},{6,4},{7,15},{8,10},{9,1},{10,... | collective-permute-start | bytes 36872 | tf_op jit(solution)/shard_map/ppermute | solution.py:458
  11.5 1.2 %collective-permute-start.3 = (f32[24,128]{1,0:T(8,128)S(1)}, f32[24,128]{1,0:T(8,128)S(1)}, u32[]{:S(2)}, u32[]{:S(2)}) collective-permute-start(f32[24,128]{1,0:T(8,128)S(1)} %collective-permute-done.2.side_ref), channel_id=1, source_target_pairs={{0,1},{1,0},{2,3},{3,2},{4,5},{5,4},{6,7},{7,6},{8,9},{9,8},{10,11... | collective-permute-start | bytes 36872 | tf_op jit(solution)/shard_map/ppermute | solution.py:459
  15.1 1.2 %collective-permute-start.4 = (f32[24,128]{1,0:T(8,128)S(1)}, f32[24,128]{1,0:T(8,128)S(1)}, u32[]{:S(2)}, u32[]{:S(2)}) collective-permute-start(f32[24,128]{1,0:T(8,128)S(1)} %shard_map.165.mine_ref), channel_id=1, source_target_pairs={{0,1},{1,0},{2,3},{3,2},{4,5},{5,4},{6,7},{7,6},{8,9},{9,8},{10,11... | collective-permute-start | bytes 36872 | tf_op jit(solution)/shard_map/ppermute | solution.py:472

commit v5 on v4

--- a/solution.py
+++ b/solution.py
@@ -87,16 +87,14 @@
     points = np.arange(count)
     phase = angles(frequencies(), points, count)
     cos, sin = np.cos(phase), np.sin(phase)
-    real_rows = lanes((0, cos), (HALF, sin), (2 * HALF, -sin), (3 * HALF, cos))
-    imag_rows = lanes((0, -sin), (HALF, cos), (2 * HALF, -cos), (3 * HALF, -sin))
-    to_cols = rows_at(
-        2 * HALF,
-        (0, real_rows),
-        (BAND, imag_rows),
-        (HALF, imag_rows),
-        (HALF + BAND, -real_rows),
-    )
-    to_rows = np.concatenate([cos.T, sin.T], 1)
+    one = np.concatenate(
+        [lanes((0, cos), (HALF, sin)), lanes((0, -sin), (HALF, cos)), np.zeros((HALF - count, 2 * HALF))]
+    )
+    none = np.zeros_like(one)
+    to_cols = np.concatenate(
+        [np.concatenate([one, none], 1), np.concatenate([none, one], 1)], 0
+    )
+    to_rows = np.concatenate([cos.T, -sin.T], 1)
     where = (np.arange(tile)[:, None] + MARGIN) / window - points[None, :] / count
     spread = np.ones((tile, count))
     for order in range(1, BAND):
@@ -105,15 +103,6 @@
     spread_cols = rows_at(HALF, (0, spread.T))
     gather_cols = lanes((0, spread), (HALF, spread))
     from_rows = np.concatenate([cos, sin], 0)
-    pad = np.zeros((HALF - count, BAND))
-    c, s = cos.T, sin.T
-
-    def both(real_part, imag_part):
-        return lanes((0, real_part), (BAND, imag_part), (HALF, imag_part), (HALF + BAND, -real_part))
-
-    blocks = [both(c, -s), both(s, c), both(-s, -c), both(c, -s)]
-    empty = np.zeros((HALF - count, 2 * HALF))
-    from_cols = np.concatenate([part for block in blocks for part in (block, empty)], 0)
     return (
         stacked(to_cols, 3),
         six(to_rows),
@@ -122,7 +111,7 @@
         three(spread.T),
         stacked(gather_cols, 2),
         three(from_rows),
-        np.concatenate(pieces(from_cols, 2), 1),
+        np.concatenate(pieces(to_cols.T, 2), 1),
     )
 
 
@@ -255,17 +244,36 @@
     out_ref[...] = jnp.where(valid, share, 0.0)
 
 
+def arrange_kernel(real_ref, imag_ref, first_ref, second_ref):
+    total = real_ref.shape[0] // BAND
+    for pair in range(total // 2):
+        first, second = 0.0, 0.0
+        for part in range(2):
+            at = (2 * pair + part) * BAND
+            pad = jnp.zeros((BAND, 2 * HALF - BAND), F32)
+            real = jnp.concatenate([real_ref[at : at + BAND, :], pad], 1)
+            imag = jnp.concatenate([imag_ref[at : at + BAND, :], pad], 1)
+
+            def moved(value, by):
+                return pltpu.roll(value, part * HALF + by, 1) if part * HALF + by else value
+
+            first = first + (moved(real, 0) + moved(imag, BAND))
+            second = second + (moved(real, BAND) - moved(imag, 0))
+        first_ref[:, pair * 2 * HALF : (pair + 1) * 2 * HALF] = first
+        second_ref[:, pair * 2 * HALF : (pair + 1) * 2 * HALF] = second
+
+
 def field_kernel(
     mesh_shape, strength_ref, own_ref, near_ref, far_ref, side_ref, other_ref,
-    kernels_ref, target_ref, to_cols_ref, to_rows_ref, spread_cols_ref, spread_ref,
-    gather_rows_ref, gather_cols_ref, from_rows_ref, from_cols_ref, out_ref, cols_ref, field_ref,
+    first_ref, second_ref, target_ref, to_cols_ref, to_rows_ref, spread_cols_ref, spread_ref,
+    gather_rows_ref, gather_cols_ref, from_rows_ref, from_cols_ref, out_ref, rows_ref, field_ref,
 ):
     conds = strength_ref.shape[0]
     count = 2 * BAND
-    total = kernels_ref.shape[0] // BAND
-    per = total // conds
+    pairs = first_ref.shape[1] // (2 * HALF)
+    per = 2 * pairs // conds
     tile = target_ref.shape[0]
-
+    wide = 4 * HALF
     col, core = lax.axis_index("col"), lax.axis_index("cond")
 
     def half(value, core):
@@ -278,43 +286,42 @@
     spectrum = own_ref[BAND:] + near_ref[BAND:] + far_ref[BAND:]
     spectrum += half(side_ref[...], core) + half(other_ref[...], 1 - core)
     lane = lane_ids(spectrum.shape) % HALF
-    onto_next = jnp.where(lane < BAND, spectrum, 0.0)
-    onto_last = jnp.where(lane >= BAND, spectrum, 0.0)
-    spectrum = jnp.where(
-        lane_ids(spectrum.shape) < HALF,
-        onto_next + pltpu.roll(onto_next, BAND, 1),
-        onto_last + pltpu.roll(onto_last, 2 * HALF - BAND, 1),
-    )
-
-    kernels = kernels_ref[...].reshape(total, BAND, 2 * HALF)
-    product = (kernels * spectrum[None]).reshape(total * BAND, 2 * HALF)
-    high, mid, low = split(product, 3)
+    real = jnp.where(lane < BAND, spectrum, 0.0)
+    imag = jnp.where(lane >= BAND, spectrum, 0.0)
+    real = real + pltpu.roll(real, BAND, 1)
+    imag = imag + pltpu.roll(imag, 2 * HALF - BAND, 1)
+
+    to_rows = to_rows_ref[...]
+    for quad in range(pairs // 2):
+        blocks = []
+        for pair in (2 * quad, 2 * quad + 1):
+            one = first_ref[:, pair * 2 * HALF : (pair + 1) * 2 * HALF]
+            two = second_ref[:, pair * 2 * HALF : (pair + 1) * 2 * HALF]
+            blocks.append(jnp.concatenate([one * real + two * imag, one * imag - two * real], 0))
+        both = dot(to_rows, six_right(jnp.concatenate(blocks, 1)))
+        for part in range(2):
+            at = (2 * quad + part) * count
+            rows_ref[at : at + count, :] = both[:, part * 2 * HALF : (part + 1) * 2 * HALF]
+
+    high, mid, low = split(rows_ref[...], 3)
     size = 2 * HALF
     wh, wm, wl = to_cols_ref[:size], to_cols_ref[size : 2 * size], to_cols_ref[2 * size :]
-    cols_ref[...] = dot(
+    field_ref[...] = dot(
         jnp.concatenate([high, mid, low, high, mid, high], 1),
         jnp.concatenate([wh, wh, wh, wm, wm, wl], 0),
     )
-
     sums = [jnp.zeros((count, 2 * HALF), F32) for _ in range(conds)]
-    to_rows = to_rows_ref[...]
-    for pair in range(total // 2):
-        rights = []
-        for k in (2 * pair, 2 * pair + 1):
-            block = cols_ref[k * BAND : (k + 1) * BAND, :]
-            block = jnp.concatenate([block[:, : 2 * HALF], block[:, 2 * HALF :]], 0)
-            rights.append(six_right(block))
-        both = dot(to_rows, jnp.concatenate(rights, 1))
-        field_ref[pair] = both
+    for pair in range(pairs):
+        both = field_ref[pair * count : (pair + 1) * count, :]
         squares = both * both
         for part in range(2):
             c = (2 * pair + part) // per
             sums[c] = sums[c] + squares[:, part * 2 * HALF : (part + 1) * 2 * HALF]
 
     coarse = jnp.concatenate([value + pltpu.roll(value, HALF, 1) for value in sums], 0)
-    wide = dot(doubled(coarse), doubled_weights(spread_cols_ref))
+    lines = dot(doubled(coarse), doubled_weights(spread_cols_ref))
     right = jnp.concatenate(
-        [six_right(wide[c * count : (c + 1) * count]) for c in range(conds)], 1
+        [six_right(lines[c * count : (c + 1) * count]) for c in range(conds)], 1
     )
     image = dot(spread_ref[...], right)
 
@@ -332,30 +339,39 @@
         jnp.concatenate([back[:, c * tile : (c + 1) * tile] for c in range(conds)], 0), 2
     )
     gh, gl = gather_cols_ref[:tile], gather_cols_ref[tile:]
-    slope = dot(
-        jnp.concatenate([high, low, high], 1), jnp.concatenate([gh, gh, gl], 0)
-    )
+    slope = dot(jnp.concatenate([high, low, high], 1), jnp.concatenate([gh, gh, gl], 0))
+
+    for pair in range(pairs):
+        weight = []
+        for k in (2 * pair, 2 * pair + 1):
+            weight.append(slope[k // per * count : (k // per + 1) * count])
+        at = pair * count
+        field_ref[at : at + count, :] = field_ref[at : at + count, :] * jnp.concatenate(weight, 1)
+    high, low = split(field_ref[...], 2)
+    weights = from_cols_ref[...]
+    back = dot(high, weights)
+    rows_ref[...] = back[:, : 2 * HALF] + back[:, 2 * HALF :] + dot(low, weights[:, : 2 * HALF])
 
     from_rows = from_rows_ref[...]
-    for pair in range(total // 2):
-        weight = [
-            slope[((2 * pair + part) // per) * count : ((2 * pair + part) // per + 1) * count]
-            for part in range(2)
-        ]
-        scaled = field_ref[pair] * jnp.concatenate(weight, 1)
-        back = dot(from_rows, three_right(scaled))
-        for part in range(2):
-            block = back[:, part * 2 * HALF : (part + 1) * 2 * HALF]
-            k = 2 * pair + part
-            cols_ref[k * BAND : (k + 1) * BAND, :] = jnp.concatenate(
-                [block[:BAND], block[BAND:]], 1
-            )
-    high, low = split(cols_ref[...], 2)
-    weights = from_cols_ref[...]
-    first = dot(high, weights)
-    back = first[:, : 2 * HALF] + first[:, 2 * HALF :] + dot(low, weights[:, : 2 * HALF])
-    back = back.reshape(total, BAND, 2 * HALF)
-    out_ref[...] = jnp.sum(kernels_ref[...].reshape(total, BAND, 2 * HALF) * back, axis=0)
+    sum_one, sum_two = 0.0, 0.0
+    for quad in range(pairs // 2):
+        at = 2 * quad * count
+        value = jnp.concatenate(
+            [rows_ref[at : at + count, :], rows_ref[at + count : at + 2 * count, :]], 1
+        )
+        back = dot(from_rows, three_right(value))
+        top, bottom = back[:BAND], back[BAND:]
+        one = first_ref[:, quad * wide : (quad + 1) * wide]
+        two = second_ref[:, quad * wide : (quad + 1) * wide]
+        sum_one = sum_one + (one * top + two * bottom)
+        sum_two = sum_two + (two * top - one * bottom)
+    sum_one = sum_one[:, : 2 * HALF] + sum_one[:, 2 * HALF :]
+    sum_two = sum_two[:, : 2 * HALF] + sum_two[:, 2 * HALF :]
+    out_ref[...] = jnp.where(
+        lane_ids(sum_one.shape) < HALF,
+        sum_one + pltpu.roll(sum_one, HALF, 1),
+        sum_two + pltpu.roll(sum_two, HALF, 1),
+    )
 
 
 def adjoint_kernel(mine_ref, theirs_ref, cols_ref, rows_ref, out_ref):
@@ -451,22 +467,21 @@
     far = lax.ppermute(near, "cond", swap)
     real = chosen[:, :, 0].reshape(conds * count * BAND, BAND)
     imag = chosen[:, :, 1].reshape(conds * count * BAND, BAND)
-    gap = jnp.zeros((real.shape[0], HALF - 2 * BAND), F32)
-    arranged = jnp.concatenate([real, imag, gap] * 2, 1)
+    total = conds * count
+    arranged = call(arrange_kernel, [(BAND, total * HALF)] * 2, [VMEM] * 2, (real, imag))
     far, arranged = lax.optimization_barrier((far, arranged))
     message = own[:BAND] + near[:BAND] + far[:BAND]
     side = lax.ppermute(message, AXES, swaps(mesh_shape, 1))
     other = lax.ppermute(side, "cond", swap)
 
-    total = conds * count
     cotangent = call(
         functools.partial(field_kernel, mesh_shape),
         [(BAND, 2 * HALF)],
-        [VMEM] * 16,
-        (strength, own, near, far, side, other, arranged, *later[:-2]),
+        [VMEM] * 17,
+        (strength, own, near, far, side, other, *arranged, *later[:-2]),
         scratch=[
+            pltpu.VMEM((total * BAND, 2 * HALF), F32),
             pltpu.VMEM((total * BAND, 4 * HALF), F32),
-            pltpu.VMEM((total // 2, 2 * BAND, 4 * HALF), F32),
         ],
     )
     theirs = lax.ppermute(cotangent, "cond", swap)

time: 17.5 us -> 17.2 us (0.983)
  local copies, waits for them, and re-layouts: 1.12 us -> 0.62 us
  waiting for transfers between devices: 4.56 us -> 4.79 us
    concatenate x1 -> x0, local copies, waits for them, and re-layouts: 0.48 us -> none  [shards(): arranged = jnp.concatenate([real, imag, gap] * 2, 1)]
    ppermute x1, waiting for transfers between devices: 0.03 us -> 0.25 us  [shards(): far = lax.ppermute(near, 'cond', swap)]
    pallas_call x4 -> x5, Pallas kernels: 5.97 us -> 6.1 us  [call(): pl.pallas_call(body, out_shape=shapes[0] if one else shapes, in_specs=spe...]
  transfers between devices with their start and end apart: 5 -> 5, of which waited for: 4 -> 5; matrix products, arithmetic and copies ran while one was open for 6% -> 4% of each run, Pallas kernels for 12% -> 14%
where the time goes in v5:
time: 17.2 us; the launch traced here: 17.1 us
  Pallas kernels  6.1 us (35%)
  starting transfers between devices  5.53 us (32%)
  waiting for transfers between devices  4.79 us (28%)
  local copies, waits for them, and re-layouts  0.62 us (4%)
    pallas_call x5, Pallas kernels, call(): pl.pallas_call(body, out_shape=shapes[0] if one else shapes, in_specs=spe...  6.1 us
    ppermute x1, starting transfers between devices, shards(): beside = lax.ppermute(mask, AXES, swaps(mesh_shape, 0))  2.97 us
    ppermute x1, starting transfers between devices, shards(): side = lax.ppermute(message, AXES, swaps(mesh_shape, 1))  2.29 us
    ppermute x1, waiting for transfers between devices, shards(): side = lax.ppermute(message, AXES, swaps(mesh_shape, 1))  1.67 us
    ppermute x1, waiting for transfers between devices, shards(): other = lax.ppermute(side, 'cond', swap)  1.18 us
    ppermute x1, waiting for transfers between devices, shards(): theirs = lax.ppermute(cotangent, 'cond', swap)  1.01 us
    ppermute x1, waiting for transfers between devices, shards(): beside = lax.ppermute(mask, AXES, swaps(mesh_shape, 0))  0.68 us
  transfers between devices with their start and end apart: 5, of which 5 were waited for; matrix products, arithmetic and copies ran while one was open for 4% of the time, Pallas kernels for 14%

profile of v5, /device:TPU:0, one launch (start us, length us, event | category | flops | bytes accessed | tf_op | source)
XLA Modules:
  0.0 17.1 jit_solution(3596246350192396930)
XLA Ops:
  0.0 3.0 %collective-permute-start = (f32[128,128]{1,0:T(8,128)}, f32[128,128]{1,0:T(8,128)S(1)}, u32[]{:S(2)}, u32[]{:S(2)}) collective-permute-start(f32[128,128]{1,0:T(8,128)} %refs_2_.1), channel_id=1, source_target_pairs={{0,8},{1,3},{2,10},{3,1},{4,12},{5,7},{6,14},{7,5},{8,0},{9,17},{1... | collective-permute-start | bytes 196616 | tf_op jit(solution)/shard_map/ppermute | solution.py:443
  3.0 2.1 %shard_map.163 = (f32[48,128]{1,0:T(8,128)S(1)}, f32[2,12,2,576]{3,2,1,0:T(2,128)S(1)}, f32[2,8,128]{2,1,0:T(8,128)S(1)}, bf16[256,256]{1,0:T(8,128)(2,1)S(1)}, ...) custom-call(s32[2]{0:T(128)} %refs_0_.1, ...), custom_call_target="tpu_custom_call" | custom-call | flops 1000000 | bytes 1000000 | tf_op jit(solution)/shard_map/pallas_call | solution.py:401
  5.1 0.7 %collective-permute-done.tile_ref = f32[128,128]{1,0:T(8,128)S(1)} collective-permute-done((f32[128,128]{1,0:T(8,128)}, f32[128,128]{1,0:T(8,128)S(1)}, u32[]{:S(2)}, u32[]{:S(2)}) %collective-permute-start) | collective-permute-done | bytes 65568 | tf_op jit(solution)/shard_map/ppermute | solution.py:443
  5.8 0.4 %shard_map.164.near_ref = f32[48,128]{1,0:T(8,128)S(1)} custom-call(f32[128,128]{1,0:T(8,128)S(1)} %collective-permute-done.tile_ref, bf16[256,256]{1,0:T(8,128)(2,1)S(1)} %get-tuple-element.62.col_ref, bf16[144,384]{1,0:T(8,128)(2,1)S(1)} %get-tuple-element.63.row_ref), custom_call_target="tpu_custom_call" | custom-call | flops 1000000 | bytes 1000000 | tf_op jit(solution)/shard_map/pallas_call | solution.py:401
  6.2 0.1 collective-permute-start.1
  6.3 0.3 %slice_reduce_fusion = (f32[2,12,576]{2,1,0:T(8,128)S(1)}, f32[2,12,576]{2,1,0:T(8,128)S(1)}) fusion(f32[2,12,2,576]{3,2,1,0:T(2,128)S(1)} %get-tuple-element.64), kind=kLoop, calls=%fused_computation | loop fusion | bytes 221184 | tf_op jit(solution)/shard_map/slice | solution.py:469
  6.6 0.1 reshape_squeeze.7.imag_ref
  6.7 0.1 reshape_squeeze.6.real_ref
  6.9 0.3 %shard_map.165 = (f32[24,1536]{1,0:T(8,128)S(1)}, f32[24,1536]{1,0:T(8,128)S(1)}) custom-call(f32[576,24]{1,0:T(8,128)S(1)} %reshape_squeeze.6.real_ref, f32[576,24]{1,0:T(8,128)S(1)} %reshape_squeeze.7.imag_ref), custom_call_target="tpu_custom_call" | custom-call | flops 1000000 | bytes 1000000 | tf_op jit(solution)/shard_map/pallas_call | solution.py:401
  7.2 0.2 %collective-permute-done.1.far_ref = f32[48,128]{1,0:T(8,128)S(1)} collective-permute-done((f32[48,128]{1,0:T(8,128)S(1)}, f32[48,128]{1,0:T(8,128)S(1)}, u32[]{:S(2)}, u32[]{:S(2)}) %collective-permute-start.1) | collective-permute-done | bytes 24608 | tf_op jit(solution)/shard_map/ppermute | solution.py:467
  7.4 2.3 %collective-permute-start.2 = (f32[24,128]{1,0:T(8,128)S(1)}, f32[24,128]{1,0:T(8,128)S(1)}, u32[]{:S(2)}, u32[]{:S(2)}) collective-permute-start(f32[24,128]{1,0:T(8,128)S(1)} %fusion), channel_id=1, source_target_pairs={{0,2},{1,9},{2,0},{3,5},{4,6},{5,3},{6,4},{7,15},{8,10},{9,1},{10,... | collective-permute-start | bytes 36872 | tf_op jit(solution)/shard_map/ppermute | solution.py:474
  9.7 1.7 %collective-permute-done.2.side_ref = f32[24,128]{1,0:T(8,128)S(1)} collective-permute-done((f32[24,128]{1,0:T(8,128)S(1)}, f32[24,128]{1,0:T(8,128)S(1)}, u32[]{:S(2)}, u32[]{:S(2)}) %collective-permute-start.2) | collective-permute-done | bytes 12320 | tf_op jit(solution)/shard_map/ppermute | solution.py:474
  11.4 0.0 collective-permute-start.3
  11.4 1.2 %collective-permute-done.3.other_ref = f32[24,128]{1,0:T(8,128)S(1)} collective-permute-done((f32[24,128]{1,0:T(8,128)S(1)}, f32[24,128]{1,0:T(8,128)S(1)}, u32[]{:S(2)}, u32[]{:S(2)}) %collective-permute-start.3) | collective-permute-done | bytes 12320 | tf_op jit(solution)/shard_map/ppermute | solution.py:475
  12.6 2.3 %shard_map.166.mine_ref = f32[24,128]{1,0:T(8,128)S(1)} custom-call(f32[2,8,128]{2,1,0:T(8,128)S(1)} %get-tuple-element.59.strength_ref, f32[48,128]{1,0:T(8,128)S(1)} %get-tuple-element.60.own_ref, f32[48,128]{1,0:T(8,128)S(1)} %shard_map.164.near_ref, f32[48,128]{1,0:T(8,128)S(1)} %collective-permute-done.1.far_ref, ...), custom_call_target="tpu_custom_call" | custom-call | flops 1000000 | bytes 1000000 | tf_op jit(solution)/shard_map/pallas_call | solution.py:401
  14.9 0.2 %collective-permute-start.4 = (f32[24,128]{1,0:T(8,128)S(1)}, f32[24,128]{1,0:T(8,128)S(1)}, u32[]{:S(2)}, u32[]{:S(2)}) collective-permute-start(f32[24,128]{1,0:T(8,128)S(1)} %shard_map.166.mine_ref), channel_id=1, source_target_pairs={{0,1},{1,0},{2,3},{3,2},{4,5},{5,4},{6,7},{7,6},{8,9},{9,8},{10,11... | collective-permute-start | bytes 36872 | tf_op jit(solution)/shard_map/ppermute | solution.py:487
  15.1 1.0 %collective-permute-done.4.theirs_ref = f32[24,128]{1,0:T(8,128)S(1)} collective-permute-done((f32[24,128]{1,0:T(8,128)S(1)}, f32[24,128]{1,0:T(8,128)S(1)}, u32[]{:S(2)}, u32[]{:S(2)}) %collective-permute-start.4) | collective-permute-done | bytes 12320 | tf_op jit(solution)/shard_map/ppermute | solution.py:487
  16.1 1.0 %shard_map.167 = f32[128,128]{1,0:T(8,128)} custom-call(f32[24,128]{1,0:T(8,128)S(1)} %shard_map.166.mine_ref, f32[24,128]{1,0:T(8,128)S(1)} %collective-permute-done.4.theirs_ref, bf16[256,256]{1,0:T(8,128)(2,1)S(1)} %get-tuple-element.79.cols_ref, bf16[128,144]{1,0:T(8,128)(2,1)S(1)} %get-tuple-element.80.rows_ref), custom_call_target="tpu_custom_call" | custom-call | flops 1000000 | bytes 1000000 | tf_op jit(solution)/shard_map/pallas_call | solution.py:401
  (1 shorter events, 0.0 us)
Async XLA Ops:
  0.0 5.8 %collective-permute-start = (f32[128,128]{1,0:T(8,128)}, f32[128,128]{1,0:T(8,128)S(1)}, u32[]{:S(2)}, u32[]{:S(2)}) collective-permute-start(f32[128,128]{1,0:T(8,128)} %refs_2_.1), channel_id=1, source_target_pairs={{0,8},{1,3},{2,10},{3,1},{4,12},{5,7},{6,14},{7,5},{8,0},{9,17},{1... | collective-permute-start | bytes 196616 | tf_op jit(solution)/shard_map/ppermute | solution.py:443
  6.2 1.3 %collective-permute-start.1 = (f32[48,128]{1,0:T(8,128)S(1)}, f32[48,128]{1,0:T(8,128)S(1)}, u32[]{:S(2)}, u32[]{:S(2)}) collective-permute-start(f32[48,128]{1,0:T(8,128)S(1)} %shard_map.164.near_ref), channel_id=1, source_target_pairs={{0,1},{1,0},{2,3},{3,2},{4,5},{5,4},{6,7},{7,6},{8,9},{9,8},{10,11... | collective-permute-start | bytes 73736 | tf_op jit(solution)/shard_map/ppermute | solution.py:467
  7.4 4.0 %collective-permute-start.2 = (f32[24,128]{1,0:T(8,128)S(1)}, f32[24,128]{1,0:T(8,128)S(1)}, u32[]{:S(2)}, u32[]{:S(2)}) collective-permute-start(f32[24,128]{1,0:T(8,128)S(1)} %fusion), channel_id=1, source_target_pairs={{0,2},{1,9},{2,0},{3,5},{4,6},{5,3},{6,4},{7,15},{8,10},{9,1},{10,... | collective-permute-start | bytes 36872 | tf_op jit(solution)/shard_map/ppermute | solution.py:474
  11.4 1.2 %collective-permute-start.3 = (f32[24,128]{1,0:T(8,128)S(1)}, f32[24,128]{1,0:T(8,128)S(1)}, u32[]{:S(2)}, u32[]{:S(2)}) collective-permute-start(f32[24,128]{1,0:T(8,128)S(1)} %collective-permute-done.2.side_ref), channel_id=1, source_target_pairs={{0,1},{1,0},{2,3},{3,2},{4,5},{5,4},{6,7},{7,6},{8,9},{9,8},{10,11... | collective-permute-start | bytes 36872 | tf_op jit(solution)/shard_map/ppermute | solution.py:475
  14.9 1.2 %collective-permute-start.4 = (f32[24,128]{1,0:T(8,128)S(1)}, f32[24,128]{1,0:T(8,128)S(1)}, u32[]{:S(2)}, u32[]{:S(2)}) collective-permute-start(f32[24,128]{1,0:T(8,128)S(1)} %shard_map.166.mine_ref), channel_id=1, source_target_pairs={{0,1},{1,0},{2,3},{3,2},{4,5},{5,4},{6,7},{7,6},{8,9},{9,8},{10,11... | collective-permute-start | bytes 36872 | tf_op jit(solution)/shard_map/ppermute | solution.py:487

commit v6 on v5

--- a/solution.py
+++ b/solution.py
@@ -52,11 +52,6 @@
     for at, block in blocks:
         out[at : at + block.shape[0]] = block
     return out
-
-
-def six(table):
-    high, mid, low = pieces(table, 3)
-    return np.concatenate([high, high, high, mid, mid, low], 1)
 
 
 def three(table):
@@ -104,10 +99,10 @@
     gather_cols = lanes((0, spread), (HALF, spread))
     from_rows = np.concatenate([cos, sin], 0)
     return (
-        stacked(to_cols, 3),
-        six(to_rows),
-        stacked(spread_cols, 3),
-        six(spread),
+        stacked(to_cols, 2),
+        three(to_rows),
+        stacked(spread_cols, 2),
+        three(spread),
         three(spread.T),
         stacked(gather_cols, 2),
         three(from_rows),
@@ -153,24 +148,15 @@
 
 
 def doubled(value):
-    low_half = lane_ids(value.shape) < HALF
     high = value.astype(BF).astype(F32)
-    rest = value - high
-    mid = rest.astype(BF).astype(F32)
-    first = jnp.where(low_half, high, rest).astype(BF)
-    second = jnp.where(low_half, rest - mid, high).astype(BF)
-    return jnp.concatenate([first, first, second], 1)
-
-
-def doubled_weights(ref):
-    size = ref.shape[0] // 3
-    high, mid, low = ref[:size], ref[size : 2 * size], ref[2 * size :]
-    return jnp.concatenate([high, high, mid, mid, high, low], 0)
-
-
-def six_right(value):
-    high, mid, low = split(value, 3)
-    return jnp.concatenate([high, mid, low, high, mid, high], 0)
+    part = jnp.where(lane_ids(value.shape) < HALF, high, value - high).astype(BF)
+    return jnp.concatenate([part, part], 1)
+
+
+def four_weights(ref):
+    size = ref.shape[0] // 2
+    high, low = ref[:size], ref[size:]
+    return jnp.concatenate([high, high, low, low], 0)
 
 
 def three_right(value):
@@ -298,18 +284,16 @@
             one = first_ref[:, pair * 2 * HALF : (pair + 1) * 2 * HALF]
             two = second_ref[:, pair * 2 * HALF : (pair + 1) * 2 * HALF]
             blocks.append(jnp.concatenate([one * real + two * imag, one * imag - two * real], 0))
-        both = dot(to_rows, six_right(jnp.concatenate(blocks, 1)))
+        both = dot(to_rows, three_right(jnp.concatenate(blocks, 1)))
         for part in range(2):
             at = (2 * quad + part) * count
             rows_ref[at : at + count, :] = both[:, part * 2 * HALF : (part + 1) * 2 * HALF]
 
-    high, mid, low = split(rows_ref[...], 3)
-    size = 2 * HALF
-    wh, wm, wl = to_cols_ref[:size], to_cols_ref[size : 2 * size], to_cols_ref[2 * size :]
-    field_ref[...] = dot(
-        jnp.concatenate([high, mid, low, high, mid, high], 1),
-        jnp.concatenate([wh, wh, wh, wm, wm, wl], 0),
-    )
+    weights = four_weights(to_cols_ref)
+    chunk = rows_ref.shape[0] // 2
+    for at in (0, chunk):
+        high, low = split(rows_ref[at : at + chunk, :], 2)
+        field_ref[at : at + chunk, :] = dot(jnp.concatenate([high, low, high, low], 1), weights)
     sums = [jnp.zeros((count, 2 * HALF), F32) for _ in range(conds)]
     for pair in range(pairs):
         both = field_ref[pair * count : (pair + 1) * count, :]
@@ -319,9 +303,9 @@
             sums[c] = sums[c] + squares[:, part * 2 * HALF : (part + 1) * 2 * HALF]
 
     coarse = jnp.concatenate([value + pltpu.roll(value, HALF, 1) for value in sums], 0)
-    lines = dot(doubled(coarse), doubled_weights(spread_cols_ref))
+    lines = dot(doubled(coarse), four_weights(spread_cols_ref))
     right = jnp.concatenate(
-        [six_right(lines[c * count : (c + 1) * count]) for c in range(conds)], 1
+        [three_right(lines[c * count : (c + 1) * count]) for c in range(conds)], 1
     )
     image = dot(spread_ref[...], right)
 
@@ -347,10 +331,18 @@
             weight.append(slope[k // per * count : (k // per + 1) * count])
         at = pair * count
         field_ref[at : at + count, :] = field_ref[at : at + count, :] * jnp.concatenate(weight, 1)
-    high, low = split(field_ref[...], 2)
     weights = from_cols_ref[...]
-    back = dot(high, weights)
-    rows_ref[...] = back[:, : 2 * HALF] + back[:, 2 * HALF :] + dot(low, weights[:, : 2 * HALF])
+    weights = jnp.concatenate(
+        [
+            weights,
+            jnp.concatenate([weights[:, : 2 * HALF], jnp.zeros((wide, 2 * HALF), BF)], 1),
+        ],
+        0,
+    )
+    for at in (0, chunk):
+        high, low = split(field_ref[at : at + chunk, :], 2)
+        back = dot(jnp.concatenate([high, low], 1), weights)
+        rows_ref[at : at + chunk, :] = back[:, : 2 * HALF] + back[:, 2 * HALF :]
 
     from_rows = from_rows_ref[...]
     sum_one, sum_two = 0.0, 0.0

time: 17.2 us -> 16.7 us (0.971)
  Pallas kernels: 6.1 us -> 5.55 us
    pallas_call x5, Pallas kernels: 6.1 us -> 5.55 us  [call(): pl.pallas_call(body, out_shape=shapes[0] if one else shapes, in_specs=spe...]
where the time goes in v6:
time: 16.7 us; the launch traced here: 16.6 us
  Pallas kernels  5.55 us (33%)
  starting transfers between devices  5.5 us (33%)
  waiting for transfers between devices  4.83 us (29%)
  local copies, waits for them, and re-layouts  0.62 us (4%)
    pallas_call x5, Pallas kernels, call(): pl.pallas_call(body, out_shape=shapes[0] if one else shapes, in_specs=spe...  5.55 us
    ppermute x1, starting transfers between devices, shards(): beside = lax.ppermute(mask, AXES, swaps(mesh_shape, 0))  2.97 us
    ppermute x1, starting transfers between devices, shards(): side = lax.ppermute(message, AXES, swaps(mesh_shape, 1))  2.29 us
    ppermute x1, waiting for transfers between devices, shards(): side = lax.ppermute(message, AXES, swaps(mesh_shape, 1))  1.67 us
    ppermute x1, waiting for transfers between devices, shards(): other = lax.ppermute(side, 'cond', swap)  1.18 us
    ppermute x1, waiting for transfers between devices, shards(): theirs = lax.ppermute(cotangent, 'cond', swap)  1.01 us
    ppermute x1, waiting for transfers between devices, shards(): beside = lax.ppermute(mask, AXES, swaps(mesh_shape, 0))  0.72 us
  transfers between devices with their start and end apart: 5, of which 5 were waited for; matrix products, arithmetic and copies ran while one was open for 4% of the time, Pallas kernels for 14%

profile of v6, /device:TPU:0, one launch (start us, length us, event | category | flops | bytes accessed | tf_op | source)
XLA Modules:
  0.0 16.6 jit_solution(10119640015467321374)
XLA Ops:
  0.0 3.0 %collective-permute-start = (f32[128,128]{1,0:T(8,128)}, f32[128,128]{1,0:T(8,128)S(1)}, u32[]{:S(2)}, u32[]{:S(2)}) collective-permute-start(f32[128,128]{1,0:T(8,128)} %refs_2_.1), channel_id=1, source_target_pairs={{0,8},{1,3},{2,10},{3,1},{4,12},{5,7},{6,14},{7,5},{8,0},{9,17},{1... | collective-permute-start | bytes 196616 | tf_op jit(solution)/shard_map/ppermute | solution.py:435
  3.0 2.1 %shard_map.163 = (f32[48,128]{1,0:T(8,128)S(1)}, f32[2,12,2,576]{3,2,1,0:T(2,128)S(1)}, f32[2,8,128]{2,1,0:T(8,128)S(1)}, bf16[256,256]{1,0:T(8,128)(2,1)S(1)}, ...) custom-call(s32[2]{0:T(128)} %refs_0_.1, ...), custom_call_target="tpu_custom_call" | custom-call | flops 1000000 | bytes 1000000 | tf_op jit(solution)/shard_map/pallas_call | solution.py:393
  5.0 0.7 %collective-permute-done.tile_ref = f32[128,128]{1,0:T(8,128)S(1)} collective-permute-done((f32[128,128]{1,0:T(8,128)}, f32[128,128]{1,0:T(8,128)S(1)}, u32[]{:S(2)}, u32[]{:S(2)}) %collective-permute-start) | collective-permute-done | bytes 65568 | tf_op jit(solution)/shard_map/ppermute | solution.py:435
  5.8 0.4 %shard_map.164.near_ref = f32[48,128]{1,0:T(8,128)S(1)} custom-call(f32[128,128]{1,0:T(8,128)S(1)} %collective-permute-done.tile_ref, bf16[256,256]{1,0:T(8,128)(2,1)S(1)} %get-tuple-element.62.col_ref, bf16[144,384]{1,0:T(8,128)(2,1)S(1)} %get-tuple-element.63.row_ref), custom_call_target="tpu_custom_call" | custom-call | flops 1000000 | bytes 1000000 | tf_op jit(solution)/shard_map/pallas_call | solution.py:393
  6.2 0.1 collective-permute-start.1
  6.3 0.3 %slice_reduce_fusion = (f32[2,12,576]{2,1,0:T(8,128)S(1)}, f32[2,12,576]{2,1,0:T(8,128)S(1)}) fusion(f32[2,12,2,576]{3,2,1,0:T(2,128)S(1)} %get-tuple-element.64), kind=kLoop, calls=%fused_computation | loop fusion | bytes 221184 | tf_op jit(solution)/shard_map/slice | solution.py:461
  6.6 0.1 reshape_squeeze.7.imag_ref
  6.7 0.1 reshape_squeeze.6.real_ref
  6.9 0.3 %shard_map.165 = (f32[24,1536]{1,0:T(8,128)S(1)}, f32[24,1536]{1,0:T(8,128)S(1)}) custom-call(f32[576,24]{1,0:T(8,128)S(1)} %reshape_squeeze.6.real_ref, f32[576,24]{1,0:T(8,128)S(1)} %reshape_squeeze.7.imag_ref), custom_call_target="tpu_custom_call" | custom-call | flops 1000000 | bytes 1000000 | tf_op jit(solution)/shard_map/pallas_call | solution.py:393
  7.2 0.2 %collective-permute-done.1.far_ref = f32[48,128]{1,0:T(8,128)S(1)} collective-permute-done((f32[48,128]{1,0:T(8,128)S(1)}, f32[48,128]{1,0:T(8,128)S(1)}, u32[]{:S(2)}, u32[]{:S(2)}) %collective-permute-start.1) | collective-permute-done | bytes 24608 | tf_op jit(solution)/shard_map/ppermute | solution.py:459
  7.4 2.3 %collective-permute-start.2 = (f32[24,128]{1,0:T(8,128)S(1)}, f32[24,128]{1,0:T(8,128)S(1)}, u32[]{:S(2)}, u32[]{:S(2)}) collective-permute-start(f32[24,128]{1,0:T(8,128)S(1)} %fusion), channel_id=1, source_target_pairs={{0,2},{1,9},{2,0},{3,5},{4,6},{5,3},{6,4},{7,15},{8,10},{9,1},{10,... | collective-permute-start | bytes 36872 | tf_op jit(solution)/shard_map/ppermute | solution.py:466
  9.7 1.7 %collective-permute-done.2.side_ref = f32[24,128]{1,0:T(8,128)S(1)} collective-permute-done((f32[24,128]{1,0:T(8,128)S(1)}, f32[24,128]{1,0:T(8,128)S(1)}, u32[]{:S(2)}, u32[]{:S(2)}) %collective-permute-start.2) | collective-permute-done | bytes 12320 | tf_op jit(solution)/shard_map/ppermute | solution.py:466
  11.4 0.0 collective-permute-start.3
  11.4 1.2 %collective-permute-done.3.other_ref = f32[24,128]{1,0:T(8,128)S(1)} collective-permute-done((f32[24,128]{1,0:T(8,128)S(1)}, f32[24,128]{1,0:T(8,128)S(1)}, u32[]{:S(2)}, u32[]{:S(2)}) %collective-permute-start.3) | collective-permute-done | bytes 12320 | tf_op jit(solution)/shard_map/ppermute | solution.py:467
  12.6 1.8 %shard_map.166.mine_ref = f32[24,128]{1,0:T(8,128)S(1)} custom-call(f32[2,8,128]{2,1,0:T(8,128)S(1)} %get-tuple-element.59.strength_ref, f32[48,128]{1,0:T(8,128)S(1)} %get-tuple-element.60.own_ref, f32[48,128]{1,0:T(8,128)S(1)} %shard_map.164.near_ref, f32[48,128]{1,0:T(8,128)S(1)} %collective-permute-done.1.far_ref, ...), custom_call_target="tpu_custom_call" | custom-call | flops 1000000 | bytes 1000000 | tf_op jit(solution)/shard_map/pallas_call | solution.py:393
  14.4 0.2 %collective-permute-start.4 = (f32[24,128]{1,0:T(8,128)S(1)}, f32[24,128]{1,0:T(8,128)S(1)}, u32[]{:S(2)}, u32[]{:S(2)}) collective-permute-start(f32[24,128]{1,0:T(8,128)S(1)} %shard_map.166.mine_ref), channel_id=1, source_target_pairs={{0,1},{1,0},{2,3},{3,2},{4,5},{5,4},{6,7},{7,6},{8,9},{9,8},{10,11... | collective-permute-start | bytes 36872 | tf_op jit(solution)/shard_map/ppermute | solution.py:479
  14.6 1.0 %collective-permute-done.4.theirs_ref = f32[24,128]{1,0:T(8,128)S(1)} collective-permute-done((f32[24,128]{1,0:T(8,128)S(1)}, f32[24,128]{1,0:T(8,128)S(1)}, u32[]{:S(2)}, u32[]{:S(2)}) %collective-permute-start.4) | collective-permute-done | bytes 12320 | tf_op jit(solution)/shard_map/ppermute | solution.py:479
  15.6 1.0 %shard_map.167 = f32[128,128]{1,0:T(8,128)} custom-call(f32[24,128]{1,0:T(8,128)S(1)} %shard_map.166.mine_ref, f32[24,128]{1,0:T(8,128)S(1)} %collective-permute-done.4.theirs_ref, bf16[256,256]{1,0:T(8,128)(2,1)S(1)} %get-tuple-element.79.cols_ref, bf16[128,144]{1,0:T(8,128)(2,1)S(1)} %get-tuple-element.80.rows_ref), custom_call_target="tpu_custom_call" | custom-call | flops 1000000 | bytes 1000000 | tf_op jit(solution)/shard_map/pallas_call | solution.py:393
  (1 shorter events, 0.0 us)
Async XLA Ops:
  0.0 5.8 %collective-permute-start = (f32[128,128]{1,0:T(8,128)}, f32[128,128]{1,0:T(8,128)S(1)}, u32[]{:S(2)}, u32[]{:S(2)}) collective-permute-start(f32[128,128]{1,0:T(8,128)} %refs_2_.1), channel_id=1, source_target_pairs={{0,8},{1,3},{2,10},{3,1},{4,12},{5,7},{6,14},{7,5},{8,0},{9,17},{1... | collective-permute-start | bytes 196616 | tf_op jit(solution)/shard_map/ppermute | solution.py:435
  6.2 1.3 %collective-permute-start.1 = (f32[48,128]{1,0:T(8,128)S(1)}, f32[48,128]{1,0:T(8,128)S(1)}, u32[]{:S(2)}, u32[]{:S(2)}) collective-permute-start(f32[48,128]{1,0:T(8,128)S(1)} %shard_map.164.near_ref), channel_id=1, source_target_pairs={{0,1},{1,0},{2,3},{3,2},{4,5},{5,4},{6,7},{7,6},{8,9},{9,8},{10,11... | collective-permute-start | bytes 73736 | tf_op jit(solution)/shard_map/ppermute | solution.py:459
  7.4 4.0 %collective-permute-start.2 = (f32[24,128]{1,0:T(8,128)S(1)}, f32[24,128]{1,0:T(8,128)S(1)}, u32[]{:S(2)}, u32[]{:S(2)}) collective-permute-start(f32[24,128]{1,0:T(8,128)S(1)} %fusion), channel_id=1, source_target_pairs={{0,2},{1,9},{2,0},{3,5},{4,6},{5,3},{6,4},{7,15},{8,10},{9,1},{10,... | collective-permute-start | bytes 36872 | tf_op jit(solution)/shard_map/ppermute | solution.py:466
  11.4 1.2 %collective-permute-start.3 = (f32[24,128]{1,0:T(8,128)S(1)}, f32[24,128]{1,0:T(8,128)S(1)}, u32[]{:S(2)}, u32[]{:S(2)}) collective-permute-start(f32[24,128]{1,0:T(8,128)S(1)} %collective-permute-done.2.side_ref), channel_id=1, source_target_pairs={{0,1},{1,0},{2,3},{3,2},{4,5},{5,4},{6,7},{7,6},{8,9},{9,8},{10,11... | collective-permute-start | bytes 36872 | tf_op jit(solution)/shard_map/ppermute | solution.py:467
  14.4 1.2 %collective-permute-start.4 = (f32[24,128]{1,0:T(8,128)S(1)}, f32[24,128]{1,0:T(8,128)S(1)}, u32[]{:S(2)}, u32[]{:S(2)}) collective-permute-start(f32[24,128]{1,0:T(8,128)S(1)} %shard_map.166.mine_ref), channel_id=1, source_target_pairs={{0,1},{1,0},{2,3},{3,2},{4,5},{5,4},{6,7},{7,6},{8,9},{9,8},{10,11... | collective-permute-start | bytes 36872 | tf_op jit(solution)/shard_map/ppermute | solution.py:479

commit v7 on v6

--- a/solution.py
+++ b/solution.py
@@ -65,16 +65,15 @@
 
 def local_tables(tile, window):
     places = np.arange(tile)
-    cols = []
-    for at, shift in ((0, 0), (HALF, 2 * MARGIN), (2 * HALF, MARGIN), (3 * HALF, MARGIN)):
+    shifts = (MARGIN, 0, 2 * MARGIN)
+    col_table, real, imag = [], [], []
+    for shift in shifts:
         phase = angles(places + shift, frequencies(), window)
-        cols += [(at, np.cos(phase)), (at + BAND, -np.sin(phase))]
-    col_table = lanes(*cols) / window
-    row_table = []
-    for shift in (MARGIN, 0, 2 * MARGIN):
-        phase = angles(frequencies(), places + shift, window)
-        row_table += [np.cos(phase), -np.sin(phase)]
-    return stacked(col_table, 2), three(np.concatenate(row_table, 0))
+        block = np.concatenate([np.cos(phase), -np.sin(phase)], 1) / window
+        col_table.append(stacked(lanes((0, block), (HALF, block)), 2))
+        real.append(np.cos(phase.T))
+        imag.append(-np.sin(phase.T))
+    return np.concatenate(col_table, 0), three(np.concatenate(real + imag, 0))
 
 
 def field_tables(tile, window):
@@ -174,13 +173,13 @@
     return copies
 
 
-def local_spectrum(tile_value, col_ref, row_table):
-    size = col_ref.shape[0] // 2
+def local_spectrum(tile_value, col_table, row_table):
+    size = col_table.shape[0] // 2
     high, low = split(tile_value, 2)
-    ch, cl = col_ref[:size], col_ref[size:]
+    ch, cl = col_table[:size], col_table[size:]
     partial = dot(jnp.concatenate([high, low, high], 1), jnp.concatenate([ch, ch, cl], 0))
     both = dot(row_table, three_right(partial))
-    top, bottom = both[:BAND], both[BAND:]
+    top, bottom = both[: 3 * BAND], both[3 * BAND :]
     lane = lane_ids(top.shape) % HALF
     turned = jnp.where(
         lane < BAND,
@@ -188,7 +187,8 @@
         jnp.where(lane < 2 * BAND, pltpu.roll(bottom, BAND, 1), 0.0),
     )
     result = top + turned
-    return jnp.concatenate([result[:, : 2 * HALF], result[:, 2 * HALF :]], 0)
+    centre, first, last = (result[at * BAND : (at + 1) * BAND] for at in range(3))
+    return jnp.concatenate([jnp.where(lane_ids(first.shape) < HALF, first, last), centre], 0)
 
 
 def open_kernel(*refs):
@@ -218,15 +218,18 @@
     for copy in first:
         copy.wait()
     col_ref, row_ref = targets[:2]
-    own_ref[...] = local_spectrum(mask_ref[...], col_ref, row_ref[: 2 * BAND])
+    own_ref[...] = local_spectrum(
+        mask_ref[...], col_ref[: 2 * mask_ref.shape[0]], row_ref[...]
+    )
     for copy in rest:
         copy.wait()
 
 
 def near_kernel(mesh_shape, tile_ref, col_ref, row_ref, out_ref):
-    down, valid = toward(lax.axis_index("row"), lax.axis_index("cond"), mesh_shape[0])
-    at = pl.multiple_of(jnp.where(down, 4 * BAND, 2 * BAND), 2 * BAND)
-    share = local_spectrum(tile_ref[...], col_ref, row_ref[pl.ds(at, 2 * BAND)])
+    right, valid = toward(lax.axis_index("col"), lax.axis_index("cond"), mesh_shape[1])
+    size = 2 * tile_ref.shape[0]
+    at = pl.multiple_of(jnp.where(right, 2 * size, size), size)
+    share = local_spectrum(tile_ref[...], col_ref[pl.ds(at, size)], row_ref[...])
     out_ref[...] = jnp.where(valid, share, 0.0)
 
 
@@ -260,10 +263,10 @@
     per = 2 * pairs // conds
     tile = target_ref.shape[0]
     wide = 4 * HALF
-    col, core = lax.axis_index("col"), lax.axis_index("cond")
+    row, core = lax.axis_index("row"), lax.axis_index("cond")
 
     def half(value, core):
-        onward, valid = toward(col, core, mesh_shape[1])
+        onward, valid = toward(row, core, mesh_shape[0])
         low_half = lane_ids(value.shape) < HALF
         kept = jnp.where(onward, jnp.where(low_half, 0.0, value), jnp.where(low_half, value, 0.0))
         kept = jnp.where(valid, kept, 0.0)
@@ -366,14 +369,23 @@
     )
 
 
-def adjoint_kernel(mine_ref, theirs_ref, cols_ref, rows_ref, out_ref):
+def adjoint_kernel(mine_ref, theirs_ref, cols_ref, rows_ref, out_hbm, out_ref, sems):
     tile = out_ref.shape[1]
     high, low = split(mine_ref[...] + theirs_ref[...], 2)
     size = cols_ref.shape[0] // 2
     ch, cl = cols_ref[:size], cols_ref[size:]
     halves = dot(jnp.concatenate([high, low, high], 1), jnp.concatenate([ch, ch, cl], 0))
-    joined = jnp.concatenate([halves[:, :tile], halves[:, tile:]], 0)
-    out_ref[...] = dot(rows_ref[...], three_right(joined))
+    joined = three_right(jnp.concatenate([halves[:, :tile], halves[:, tile:]], 0))
+    count = sems.shape[0]
+    step = tile // count
+    copies = []
+    for at in range(count):
+        rows = pl.ds(at * step, step)
+        out_ref[rows] = dot(rows_ref[rows], joined)
+        copies.append(pltpu.make_async_copy(out_ref.at[rows], out_hbm.at[rows], sems.at[at]))
+        copies[-1].start()
+    for copy in copies:
+        copy.wait()
 
 
 VMEM = pl.BlockSpec(memory_space=pltpu.VMEM)
@@ -381,7 +393,7 @@
 HBM = pl.BlockSpec(memory_space=pltpu.HBM)
 
 
-def call(body, outs, specs, args, scratch=(), flops=1000000, grant=8):
+def call(body, outs, specs, args, scratch=(), flops=1000000, grant=8, out_spec=None):
     shapes = [
         shape if hasattr(shape, "dtype") else jax.ShapeDtypeStruct(shape, F32) for shape in outs
     ]
@@ -394,7 +406,7 @@
         body,
         out_shape=shapes[0] if one else shapes,
         in_specs=specs,
-        out_specs=VMEM if one else [VMEM] * len(outs),
+        out_specs=(out_spec or VMEM) if one else [VMEM] * len(outs),
         scratch_shapes=list(scratch),
         compiler_params=pltpu.CompilerParams(vmem_limit_bytes=grant * 2**20),
         cost_estimate=pl.CostEstimate(flops=flops, bytes_accessed=1000000, transcendentals=0),
@@ -432,7 +444,7 @@
     conds = cond_index.shape[0]
     count = kernels.shape[2]
     block = (2 * BAND, 2 * HALF)
-    beside = lax.ppermute(mask, AXES, swaps(mesh_shape, 0))
+    beside = lax.ppermute(mask, AXES, swaps(mesh_shape, 1))
     fetched = local_tables(tile, window) + (target,)
     fetched += field_tables(tile, window) + adjoint_tables(tile, window)
     own, chosen, strength, *fetched = call(
@@ -463,7 +475,7 @@
     arranged = call(arrange_kernel, [(BAND, total * HALF)] * 2, [VMEM] * 2, (real, imag))
     far, arranged = lax.optimization_barrier((far, arranged))
     message = own[:BAND] + near[:BAND] + far[:BAND]
-    side = lax.ppermute(message, AXES, swaps(mesh_shape, 1))
+    side = lax.ppermute(message, AXES, swaps(mesh_shape, 0))
     other = lax.ppermute(side, "cond", swap)
 
     cotangent = call(
@@ -478,7 +490,8 @@
     )
     theirs = lax.ppermute(cotangent, "cond", swap)
     return call(
-        adjoint_kernel, [(tile, tile)], [VMEM] * 4, (cotangent, theirs, *later[-2:])
+        adjoint_kernel, [(tile, tile)], [VMEM] * 4, (cotangent, theirs, *later[-2:]),
+        scratch=[pltpu.VMEM((tile, tile), F32), pltpu.SemaphoreType.DMA((4,))], out_spec=HBM,
     )
 
 

time: 16.7 us -> 16.2 us (0.970)
  starting transfers between devices: 5.5 us -> 5.25 us
  waiting for transfers between devices: 4.83 us -> 4.58 us
    ppermute x2, starting transfers between devices: 5.25 us -> 4.99 us  [the longest x1 3.05 us: shards(): beside = lax.ppermute(mask, AXES, swaps(mesh_shape, 1))]
    ppermute x2, waiting for transfers between devices: 2.39 us -> 2.15 us  [the longest x1 1.76 us: shards(): side = lax.ppermute(message, AXES, swaps(mesh_shape, 0))]
  transfers between devices with their start and end apart: 5 -> 5, of which waited for: 5 -> 5; matrix products, arithmetic and copies ran while one was open for 4% -> 4% of each run, Pallas kernels for 14% -> 15%
where the time goes in v7:
time: 16.2 us; the launch traced here: 16.1 us
  Pallas kernels  5.59 us (35%)
  starting transfers between devices  5.25 us (32%)
  waiting for transfers between devices  4.58 us (28%)
  local copies, waits for them, and re-layouts  0.62 us (4%)
    pallas_call x5, Pallas kernels, call(): pl.pallas_call(body, out_shape=shapes[0] if one else shapes, in_specs=spe...  5.59 us
    ppermute x1, starting transfers between devices, shards(): beside = lax.ppermute(mask, AXES, swaps(mesh_shape, 1))  3.05 us
    ppermute x1, starting transfers between devices, shards(): side = lax.ppermute(message, AXES, swaps(mesh_shape, 0))  1.94 us
    ppermute x1, waiting for transfers between devices, shards(): side = lax.ppermute(message, AXES, swaps(mesh_shape, 0))  1.76 us
    ppermute x1, waiting for transfers between devices, shards(): other = lax.ppermute(side, 'cond', swap)  1.18 us
    ppermute x1, waiting for transfers between devices, shards(): theirs = lax.ppermute(cotangent, 'cond', swap)  1 us
    ppermute x1, waiting for transfers between devices, shards(): beside = lax.ppermute(mask, AXES, swaps(mesh_shape, 1))  0.39 us
  transfers between devices with their start and end apart: 5, of which 5 were waited for; matrix products, arithmetic and copies ran while one was open for 4% of the time, Pallas kernels for 15%

profile of v7, /device:TPU:0, one launch (start us, length us, event | category | flops | bytes accessed | tf_op | source)
XLA Modules:
  0.0 16.1 jit_solution(1481218708052020316)
XLA Ops:
  0.0 3.1 %collective-permute-start = (f32[128,128]{1,0:T(8,128)}, f32[128,128]{1,0:T(8,128)S(1)}, u32[]{:S(2)}, u32[]{:S(2)}) collective-permute-start(f32[128,128]{1,0:T(8,128)} %refs_2_.1), channel_id=1, source_target_pairs={{0,2},{1,9},{2,0},{3,5},{4,6},{5,3},{6,4},{7,15},{8,10},{9,1},{10,... | collective-permute-start | bytes 196616 | tf_op jit(solution)/shard_map/ppermute | solution.py:447
  3.1 2.1 %shard_map.163 = (f32[48,128]{1,0:T(8,128)S(1)}, f32[2,12,2,576]{3,2,1,0:T(2,128)S(1)}, f32[2,8,128]{2,1,0:T(8,128)S(1)}, bf16[768,128]{1,0:T(8,128)(2,1)S(1)}, ...) custom-call(s32[2]{0:T(128)} %refs_0_.1, ...), custom_call_target="tpu_custom_call" | custom-call | flops 1000000 | bytes 1000000 | tf_op jit(solution)/shard_map/pallas_call | solution.py:405
  5.1 0.4 %collective-permute-done.tile_ref = f32[128,128]{1,0:T(8,128)S(1)} collective-permute-done((f32[128,128]{1,0:T(8,128)}, f32[128,128]{1,0:T(8,128)S(1)}, u32[]{:S(2)}, u32[]{:S(2)}) %collective-permute-start) | collective-permute-done | bytes 65568 | tf_op jit(solution)/shard_map/ppermute | solution.py:447
  5.5 0.4 %shard_map.164.near_ref = f32[48,128]{1,0:T(8,128)S(1)} custom-call(f32[128,128]{1,0:T(8,128)S(1)} %collective-permute-done.tile_ref, bf16[768,128]{1,0:T(8,128)(2,1)S(1)} %get-tuple-element.62.col_ref, bf16[144,384]{1,0:T(8,128)(2,1)S(1)} %get-tuple-element.63.row_ref), custom_call_target="tpu_custom_call" | custom-call | flops 1000000 | bytes 1000000 | tf_op jit(solution)/shard_map/pallas_call | solution.py:405
  6.0 0.1 collective-permute-start.1
  6.0 0.3 %slice_reduce_fusion = (f32[2,12,576]{2,1,0:T(8,128)S(1)}, f32[2,12,576]{2,1,0:T(8,128)S(1)}) fusion(f32[2,12,2,576]{3,2,1,0:T(2,128)S(1)} %get-tuple-element.64), kind=kLoop, calls=%fused_computation | loop fusion | bytes 221184 | tf_op jit(solution)/shard_map/slice | solution.py:473
  6.4 0.1 reshape_squeeze.7.imag_ref
  6.5 0.1 reshape_squeeze.6.real_ref
  6.7 0.3 %shard_map.165 = (f32[24,1536]{1,0:T(8,128)S(1)}, f32[24,1536]{1,0:T(8,128)S(1)}) custom-call(f32[576,24]{1,0:T(8,128)S(1)} %reshape_squeeze.6.real_ref, f32[576,24]{1,0:T(8,128)S(1)} %reshape_squeeze.7.imag_ref), custom_call_target="tpu_custom_call" | custom-call | flops 1000000 | bytes 1000000 | tf_op jit(solution)/shard_map/pallas_call | solution.py:405
  7.0 0.2 %collective-permute-done.1.far_ref = f32[48,128]{1,0:T(8,128)S(1)} collective-permute-done((f32[48,128]{1,0:T(8,128)S(1)}, f32[48,128]{1,0:T(8,128)S(1)}, u32[]{:S(2)}, u32[]{:S(2)}) %collective-permute-start.1) | collective-permute-done | bytes 24608 | tf_op jit(solution)/shard_map/ppermute | solution.py:471
  7.2 1.9 %collective-permute-start.2 = (f32[24,128]{1,0:T(8,128)S(1)}, f32[24,128]{1,0:T(8,128)S(1)}, u32[]{:S(2)}, u32[]{:S(2)}) collective-permute-start(f32[24,128]{1,0:T(8,128)S(1)} %fusion), channel_id=1, source_target_pairs={{0,8},{1,3},{2,10},{3,1},{4,12},{5,7},{6,14},{7,5},{8,0},{9,17},{1... | collective-permute-start | bytes 36872 | tf_op jit(solution)/shard_map/ppermute | solution.py:478
  9.2 1.8 %collective-permute-done.2.side_ref = f32[24,128]{1,0:T(8,128)S(1)} collective-permute-done((f32[24,128]{1,0:T(8,128)S(1)}, f32[24,128]{1,0:T(8,128)S(1)}, u32[]{:S(2)}, u32[]{:S(2)}) %collective-permute-start.2) | collective-permute-done | bytes 12320 | tf_op jit(solution)/shard_map/ppermute | solution.py:478
  10.9 0.0 collective-permute-start.3
  10.9 1.2 %collective-permute-done.3.other_ref = f32[24,128]{1,0:T(8,128)S(1)} collective-permute-done((f32[24,128]{1,0:T(8,128)S(1)}, f32[24,128]{1,0:T(8,128)S(1)}, u32[]{:S(2)}, u32[]{:S(2)}) %collective-permute-start.3) | collective-permute-done | bytes 12320 | tf_op jit(solution)/shard_map/ppermute | solution.py:479
  12.1 1.8 %shard_map.166.mine_ref = f32[24,128]{1,0:T(8,128)S(1)} custom-call(f32[2,8,128]{2,1,0:T(8,128)S(1)} %get-tuple-element.59.strength_ref, f32[48,128]{1,0:T(8,128)S(1)} %get-tuple-element.60.own_ref, f32[48,128]{1,0:T(8,128)S(1)} %shard_map.164.near_ref, f32[48,128]{1,0:T(8,128)S(1)} %collective-permute-done.1.far_ref, ...), custom_call_target="tpu_custom_call" | custom-call | flops 1000000 | bytes 1000000 | tf_op jit(solution)/shard_map/pallas_call | solution.py:405
  13.9 0.2 %collective-permute-start.4 = (f32[24,128]{1,0:T(8,128)S(1)}, f32[24,128]{1,0:T(8,128)S(1)}, u32[]{:S(2)}, u32[]{:S(2)}) collective-permute-start(f32[24,128]{1,0:T(8,128)S(1)} %shard_map.166.mine_ref), channel_id=1, source_target_pairs={{0,1},{1,0},{2,3},{3,2},{4,5},{5,4},{6,7},{7,6},{8,9},{9,8},{10,11... | collective-permute-start | bytes 36872 | tf_op jit(solution)/shard_map/ppermute | solution.py:491
  14.1 1.0 %collective-permute-done.4.theirs_ref = f32[24,128]{1,0:T(8,128)S(1)} collective-permute-done((f32[24,128]{1,0:T(8,128)S(1)}, f32[24,128]{1,0:T(8,128)S(1)}, u32[]{:S(2)}, u32[]{:S(2)}) %collective-permute-start.4) | collective-permute-done | bytes 12320 | tf_op jit(solution)/shard_map/ppermute | solution.py:491
  15.1 1.0 %shard_map.167 = f32[128,128]{1,0:T(8,128)} custom-call(f32[24,128]{1,0:T(8,128)S(1)} %shard_map.166.mine_ref, f32[24,128]{1,0:T(8,128)S(1)} %collective-permute-done.4.theirs_ref, bf16[256,256]{1,0:T(8,128)(2,1)S(1)} %get-tuple-element.79.cols_ref, bf16[128,144]{1,0:T(8,128)(2,1)S(1)} %get-tuple-element.80.rows_ref), custom_call_target="tpu_custom_call" | custom-call | flops 1000000 | bytes 1000000 | tf_op jit(solution)/shard_map/pallas_call | solution.py:405
  (1 shorter events, 0.0 us)
Async XLA Ops:
  0.0 5.5 %collective-permute-start = (f32[128,128]{1,0:T(8,128)}, f32[128,128]{1,0:T(8,128)S(1)}, u32[]{:S(2)}, u32[]{:S(2)}) collective-permute-start(f32[128,128]{1,0:T(8,128)} %refs_2_.1), channel_id=1, source_target_pairs={{0,2},{1,9},{2,0},{3,5},{4,6},{5,3},{6,4},{7,15},{8,10},{9,1},{10,... | collective-permute-start | bytes 196616 | tf_op jit(solution)/shard_map/ppermute | solution.py:447
  6.0 1.3 %collective-permute-start.1 = (f32[48,128]{1,0:T(8,128)S(1)}, f32[48,128]{1,0:T(8,128)S(1)}, u32[]{:S(2)}, u32[]{:S(2)}) collective-permute-start(f32[48,128]{1,0:T(8,128)S(1)} %shard_map.164.near_ref), channel_id=1, source_target_pairs={{0,1},{1,0},{2,3},{3,2},{4,5},{5,4},{6,7},{7,6},{8,9},{9,8},{10,11... | collective-permute-start | bytes 73736 | tf_op jit(solution)/shard_map/ppermute | solution.py:471
  7.2 3.7 %collective-permute-start.2 = (f32[24,128]{1,0:T(8,128)S(1)}, f32[24,128]{1,0:T(8,128)S(1)}, u32[]{:S(2)}, u32[]{:S(2)}) collective-permute-start(f32[24,128]{1,0:T(8,128)S(1)} %fusion), channel_id=1, source_target_pairs={{0,8},{1,3},{2,10},{3,1},{4,12},{5,7},{6,14},{7,5},{8,0},{9,17},{1... | collective-permute-start | bytes 36872 | tf_op jit(solution)/shard_map/ppermute | solution.py:478
  10.9 1.2 %collective-permute-start.3 = (f32[24,128]{1,0:T(8,128)S(1)}, f32[24,128]{1,0:T(8,128)S(1)}, u32[]{:S(2)}, u32[]{:S(2)}) collective-permute-start(f32[24,128]{1,0:T(8,128)S(1)} %collective-permute-done.2.side_ref), channel_id=1, source_target_pairs={{0,1},{1,0},{2,3},{3,2},{4,5},{5,4},{6,7},{7,6},{8,9},{9,8},{10,11... | collective-permute-start | bytes 36872 | tf_op jit(solution)/shard_map/ppermute | solution.py:479
  13.9 1.2 %collective-permute-start.4 = (f32[24,128]{1,0:T(8,128)S(1)}, f32[24,128]{1,0:T(8,128)S(1)}, u32[]{:S(2)}, u32[]{:S(2)}) collective-permute-start(f32[24,128]{1,0:T(8,128)S(1)} %shard_map.166.mine_ref), channel_id=1, source_target_pairs={{0,1},{1,0},{2,3},{3,2},{4,5},{5,4},{6,7},{7,6},{8,9},{9,8},{10,11... | collective-permute-start | bytes 36872 | tf_op jit(solution)/shard_map/ppermute | solution.py:491
